TPU v7x, 128 devices: a whole 4x4x4 slice. The times are simulated.
128 devices in a mesh: gx: 16 (over z, y), gy: 8 (over x, core).
Axes of the slice: x: 4, y: 4, z: 4, core: 2. Of those that a mesh axis runs over, the one named last changes fastest.
Arguments:
- jacobian: bfloat16 [16384, 192, 384], P(('gx', 'gy')), may hold values from -0.3125 to 0.3125
- grain_slots: int32 [16384, 64], P(('gx', 'gy')), may hold values from 0 to 18431, as said below
- block_count: int32 [128], P(('gx', 'gy')), may hold values from 1 to 128, as said below
- impulse_start: float32 [16384, 192], P(('gx', 'gy')), may hold values from -3 to 3
- velocity_bias: float32 [16384, 192], P(('gx', 'gy')), may hold values from -6 to 6
- friction: float32 [16384, 64], P(('gx', 'gy')), may hold values from 0.2 to 0.8
- free_velocity: float32 [6, 262144], P(None, ('gx', 'gy')), may hold values from -6 to 6
- inverse_mass: float32 [6, 262144], P(None, ('gx', 'gy')), may hold values from 0.5 to 4
Outputs:
- impulses: float32 [16384, 192], P(('gx', 'gy'))
- velocities: float32 [6, 262144], P(None, ('gx', 'gy'))
Inputs may be any that keep to these rules, and one draw needn't show every extreme that they name: `grain_slots`: A slot value s * 2048 + l names grain l of the device at offset (s // 3 - 1, s % 3 - 1) along (gx, gy) from the block's device (the device holding the block's row); that device always exists. A device's first block_count block slots are live, the rest are not; some device has all 128 live.
All inputs are finite; a program needn't handle non-finite values.
Results may differ from a plain program's by a relative error of at most 0.014.
Values may be sent and summed in bfloat16 or wider, within the bound.
A program may use at most 128 MiB of HBM per device.

v0:
```python
import math

import jax
import jax.numpy as jnp
from jax import lax
from jax.sharding import Mesh
from jax.sharding import PartitionSpec as P

CB = 64
GB = 64
ITERS = 3
GX_GY = ("gx_0", "gx_1", "gy_0", "gy_1")
GX = ("gx_0", "gx_1")
GY = ("gy_0", "gy_1")


epsilon = 1e-06


def with_halo(array, sides, width):
    for axis, dim in sides:
        size, length = (lax.axis_size(axis), array.shape[dim])
        up = [(i, (i + 1) % size) for i in range(size - 1)]
        down = [(j, i) for i, j in up]
        last = lax.slice_in_dim(array, length - width, length, axis=dim)
        leading = lax.slice_in_dim(array, 0, width, axis=dim)
        before = lax.ppermute(last, axis, up)
        after = lax.ppermute(leading, axis, down)
        array = jnp.concatenate([before, array, after], axis=dim)
    return array


def from_behind(block, axis, distance):
    devices = range(lax.axis_size(axis))
    route = [(i - distance, i) for i in devices if i - distance in devices]
    return lax.ppermute(block, axis, route)


def one_axis_at_a_time(array, axes):
    for axis in axes:
        array = lax.psum(array, axis)
    return array


def momentum_weights(iterations):
    momentum = 1.0
    weights = []
    for iteration in range(iterations):
        upcoming = (-momentum * momentum + momentum * math.sqrt(momentum * momentum + 4.0)) / 2.0
        weights.append(momentum * (1.0 - momentum) / (momentum * momentum + upcoming))
        momentum = upcoming
    return weights


def project_cone(target, friction):
    normal = target[:, :CB]
    tangent_one = target[:, CB : 2 * CB]
    tangent_two = target[:, 2 * CB :]
    tangent_norm = jnp.sqrt(tangent_one * tangent_one + tangent_two * tangent_two)
    inside = tangent_norm <= friction * normal
    opposite = friction * tangent_norm <= -normal
    cone_normal = (normal + friction * tangent_norm) / (1.0 + friction * friction)
    cone_ratio = friction * cone_normal / jnp.where(tangent_norm > 0, tangent_norm, 1.0)
    new_normal = jnp.where(inside, normal, jnp.where(opposite, 0.0, cone_normal))
    shrink = jnp.where(inside, 1.0, jnp.where(opposite, 0.0, cone_ratio))
    return jnp.concatenate([new_normal, tangent_one * shrink, tangent_two * shrink], axis=1)


def shards(
    jacobian,
    grain_slots,
    block_count,
    impulse_start,
    velocity_bias,
    friction,
    free_velocity,
    inverse_mass,
):
    blocks = jacobian.shape[0]
    grains = free_velocity.shape[1]
    live_mask = (jnp.arange(blocks, dtype=jnp.int32) < block_count[0]).astype(jnp.float32)[:, None]

    def forward(grain_field):
        nearby = with_halo(grain_field.reshape(6, 1, 1, grains), ((GX, 1), (GY, 2)), 1)
        nearby = nearby.reshape(6, 9 * grains)
        picked = jnp.take(nearby, grain_slots, axis=1)
        picked = jnp.transpose(picked, (1, 0, 2)).reshape(blocks, 6 * GB)
        return jnp.einsum("bij,bj->bi", jacobian, picked, preferred_element_type=jnp.float32)

    def backward(impulse_field):
        pushes = jnp.einsum(
            "bij,bi->bj", jacobian, impulse_field, preferred_element_type=jnp.float32
        )
        pushes = jnp.transpose(pushes.reshape(blocks, 6, GB), (1, 0, 2))
        nearby = jnp.zeros((6, 9 * grains), jnp.float32).at[:, grain_slots].add(pushes)
        nearby = nearby.reshape(6, 3, 3, grains)
        row_sums = nearby[:, :, 1]
        for step_y in (-1, 1):
            row_sums = row_sums + from_behind(
                nearby[:, :, step_y + 1].astype(jnp.bfloat16), GY, step_y
            ).astype(jnp.float32)
        summed = row_sums[:, 1]
        for step_x in (-1, 1):
            summed = summed + from_behind(row_sums[:, step_x + 1], GX, step_x)
        return summed

    constraint_bias = velocity_bias + forward(free_velocity.astype(jnp.bfloat16))
    extrapolated = impulse_start * live_mask
    previous = extrapolated
    current = extrapolated
    weights = momentum_weights(ITERS)
    for iteration in range(ITERS):
        pushed = backward(extrapolated.astype(jnp.bfloat16))
        moved = inverse_mass * pushed
        size_total, energy_total = (
            one_axis_at_a_time(jnp.sum(extrapolated * extrapolated), GX_GY),
            one_axis_at_a_time(jnp.sum(pushed * moved), GX_GY),
        )
        gradient = (forward(moved.astype(jnp.bfloat16)) + constraint_bias) * live_mask
        step_size = size_total / (energy_total + epsilon)
        current = project_cone(extrapolated - step_size * gradient, friction) * live_mask
        extrapolated = current + weights[iteration] * (current - previous)
        previous = current
    final_push = backward(current.astype(jnp.bfloat16))
    return (current, free_velocity + inverse_mass * final_push)


def solution(mesh):
    finer = Mesh(mesh.devices.reshape(4, 4, 4, 2), ("gx_0", "gx_1", "gy_0", "gy_1"))
    placed = (
        P(GX_GY, None, None),
        P(GX_GY, None),
        P(GX_GY),
        P(GX_GY, None),
        P(GX_GY, None),
        P(GX_GY, None),
        P(None, GX_GY),
        P(None, GX_GY),
    )
    return jax.shard_map(
        shards,
        mesh=finer,
        in_specs=placed,
        out_specs=(P(GX_GY, None), P(None, GX_GY)),
        check_vma=False,
    )
```

profile of v0, /device:TPU:34, one launch (start us, length us, event | category | flops | bytes accessed | tf_op | source)
XLA Modules:
  0.0 701.7 jit_solution(708703900480097008)
XLA Ops:
  11.1 9.1 %fusion = f32[128,384]{1,0:T(8,128)S(1)} fusion(bf16[128,192,384]{2,1,0:T(8,128)(2,1)} %param.10, f32[128,192]{1,0:T(8,128)S(1)} %copy.120), kind=kLoop, calls=%fused_computation.16 | loop fusion | flops 28262400 | bytes 19169280
  24.9 48.5 %scatter_custom_fusion = f32[6,18432]{0,1:T(8,128)} fusion(s32[8192]{0:T(1024)S(1)} %reshape.136, f32[8192,6]{1,0:T(8,128)} %bitcast.175, f32[]{:T(128)} %constant.14.clone.1), kind=kCustom, calls=%fused_computation.30 | custom fusion | flops 49152 | bytes 442880 | tf_op jit(solution)/shard_map/scatter-add | solution.py:95
  120.9 24.8 %gather_fusion.1 = bf16[8192,6]{1,0:T(8,128)(2,1)S(1)} fusion(bf16[6,18432]{0,1:T(8,128)(2,1)} %bitcast.171, s32[8192]{0:T(1024)S(1)} %broadcast_clamp_fusion), kind=kCustom, calls=%fused_computation.1.clone | custom fusion | bytes 229376 | tf_op jit(solution)/shard_map/jit(_take)/gather | solution.py:86
  148.0 9.7 %all-reduce.8 = (f32[]{:T(128)}, f32[]{:T(128)}) all-reduce(f32[]{:T(128)} %get-tuple-element.68, f32[]{:T(128)} %get-tuple-element.47), channel_id=1, replica_groups=mesh['gx_0'=4,'gx_1'=4,'gy_0'=4,'gy_1'=2] {'gx_0'}, use_global_device_ids=true, to_apply=%region_1.2 | all-reduce | flops 2 | bytes 16 | tf_op jit(solution)/shard_map/psum | solution.py:41
  157.7 10.9 %all-reduce.5 = (f32[]{:T(128)}, f32[]{:T(128)}) all-reduce(f32[]{:T(128)} %get-tuple-element.21, f32[]{:T(128)} %get-tuple-element.22), channel_id=1, replica_groups=mesh['gx_0'=4,'gx_1'=4,'gy_0'=4,'gy_1'=2] {'gx_1'}, use_global_device_ids=true, to_apply=%region_2.3 | all-reduce | flops 2 | bytes 16 | tf_op jit(solution)/shard_map/psum | solution.py:41
  168.6 9.2 %all-reduce.2 = (f32[]{:T(128)}, f32[]{:T(128)}) all-reduce(f32[]{:T(128)} %get-tuple-element.15, f32[]{:T(128)} %get-tuple-element.16), channel_id=1, replica_groups=mesh['gx_0'=4,'gx_1'=4,'gy_0'=4,'gy_1'=2] {'gy_0'}, use_global_device_ids=true, to_apply=%region_3.4 | all-reduce | flops 2 | bytes 16 | tf_op jit(solution)/shard_map/psum | solution.py:41
  186.2 24.8 %gather_fusion = bf16[8192,6]{1,0:T(8,128)(2,1)S(1)} fusion(bf16[6,18432]{0,1:T(8,128)(2,1)} %bitcast.172, s32[8192]{0:T(1024)S(1)} %broadcast_clamp_fusion), kind=kCustom, calls=%fused_computation.clone | custom fusion | bytes 229376 | tf_op jit(solution)/shard_map/jit(_take)/gather | solution.py:86
  213.7 29.2 %fusion.5 = (f32[128,192]{1,0:T(8,128)S(1)}, f32[128,192]{1,0:T(8,128)S(1)}) fusion(f32[128,384]{1,0:T(8,128)S(1)} %copy.122, bf16[128,192,384]{2,1,0:T(8,128)(2,1)} %param.10, f32[128,384]{1,0:T(8,128)S(1)} %copy.121), kind=kLoop, calls=%fused_computation.21 | loop fusion | flops 47136768 | bytes 19464192
  244.0 9.1 %fusion.1 = f32[128,384]{1,0:T(8,128)S(1)} fusion(bf16[128,192,384]{2,1,0:T(8,128)(2,1)} %param.10, f32[128,192]{1,0:T(8,128)S(1)} %copy.123), kind=kLoop, calls=%fused_computation.17 | loop fusion | flops 28262400 | bytes 19169280
  257.8 48.5 %scatter_custom_fusion.1 = f32[6,18432]{0,1:T(8,128)} fusion(s32[8192]{0:T(1024)S(1)} %reshape.136, f32[8192,6]{1,0:T(8,128)} %bitcast.176, f32[]{:T(128)} %constant.14.clone.1), kind=kCustom, calls=%fused_computation.28 | custom fusion | flops 49152 | bytes 442880 | tf_op jit(solution)/shard_map/scatter-add | solution.py:95
  349.2 7.2 %all-reduce.7 = (f32[]{:T(128)}, f32[]{:T(128)}) all-reduce(f32[]{:T(128)} %get-tuple-element.37, f32[]{:T(128)} %get-tuple-element.45), channel_id=1, replica_groups=mesh['gx_0'=4,'gx_1'=4,'gy_0'=4,'gy_1'=2] {'gx_0'}, use_global_device_ids=true, to_apply=%region_12.14 | all-reduce | flops 2 | bytes 16 | tf_op jit(solution)/shard_map/psum | solution.py:41
  356.4 9.8 %all-reduce.4 = (f32[]{:T(128)}, f32[]{:T(128)}) all-reduce(f32[]{:T(128)} %get-tuple-element.19, f32[]{:T(128)} %get-tuple-element.20), channel_id=1, replica_groups=mesh['gx_0'=4,'gx_1'=4,'gy_0'=4,'gy_1'=2] {'gx_1'}, use_global_device_ids=true, to_apply=%region_13.15 | all-reduce | flops 2 | bytes 16 | tf_op jit(solution)/shard_map/psum | solution.py:41
  366.2 7.3 %all-reduce.1 = (f32[]{:T(128)}, f32[]{:T(128)}) all-reduce(f32[]{:T(128)} %get-tuple-element.13, f32[]{:T(128)} %get-tuple-element.14), channel_id=1, replica_groups=mesh['gx_0'=4,'gx_1'=4,'gy_0'=4,'gy_1'=2] {'gy_0'}, use_global_device_ids=true, to_apply=%region_14.16 | all-reduce | flops 2 | bytes 16 | tf_op jit(solution)/shard_map/psum | solution.py:41
  381.5 24.8 %gather_fusion.2 = bf16[8192,6]{1,0:T(8,128)(2,1)S(1)} fusion(bf16[6,18432]{0,1:T(8,128)(2,1)} %bitcast.173, s32[8192]{0:T(1024)S(1)} %broadcast_clamp_fusion), kind=kCustom, calls=%fused_computation.2.clone | custom fusion | bytes 229376 | tf_op jit(solution)/shard_map/jit(_take)/gather | solution.py:86
  408.8 15.7 %fusion.6 = f32[128,192]{1,0:T(8,128)S(1)} fusion(f32[128,384]{1,0:T(8,128)S(1)} %copy.124, bf16[128,192,384]{2,1,0:T(8,128)(2,1)} %param.10), kind=kLoop, calls=%fused_computation.22 | loop fusion | flops 28286976 | bytes 19169280
  425.5 9.1 %fusion.2 = f32[128,384]{1,0:T(8,128)S(1)} fusion(bf16[128,192,384]{2,1,0:T(8,128)(2,1)} %param.10, f32[128,192]{1,0:T(8,128)S(1)} %copy.125), kind=kLoop, calls=%fused_computation.18 | loop fusion | flops 28262400 | bytes 19169280
  439.2 48.5 %scatter_custom_fusion.2 = f32[6,18432]{0,1:T(8,128)} fusion(s32[8192]{0:T(1024)S(1)} %reshape.136, f32[8192,6]{1,0:T(8,128)} %bitcast.177, f32[]{:T(128)} %constant.14.clone.1), kind=kCustom, calls=%fused_computation.26 | custom fusion | flops 49152 | bytes 442880 | tf_op jit(solution)/shard_map/scatter-add | solution.py:95
  532.3 7.2 %all-reduce.6 = (f32[]{:T(128)}, f32[]{:T(128)}) all-reduce(f32[]{:T(128)} %get-tuple-element.33, f32[]{:T(128)} %get-tuple-element.43), channel_id=1, replica_groups=mesh['gx_0'=4,'gx_1'=4,'gy_0'=4,'gy_1'=2] {'gx_0'}, use_global_device_ids=true, to_apply=%region_23.25 | all-reduce | flops 2 | bytes 16 | tf_op jit(solution)/shard_map/psum | solution.py:41
  539.5 9.8 %all-reduce.3 = (f32[]{:T(128)}, f32[]{:T(128)}) all-reduce(f32[]{:T(128)} %get-tuple-element.17, f32[]{:T(128)} %get-tuple-element.18), channel_id=1, replica_groups=mesh['gx_0'=4,'gx_1'=4,'gy_0'=4,'gy_1'=2] {'gx_1'}, use_global_device_ids=true, to_apply=%region_24.26 | all-reduce | flops 2 | bytes 16 | tf_op jit(solution)/shard_map/psum | solution.py:41
  549.3 7.1 %all-reduce = (f32[]{:T(128)}, f32[]{:T(128)}) all-reduce(f32[]{:T(128)} %get-tuple-element.11, f32[]{:T(128)} %get-tuple-element.12), channel_id=1, replica_groups=mesh['gx_0'=4,'gx_1'=4,'gy_0'=4,'gy_1'=2] {'gy_0'}, use_global_device_ids=true, to_apply=%region_25.27 | all-reduce | flops 2 | bytes 16 | tf_op jit(solution)/shard_map/psum | solution.py:41
  564.6 24.8 %gather_fusion.3 = bf16[8192,6]{1,0:T(8,128)(2,1)S(1)} fusion(bf16[6,18432]{0,1:T(8,128)(2,1)} %bitcast.170, s32[8192]{0:T(1024)S(1)} %broadcast_clamp_fusion), kind=kCustom, calls=%fused_computation.3.clone | custom fusion | bytes 229376 | tf_op jit(solution)/shard_map/jit(_take)/gather | solution.py:86
  591.9 15.7 %fusion.7 = f32[128,192]{1,0:T(8,128)S(1)} fusion(f32[128,384]{1,0:T(8,128)S(1)} %copy.126, bf16[128,192,384]{2,1,0:T(8,128)(2,1)} %param.10), kind=kLoop, calls=%fused_computation.23 | loop fusion | flops 28286976 | bytes 19169280
  608.6 9.1 %fusion.3 = f32[128,384]{1,0:T(8,128)S(1)} fusion(bf16[128,192,384]{2,1,0:T(8,128)(2,1)} %param.10, f32[128,192]{1,0:T(8,128)S(1)} %copy.127), kind=kLoop, calls=%fused_computation.19 | loop fusion | flops 28262400 | bytes 19169280
  622.3 48.5 %scatter_custom_fusion.3 = f32[6,18432]{0,1:T(8,128)} fusion(s32[8192]{0:T(1024)S(1)} %reshape.136, f32[8192,6]{1,0:T(8,128)} %bitcast.174, f32[]{:T(128)} %constant.14.clone.1), kind=kCustom, calls=%fused_computation.24 | custom fusion | flops 49152 | bytes 442880 | tf_op jit(solution)/shard_map/scatter-add | solution.py:95
  (167 shorter events, 226.6 us)
Async XLA Ops:
  1.5 106.3 %collective-permute-start.9 = (bf16[6,1,1,2048]{3,0,2,1:T(8,128)(2,1)S(1)}, bf16[6,1,1,2048]{3,0,2,1:T(8,128)(2,1)S(1)}, u32[]{:S(2)}, u32[]{:S(2)}) collective-permute-start(bf16[6,1,1,2048]{3,0,2,1:T(8,128)(2,1)S(1)} %convert_bitcast_fusion), channel_id=1, source_target_pairs={{8,0},{16,8},{24,16},{32,24},{40,32},{48,40},{56,48},{64,56},{72,6... | collective-permute-start | bytes 73736 | tf_op jit(solution)/shard_map/ppermute | solution.py:28
  5.9 101.8 %collective-permute-start.8 = (bf16[6,1,1,2048]{3,0,2,1:T(8,128)(2,1)S(1)}, bf16[6,1,1,2048]{3,0,2,1:T(8,128)(2,1)S(1)}, u32[]{:S(2)}, u32[]{:S(2)}) collective-permute-start(bf16[6,1,1,2048]{3,0,2,1:T(8,128)(2,1)S(1)} %convert_bitcast_fusion), channel_id=1, source_target_pairs={{0,8},{8,16},{16,24},{24,32},{32,40},{40,48},{48,56},{56,64},{64,7... | collective-permute-start | bytes 73736 | tf_op jit(solution)/shard_map/ppermute | solution.py:27
  87.0 8.0 %collective-permute-start.2 = (f32[6,2048]{1,0:T(8,128)S(1)}, f32[6,2048]{1,0:T(8,128)S(1)}, u32[]{:S(2)}, u32[]{:S(2)}) collective-permute-start(f32[6,2048]{1,0:T(8,128)S(1)} %get-tuple-element.63), channel_id=1, source_target_pairs={{8,0},{16,8},{24,16},{32,24},{40,32},{48,40},{56,48},{64,56},{72,6... | collective-permute-start | bytes 147464 | tf_op jit(solution)/shard_map/ppermute | solution.py:36
  93.0 8.3 %collective-permute-start.3 = (f32[6,2048]{1,0:T(8,128)S(1)}, f32[6,2048]{1,0:T(8,128)S(1)}, u32[]{:S(2)}, u32[]{:S(2)}) collective-permute-start(f32[6,2048]{1,0:T(8,128)S(1)} %get-tuple-element.64), channel_id=1, source_target_pairs={{0,8},{8,16},{16,24},{24,32},{32,40},{40,48},{48,56},{56,64},{64,7... | collective-permute-start | bytes 147464 | tf_op jit(solution)/shard_map/ppermute | solution.py:36
  101.9 10.2 %collective-permute-start.5 = (bf16[6,1,1,2048]{3,0,2,1:T(8,128)(2,1)S(1)}, bf16[6,1,1,2048]{3,0,2,1:T(8,128)(2,1)S(1)}, u32[]{:S(2)}, u32[]{:S(2)}) collective-permute-start(bf16[6,1,1,2048]{3,0,2,1:T(8,128)(2,1)S(1)} %get-tuple-element.48), channel_id=1, source_target_pairs={{8,0},{16,8},{24,16},{32,24},{40,32},{48,40},{56,48},{64,56},{72,6... | collective-permute-start | bytes 73736 | tf_op jit(solution)/shard_map/ppermute | solution.py:28
  103.8 8.3 %collective-permute-start.4 = (bf16[6,1,1,2048]{3,0,2,1:T(8,128)(2,1)S(1)}, bf16[6,1,1,2048]{3,0,2,1:T(8,128)(2,1)S(1)}, u32[]{:S(2)}, u32[]{:S(2)}) collective-permute-start(bf16[6,1,1,2048]{3,0,2,1:T(8,128)(2,1)S(1)} %get-tuple-element.48), channel_id=1, source_target_pairs={{0,8},{8,16},{16,24},{24,32},{32,40},{40,48},{48,56},{56,64},{64,7... | collective-permute-start | bytes 73736 | tf_op jit(solution)/shard_map/ppermute | solution.py:27
  107.8 9.5 %collective-permute-start.11 = (bf16[6,3,1,2048]{3,0,2,1:T(8,128)(2,1)S(1)}, bf16[6,3,1,2048]{3,0,2,1:T(8,128)(2,1)S(1)}, u32[]{:S(2)}, u32[]{:S(2)}) collective-permute-start(bf16[6,3,1,2048]{3,0,2,1:T(8,128)(2,1)S(1)} %pad_maximum_fusion.5), channel_id=1, source_target_pairs={{1,0},{2,1},{3,2},{4,3},{5,4},{6,5},{7,6},{9,8},{10,9},{11,10},{12... | collective-permute-start | bytes 221192 | tf_op jit(solution)/shard_map/ppermute | solution.py:28
  109.7 7.6 %collective-permute-start.10 = (bf16[6,3,1,2048]{3,0,2,1:T(8,128)(2,1)S(1)}, bf16[6,3,1,2048]{3,0,2,1:T(8,128)(2,1)S(1)}, u32[]{:S(2)}, u32[]{:S(2)}) collective-permute-start(bf16[6,3,1,2048]{3,0,2,1:T(8,128)(2,1)S(1)} %pad_maximum_fusion.5), channel_id=1, source_target_pairs={{0,1},{1,2},{2,3},{3,4},{4,5},{5,6},{6,7},{8,9},{9,10},{10,11},{11... | collective-permute-start | bytes 221192 | tf_op jit(solution)/shard_map/ppermute | solution.py:27
  112.2 70.5 %collective-permute-start.7 = (bf16[6,3,1,2048]{3,0,2,1:T(8,128)(2,1)S(1)}, bf16[6,3,1,2048]{3,0,2,1:T(8,128)(2,1)S(1)}, u32[]{:S(2)}, u32[]{:S(2)}) collective-permute-start(bf16[6,3,1,2048]{3,0,2,1:T(8,128)(2,1)S(1)} %pad_maximum_fusion.4), channel_id=1, source_target_pairs={{1,0},{2,1},{3,2},{4,3},{5,4},{6,5},{7,6},{9,8},{10,9},{11,10},{12... | collective-permute-start | bytes 221192 | tf_op jit(solution)/shard_map/ppermute | solution.py:28
  115.4 67.3 %collective-permute-start.6 = (bf16[6,3,1,2048]{3,0,2,1:T(8,128)(2,1)S(1)}, bf16[6,3,1,2048]{3,0,2,1:T(8,128)(2,1)S(1)}, u32[]{:S(2)}, u32[]{:S(2)}) collective-permute-start(bf16[6,3,1,2048]{3,0,2,1:T(8,128)(2,1)S(1)} %pad_maximum_fusion.4), channel_id=1, source_target_pairs={{0,1},{1,2},{2,3},{3,4},{4,5},{5,6},{6,7},{8,9},{9,10},{10,11},{11... | collective-permute-start | bytes 221192 | tf_op jit(solution)/shard_map/ppermute | solution.py:27
  312.0 6.3 collective-permute-start.12
  326.0 8.3 %collective-permute-start.15 = (f32[6,2048]{1,0:T(8,128)S(1)}, f32[6,2048]{1,0:T(8,128)S(1)}, u32[]{:S(2)}, u32[]{:S(2)}) collective-permute-start(f32[6,2048]{1,0:T(8,128)S(1)} %get-tuple-element.62), channel_id=1, source_target_pairs={{0,8},{8,16},{16,24},{24,32},{32,40},{40,48},{48,56},{56,64},{64,7... | collective-permute-start | bytes 147464 | tf_op jit(solution)/shard_map/ppermute | solution.py:36
  336.8 7.9 %collective-permute-start.16 = (bf16[6,1,1,2048]{3,0,2,1:T(8,128)(2,1)S(1)}, bf16[6,1,1,2048]{3,0,2,1:T(8,128)(2,1)S(1)}, u32[]{:S(2)}, u32[]{:S(2)}) collective-permute-start(bf16[6,1,1,2048]{3,0,2,1:T(8,128)(2,1)S(1)} %get-tuple-element.46), channel_id=1, source_target_pairs={{0,8},{8,16},{16,24},{24,32},{32,40},{40,48},{48,56},{56,64},{64,7... | collective-permute-start | bytes 73736 | tf_op jit(solution)/shard_map/ppermute | solution.py:27
  344.7 33.2 %collective-permute-start.19 = (bf16[6,3,1,2048]{3,0,2,1:T(8,128)(2,1)S(1)}, bf16[6,3,1,2048]{3,0,2,1:T(8,128)(2,1)S(1)}, u32[]{:S(2)}, u32[]{:S(2)}) collective-permute-start(bf16[6,3,1,2048]{3,0,2,1:T(8,128)(2,1)S(1)} %pad_maximum_fusion.6), channel_id=1, source_target_pairs={{1,0},{2,1},{3,2},{4,3},{5,4},{6,5},{7,6},{9,8},{10,9},{11,10},{12... | collective-permute-start | bytes 221192 | tf_op jit(solution)/shard_map/ppermute | solution.py:28
  346.7 31.3 %collective-permute-start.18 = (bf16[6,3,1,2048]{3,0,2,1:T(8,128)(2,1)S(1)}, bf16[6,3,1,2048]{3,0,2,1:T(8,128)(2,1)S(1)}, u32[]{:S(2)}, u32[]{:S(2)}) collective-permute-start(bf16[6,3,1,2048]{3,0,2,1:T(8,128)(2,1)S(1)} %pad_maximum_fusion.6), channel_id=1, source_target_pairs={{0,1},{1,2},{2,3},{3,4},{4,5},{5,6},{6,7},{8,9},{9,10},{10,11},{11... | collective-permute-start | bytes 221192 | tf_op jit(solution)/shard_map/ppermute | solution.py:27
  493.4 6.9 collective-permute-start.20
  504.1 7.1 %collective-permute-start.22 = (f32[6,2048]{1,0:T(8,128)S(1)}, f32[6,2048]{1,0:T(8,128)S(1)}, u32[]{:S(2)}, u32[]{:S(2)}) collective-permute-start(f32[6,2048]{1,0:T(8,128)S(1)} %get-tuple-element.59), channel_id=1, source_target_pairs={{8,0},{16,8},{24,16},{32,24},{40,32},{48,40},{56,48},{64,56},{72,6... | collective-permute-start | bytes 147464 | tf_op jit(solution)/shard_map/ppermute | solution.py:36
  509.2 8.3 %collective-permute-start.23 = (f32[6,2048]{1,0:T(8,128)S(1)}, f32[6,2048]{1,0:T(8,128)S(1)}, u32[]{:S(2)}, u32[]{:S(2)}) collective-permute-start(f32[6,2048]{1,0:T(8,128)S(1)} %get-tuple-element.60), channel_id=1, source_target_pairs={{0,8},{8,16},{16,24},{24,32},{32,40},{40,48},{48,56},{56,64},{64,7... | collective-permute-start | bytes 147464 | tf_op jit(solution)/shard_map/ppermute | solution.py:36
  520.1 7.9 %collective-permute-start.24 = (bf16[6,1,1,2048]{3,0,2,1:T(8,128)(2,1)S(1)}, bf16[6,1,1,2048]{3,0,2,1:T(8,128)(2,1)S(1)}, u32[]{:S(2)}, u32[]{:S(2)}) collective-permute-start(bf16[6,1,1,2048]{3,0,2,1:T(8,128)(2,1)S(1)} %get-tuple-element.44), channel_id=1, source_target_pairs={{0,8},{8,16},{16,24},{24,32},{32,40},{40,48},{48,56},{56,64},{64,7... | collective-permute-start | bytes 73736 | tf_op jit(solution)/shard_map/ppermute | solution.py:27
  528.0 33.1 %collective-permute-start.27 = (bf16[6,3,1,2048]{3,0,2,1:T(8,128)(2,1)S(1)}, bf16[6,3,1,2048]{3,0,2,1:T(8,128)(2,1)S(1)}, u32[]{:S(2)}, u32[]{:S(2)}) collective-permute-start(bf16[6,3,1,2048]{3,0,2,1:T(8,128)(2,1)S(1)} %pad_maximum_fusion.7), channel_id=1, source_target_pairs={{1,0},{2,1},{3,2},{4,3},{5,4},{6,5},{7,6},{9,8},{10,9},{11,10},{12... | collective-permute-start | bytes 221192 | tf_op jit(solution)/shard_map/ppermute | solution.py:28
  529.9 31.2 %collective-permute-start.26 = (bf16[6,3,1,2048]{3,0,2,1:T(8,128)(2,1)S(1)}, bf16[6,3,1,2048]{3,0,2,1:T(8,128)(2,1)S(1)}, u32[]{:S(2)}, u32[]{:S(2)}) collective-permute-start(bf16[6,3,1,2048]{3,0,2,1:T(8,128)(2,1)S(1)} %pad_maximum_fusion.7), channel_id=1, source_target_pairs={{0,1},{1,2},{2,3},{3,4},{4,5},{5,6},{6,7},{8,9},{9,10},{10,11},{11... | collective-permute-start | bytes 221192 | tf_op jit(solution)/shard_map/ppermute | solution.py:27
  676.5 7.1 %collective-permute-start.28 = (bf16[6,3,2048]{2,0,1:T(8,128)(2,1)S(1)}, bf16[6,3,2048]{2,0,1:T(8,128)(2,1)S(1)}, u32[]{:S(2)}, u32[]{:S(2)}) collective-permute-start(bf16[6,3,2048]{2,0,1:T(8,128)(2,1)S(1)} %get-tuple-element.49), channel_id=1, source_target_pairs={{1,0},{2,1},{3,2},{4,3},{5,4},{6,5},{7,6},{9,8},{10,9},{11,10},{12... | collective-permute-start | bytes 221192 | tf_op jit(solution)/shard_map/ppermute | solution.py:36
  687.4 7.1 %collective-permute-start.30 = (f32[6,2048]{1,0:T(8,128)S(1)}, f32[6,2048]{1,0:T(8,128)S(1)}, u32[]{:S(2)}, u32[]{:S(2)}) collective-permute-start(f32[6,2048]{1,0:T(8,128)S(1)} %get-tuple-element.57), channel_id=1, source_target_pairs={{8,0},{16,8},{24,16},{32,24},{40,32},{48,40},{56,48},{64,56},{72,6... | collective-permute-start | bytes 147464 | tf_op jit(solution)/shard_map/ppermute | solution.py:36
  692.6 8.3 %collective-permute-start.31 = (f32[6,2048]{1,0:T(8,128)S(1)}, f32[6,2048]{1,0:T(8,128)S(1)}, u32[]{:S(2)}, u32[]{:S(2)}) collective-permute-start(f32[6,2048]{1,0:T(8,128)S(1)} %get-tuple-element.58), channel_id=1, source_target_pairs={{0,8},{8,16},{16,24},{24,32},{32,40},{40,48},{48,56},{56,64},{64,7... | collective-permute-start | bytes 147464 | tf_op jit(solution)/shard_map/ppermute | solution.py:36
  (14 other events, 359.3 us)
where the time goes:
time: 711 us; the launch traced here: 702 us
  other arithmetic  300 us (42%)
  local copies, waits for them, and re-layouts  165 us (23%)
  starting transfers between devices  93.8 us (13%)
  blocking collectives  88.2 us (12%)
  waiting for transfers between devices  48.8 us (7%)
    scatter-add x4, other arithmetic, backward(): jnp.zeros((6, 9 * grains), jnp.float32).at[:, grain_slots].add(pushes)  194 us
    gather x8, local copies, waits for them, and re-layouts, forward(): picked = jnp.take(nearby, grain_slots, axis=1)  108 us
    unnamed x13, other arithmetic  97.8 us
    psum x12, blocking collectives, one_axis_at_a_time(): array = lax.psum(array, axis)  88.2 us
    ppermute x16, starting transfers between devices, from_behind(): return lax.ppermute(block, axis, route)  51.7 us
    ppermute x16, waiting for transfers between devices, from_behind(): return lax.ppermute(block, axis, route)  40.8 us
    ppermute x8, starting transfers between devices, with_halo(): before = lax.ppermute(last, axis, up)  23 us
    reshape x4, local copies, waits for them, and re-layouts, backward(): nearby = nearby.reshape(6, 3, 3, grains)  22.5 us
  transfers between devices with their start and end apart: 32, of which 14 were waited for; matrix products, arithmetic and copies ran while one was open for 15% of the time, Pallas kernels for 0%

commit v1 on v0

--- a/solution.py
+++ b/solution.py
@@ -112,10 +112,10 @@
     for iteration in range(ITERS):
         pushed = backward(extrapolated.astype(jnp.bfloat16))
         moved = inverse_mass * pushed
-        size_total, energy_total = (
-            one_axis_at_a_time(jnp.sum(extrapolated * extrapolated), GX_GY),
-            one_axis_at_a_time(jnp.sum(pushed * moved), GX_GY),
+        totals = lax.psum(
+            jnp.stack([jnp.sum(extrapolated * extrapolated), jnp.sum(pushed * moved)]), GX_GY
         )
+        size_total, energy_total = totals[0], totals[1]
         gradient = (forward(moved.astype(jnp.bfloat16)) + constraint_bias) * live_mask
         step_size = size_total / (energy_total + epsilon)
         current = project_cone(extrapolated - step_size * gradient, friction) * live_mask

time: 711 us -> 799 us (1.12)
  blocking collectives: 88.2 us -> 189 us
  waiting for transfers between devices: 48.8 us -> 35 us
    psum x12 -> x3, blocking collectives: 88.2 us -> 189 us  [shards(): lax.psum(jnp.stack([jnp.sum(extrapolated * extrapolated), jnp.sum(pushed...]
    ppermute x16, waiting for transfers between devices: 40.8 us -> 29.1 us  [from_behind(): return lax.ppermute(block, axis, route)]
    ppermute x16, starting transfers between devices: 51.7 us -> 42.9 us  [from_behind(): return lax.ppermute(block, axis, route)]
  transfers between devices with their start and end apart: 32 -> 32, of which waited for: 14 -> 12; matrix products, arithmetic and copies ran while one was open for 15% -> 14% of each run, Pallas kernels for 0% -> 0%
where the time goes in v1:
time: 799 us; the launch traced here: 790 us
  other arithmetic  304 us (38%)
  blocking collectives  189 us (24%)
  local copies, waits for them, and re-layouts  167 us (21%)
  starting transfers between devices  89.1 us (11%)
  waiting for transfers between devices  35 us (4%)
    scatter-add x4, other arithmetic, backward(): jnp.zeros((6, 9 * grains), jnp.float32).at[:, grain_slots].add(pushes)  194 us
    psum x3, blocking collectives, shards(): lax.psum(jnp.stack([jnp.sum(extrapolated * extrapolated), jnp.sum(pushed...  189 us
    gather x8, local copies, waits for them, and re-layouts, forward(): picked = jnp.take(nearby, grain_slots, axis=1)  108 us
    unnamed x13, other arithmetic  97.8 us
    ppermute x16, starting transfers between devices, from_behind(): return lax.ppermute(block, axis, route)  42.9 us
    ppermute x16, waiting for transfers between devices, from_behind(): return lax.ppermute(block, axis, route)  29.1 us
    ppermute x8, starting transfers between devices, with_halo(): after = lax.ppermute(leading, axis, down)  26.3 us
    reshape x4, local copies, waits for them, and re-layouts, backward(): nearby = nearby.reshape(6, 3, 3, grains)  22.5 us
  transfers between devices with their start and end apart: 32, of which 12 were waited for; matrix products, arithmetic and copies ran while one was open for 14% of the time, Pallas kernels for 0%

profile of v1, /device:TPU:34, one launch (start us, length us, event | category | flops | bytes accessed | tf_op | source)
XLA Modules:
  0.0 789.8 jit_solution(12597441963960114974)
XLA Ops:
  11.1 9.1 %fusion = f32[128,384]{1,0:T(8,128)S(1)} fusion(bf16[128,192,384]{2,1,0:T(8,128)(2,1)} %param.10, f32[128,192]{1,0:T(8,128)S(1)} %copy.120), kind=kLoop, calls=%fused_computation.16 | loop fusion | flops 28262400 | bytes 19169280
  24.9 48.5 %scatter_custom_fusion = f32[6,18432]{0,1:T(8,128)} fusion(s32[8192]{0:T(1024)S(1)} %reshape.145, f32[8192,6]{1,0:T(8,128)} %bitcast.184, f32[]{:T(128)} %constant.14.clone.1), kind=kCustom, calls=%fused_computation.30 | custom fusion | flops 49152 | bytes 442880 | tf_op jit(solution)/shard_map/scatter-add | solution.py:95
  73.4 5.6 copy.50
  88.7 6.0 collective-permute-start.2
  100.2 24.8 %gather_fusion.1 = bf16[8192,6]{1,0:T(8,128)(2,1)S(1)} fusion(bf16[6,18432]{0,1:T(8,128)(2,1)} %bitcast.180, s32[8192]{0:T(1024)S(1)} %broadcast_clamp_fusion), kind=kCustom, calls=%fused_computation.1.clone | custom fusion | bytes 229376 | tf_op jit(solution)/shard_map/jit(_take)/gather | solution.py:86
  125.7 6.0 collective-permute-start.5
  137.3 65.9 %psum.21 = f32[2]{0:T(128)S(1)} all-reduce(f32[2]{0:T(128)S(1)} %pad_maximum_fusion.8), channel_id=1, replica_groups=mesh['gx_0'=4,'gx_1'=4,'gy_0'=4,'gy_1'=2] {'gx_0','gx_1','gy_0','gy_1'}, use_global_device_ids=true, to_apply=%region_3.4 | all-reduce | flops 2 | bytes 16 | tf_op jit(solution)/shard_map/psum | solution.py:115
  215.8 24.8 %gather_fusion = bf16[8192,6]{1,0:T(8,128)(2,1)S(1)} fusion(bf16[6,18432]{0,1:T(8,128)(2,1)} %bitcast.181, s32[8192]{0:T(1024)S(1)} %broadcast_clamp_fusion), kind=kCustom, calls=%fused_computation.clone | custom fusion | bytes 229376 | tf_op jit(solution)/shard_map/jit(_take)/gather | solution.py:86
  243.3 29.2 %fusion.5 = (f32[128,192]{1,0:T(8,128)S(1)}, f32[128,192]{1,0:T(8,128)S(1)}) fusion(f32[128,384]{1,0:T(8,128)S(1)} %copy.122, bf16[128,192,384]{2,1,0:T(8,128)(2,1)} %param.10, f32[128,384]{1,0:T(8,128)S(1)} %copy.121), kind=kLoop, calls=%fused_computation.21 | loop fusion | flops 47136768 | bytes 19464192
  273.6 9.1 %fusion.1 = f32[128,384]{1,0:T(8,128)S(1)} fusion(bf16[128,192,384]{2,1,0:T(8,128)(2,1)} %param.10, f32[128,192]{1,0:T(8,128)S(1)} %copy.123), kind=kLoop, calls=%fused_computation.17 | loop fusion | flops 28262400 | bytes 19169280
  287.4 48.5 %scatter_custom_fusion.1 = f32[6,18432]{0,1:T(8,128)} fusion(s32[8192]{0:T(1024)S(1)} %reshape.145, f32[8192,6]{1,0:T(8,128)} %bitcast.185, f32[]{:T(128)} %constant.14.clone.1), kind=kCustom, calls=%fused_computation.28 | custom fusion | flops 49152 | bytes 442880 | tf_op jit(solution)/shard_map/scatter-add | solution.py:95
  355.7 5.8 collective-permute-done.15
  369.4 61.6 %psum.22 = f32[2]{0:T(128)S(1)} all-reduce(f32[2]{0:T(128)S(1)} %pad_maximum_fusion.9), channel_id=1, replica_groups=mesh['gx_0'=4,'gx_1'=4,'gy_0'=4,'gy_1'=2] {'gx_0','gx_1','gy_0','gy_1'}, use_global_device_ids=true, to_apply=%region_7.9 | all-reduce | flops 2 | bytes 16 | tf_op jit(solution)/shard_map/psum | solution.py:115
  443.4 24.8 %gather_fusion.2 = bf16[8192,6]{1,0:T(8,128)(2,1)S(1)} fusion(bf16[6,18432]{0,1:T(8,128)(2,1)} %bitcast.182, s32[8192]{0:T(1024)S(1)} %broadcast_clamp_fusion), kind=kCustom, calls=%fused_computation.2.clone | custom fusion | bytes 229376 | tf_op jit(solution)/shard_map/jit(_take)/gather | solution.py:86
  470.7 15.7 %fusion.6 = f32[128,192]{1,0:T(8,128)S(1)} fusion(f32[128,384]{1,0:T(8,128)S(1)} %copy.124, bf16[128,192,384]{2,1,0:T(8,128)(2,1)} %param.10), kind=kLoop, calls=%fused_computation.22 | loop fusion | flops 28286976 | bytes 19169280
  487.3 9.1 %fusion.2 = f32[128,384]{1,0:T(8,128)S(1)} fusion(bf16[128,192,384]{2,1,0:T(8,128)(2,1)} %param.10, f32[128,192]{1,0:T(8,128)S(1)} %copy.125), kind=kLoop, calls=%fused_computation.18 | loop fusion | flops 28262400 | bytes 19169280
  501.1 48.5 %scatter_custom_fusion.2 = f32[6,18432]{0,1:T(8,128)} fusion(s32[8192]{0:T(1024)S(1)} %reshape.145, f32[8192,6]{1,0:T(8,128)} %bitcast.186, f32[]{:T(128)} %constant.14.clone.1), kind=kCustom, calls=%fused_computation.26 | custom fusion | flops 49152 | bytes 442880 | tf_op jit(solution)/shard_map/scatter-add | solution.py:95
  569.4 5.7 collective-permute-done.23
  582.9 61.4 %psum.23 = f32[2]{0:T(128)S(1)} all-reduce(f32[2]{0:T(128)S(1)} %pad_maximum_fusion.10), channel_id=1, replica_groups=mesh['gx_0'=4,'gx_1'=4,'gy_0'=4,'gy_1'=2] {'gx_0','gx_1','gy_0','gy_1'}, use_global_device_ids=true, to_apply=%region_11.13 | all-reduce | flops 2 | bytes 16 | tf_op jit(solution)/shard_map/psum | solution.py:115
  656.8 24.8 %gather_fusion.3 = bf16[8192,6]{1,0:T(8,128)(2,1)S(1)} fusion(bf16[6,18432]{0,1:T(8,128)(2,1)} %bitcast.179, s32[8192]{0:T(1024)S(1)} %broadcast_clamp_fusion), kind=kCustom, calls=%fused_computation.3.clone | custom fusion | bytes 229376 | tf_op jit(solution)/shard_map/jit(_take)/gather | solution.py:86
  684.1 15.7 %fusion.7 = f32[128,192]{1,0:T(8,128)S(1)} fusion(f32[128,384]{1,0:T(8,128)S(1)} %copy.126, bf16[128,192,384]{2,1,0:T(8,128)(2,1)} %param.10), kind=kLoop, calls=%fused_computation.23 | loop fusion | flops 28286976 | bytes 19169280
  700.7 9.1 %fusion.3 = f32[128,384]{1,0:T(8,128)S(1)} fusion(bf16[128,192,384]{2,1,0:T(8,128)(2,1)} %param.10, f32[128,192]{1,0:T(8,128)S(1)} %copy.127), kind=kLoop, calls=%fused_computation.19 | loop fusion | flops 28262400 | bytes 19169280
  714.5 48.5 %scatter_custom_fusion.3 = f32[6,18432]{0,1:T(8,128)} fusion(s32[8192]{0:T(1024)S(1)} %reshape.145, f32[8192,6]{1,0:T(8,128)} %bitcast.183, f32[]{:T(128)} %constant.14.clone.1), kind=kCustom, calls=%fused_computation.24 | custom fusion | flops 49152 | bytes 442880 | tf_op jit(solution)/shard_map/scatter-add | solution.py:95
  782.8 6.2 collective-permute-done.31
  (164 shorter events, 168.7 us)
Async XLA Ops:
  1.5 82.0 %collective-permute-start.9 = (bf16[6,1,1,2048]{3,0,2,1:T(8,128)(2,1)S(1)}, bf16[6,1,1,2048]{3,0,2,1:T(8,128)(2,1)S(1)}, u32[]{:S(2)}, u32[]{:S(2)}) collective-permute-start(bf16[6,1,1,2048]{3,0,2,1:T(8,128)(2,1)S(1)} %convert_bitcast_fusion), channel_id=1, source_target_pairs={{8,0},{16,8},{24,16},{32,24},{40,32},{48,40},{56,48},{64,56},{72,6... | collective-permute-start | bytes 73736 | tf_op jit(solution)/shard_map/ppermute | solution.py:28
  5.9 77.5 %collective-permute-start.8 = (bf16[6,1,1,2048]{3,0,2,1:T(8,128)(2,1)S(1)}, bf16[6,1,1,2048]{3,0,2,1:T(8,128)(2,1)S(1)}, u32[]{:S(2)}, u32[]{:S(2)}) collective-permute-start(bf16[6,1,1,2048]{3,0,2,1:T(8,128)(2,1)S(1)} %convert_bitcast_fusion), channel_id=1, source_target_pairs={{0,8},{8,16},{16,24},{24,32},{32,40},{40,48},{48,56},{56,64},{64,7... | collective-permute-start | bytes 73736 | tf_op jit(solution)/shard_map/ppermute | solution.py:27
  79.1 9.5 %collective-permute-start = (bf16[6,3,2048]{2,0,1:T(8,128)(2,1)S(1)}, bf16[6,3,2048]{2,0,1:T(8,128)(2,1)S(1)}, u32[]{:S(2)}, u32[]{:S(2)}) collective-permute-start(bf16[6,3,2048]{2,0,1:T(8,128)(2,1)S(1)} %get-tuple-element.31), channel_id=1, source_target_pairs={{1,0},{2,1},{3,2},{4,3},{5,4},{6,5},{7,6},{9,8},{10,9},{11,10},{12... | collective-permute-start | bytes 221192 | tf_op jit(solution)/shard_map/ppermute | solution.py:36
  81.0 7.6 collective-permute-start.1
  83.5 13.1 %collective-permute-start.11 = (bf16[6,3,1,2048]{3,0,2,1:T(8,128)(2,1)S(1)}, bf16[6,3,1,2048]{3,0,2,1:T(8,128)(2,1)S(1)}, u32[]{:S(2)}, u32[]{:S(2)}) collective-permute-start(bf16[6,3,1,2048]{3,0,2,1:T(8,128)(2,1)S(1)} %pad_maximum_fusion.5), channel_id=1, source_target_pairs={{1,0},{2,1},{3,2},{4,3},{5,4},{6,5},{7,6},{9,8},{10,9},{11,10},{12... | collective-permute-start | bytes 221192 | tf_op jit(solution)/shard_map/ppermute | solution.py:28
  86.7 10.0 %collective-permute-start.10 = (bf16[6,3,1,2048]{3,0,2,1:T(8,128)(2,1)S(1)}, bf16[6,3,1,2048]{3,0,2,1:T(8,128)(2,1)S(1)}, u32[]{:S(2)}, u32[]{:S(2)}) collective-permute-start(bf16[6,3,1,2048]{3,0,2,1:T(8,128)(2,1)S(1)} %pad_maximum_fusion.5), channel_id=1, source_target_pairs={{0,1},{1,2},{2,3},{3,4},{4,5},{5,6},{6,7},{8,9},{9,10},{10,11},{11... | collective-permute-start | bytes 221192 | tf_op jit(solution)/shard_map/ppermute | solution.py:27
  88.7 36.4 %collective-permute-start.2 = (f32[6,2048]{1,0:T(8,128)S(1)}, f32[6,2048]{1,0:T(8,128)S(1)}, u32[]{:S(2)}, u32[]{:S(2)}) collective-permute-start(f32[6,2048]{1,0:T(8,128)S(1)} %get-tuple-element.39), channel_id=1, source_target_pairs={{8,0},{16,8},{24,16},{32,24},{40,32},{48,40},{56,48},{64,56},{72,6... | collective-permute-start | bytes 147464 | tf_op jit(solution)/shard_map/ppermute | solution.py:36
  94.7 30.4 %collective-permute-start.3 = (f32[6,2048]{1,0:T(8,128)S(1)}, f32[6,2048]{1,0:T(8,128)S(1)}, u32[]{:S(2)}, u32[]{:S(2)}) collective-permute-start(f32[6,2048]{1,0:T(8,128)S(1)} %get-tuple-element.40), channel_id=1, source_target_pairs={{0,8},{8,16},{16,24},{24,32},{32,40},{40,48},{48,56},{56,64},{64,7... | collective-permute-start | bytes 147464 | tf_op jit(solution)/shard_map/ppermute | solution.py:36
  125.7 77.5 %collective-permute-start.5 = (bf16[6,1,1,2048]{3,0,2,1:T(8,128)(2,1)S(1)}, bf16[6,1,1,2048]{3,0,2,1:T(8,128)(2,1)S(1)}, u32[]{:S(2)}, u32[]{:S(2)}) collective-permute-start(bf16[6,1,1,2048]{3,0,2,1:T(8,128)(2,1)S(1)} %get-tuple-element.24), channel_id=1, source_target_pairs={{8,0},{16,8},{24,16},{32,24},{40,32},{48,40},{56,48},{64,56},{72,6... | collective-permute-start | bytes 73736 | tf_op jit(solution)/shard_map/ppermute | solution.py:28
  131.8 71.5 %collective-permute-start.4 = (bf16[6,1,1,2048]{3,0,2,1:T(8,128)(2,1)S(1)}, bf16[6,1,1,2048]{3,0,2,1:T(8,128)(2,1)S(1)}, u32[]{:S(2)}, u32[]{:S(2)}) collective-permute-start(bf16[6,1,1,2048]{3,0,2,1:T(8,128)(2,1)S(1)} %get-tuple-element.24), channel_id=1, source_target_pairs={{0,8},{8,16},{16,24},{24,32},{32,40},{40,48},{48,56},{56,64},{64,7... | collective-permute-start | bytes 73736 | tf_op jit(solution)/shard_map/ppermute | solution.py:27
  203.3 7.3 collective-permute-start.7
  206.4 5.9 collective-permute-start.6
  349.6 6.2 collective-permute-start.14
  353.3 8.3 %collective-permute-start.15 = (f32[6,2048]{1,0:T(8,128)S(1)}, f32[6,2048]{1,0:T(8,128)S(1)}, u32[]{:S(2)}, u32[]{:S(2)}) collective-permute-start(f32[6,2048]{1,0:T(8,128)S(1)} %get-tuple-element.38), channel_id=1, source_target_pairs={{0,8},{8,16},{16,24},{24,32},{32,40},{40,48},{48,56},{56,64},{64,7... | collective-permute-start | bytes 147464 | tf_op jit(solution)/shard_map/ppermute | solution.py:36
  362.2 68.8 %collective-permute-start.17 = (bf16[6,1,1,2048]{3,0,2,1:T(8,128)(2,1)S(1)}, bf16[6,1,1,2048]{3,0,2,1:T(8,128)(2,1)S(1)}, u32[]{:S(2)}, u32[]{:S(2)}) collective-permute-start(bf16[6,1,1,2048]{3,0,2,1:T(8,128)(2,1)S(1)} %get-tuple-element.22), channel_id=1, source_target_pairs={{8,0},{16,8},{24,16},{32,24},{40,32},{48,40},{56,48},{64,56},{72,6... | collective-permute-start | bytes 73736 | tf_op jit(solution)/shard_map/ppermute | solution.py:28
  364.1 66.9 %collective-permute-start.16 = (bf16[6,1,1,2048]{3,0,2,1:T(8,128)(2,1)S(1)}, bf16[6,1,1,2048]{3,0,2,1:T(8,128)(2,1)S(1)}, u32[]{:S(2)}, u32[]{:S(2)}) collective-permute-start(bf16[6,1,1,2048]{3,0,2,1:T(8,128)(2,1)S(1)} %get-tuple-element.22), channel_id=1, source_target_pairs={{0,8},{8,16},{16,24},{24,32},{32,40},{40,48},{48,56},{56,64},{64,7... | collective-permute-start | bytes 73736 | tf_op jit(solution)/shard_map/ppermute | solution.py:27
  431.0 6.7 collective-permute-start.19
  563.2 6.2 collective-permute-start.22
  566.8 8.3 %collective-permute-start.23 = (f32[6,2048]{1,0:T(8,128)S(1)}, f32[6,2048]{1,0:T(8,128)S(1)}, u32[]{:S(2)}, u32[]{:S(2)}) collective-permute-start(f32[6,2048]{1,0:T(8,128)S(1)} %get-tuple-element.36), channel_id=1, source_target_pairs={{0,8},{8,16},{16,24},{24,32},{32,40},{40,48},{48,56},{56,64},{64,7... | collective-permute-start | bytes 147464 | tf_op jit(solution)/shard_map/ppermute | solution.py:36
  575.7 68.6 %collective-permute-start.25 = (bf16[6,1,1,2048]{3,0,2,1:T(8,128)(2,1)S(1)}, bf16[6,1,1,2048]{3,0,2,1:T(8,128)(2,1)S(1)}, u32[]{:S(2)}, u32[]{:S(2)}) collective-permute-start(bf16[6,1,1,2048]{3,0,2,1:T(8,128)(2,1)S(1)} %get-tuple-element.20), channel_id=1, source_target_pairs={{8,0},{16,8},{24,16},{32,24},{40,32},{48,40},{56,48},{64,56},{72,6... | collective-permute-start | bytes 73736 | tf_op jit(solution)/shard_map/ppermute | solution.py:28
  577.6 66.7 %collective-permute-start.24 = (bf16[6,1,1,2048]{3,0,2,1:T(8,128)(2,1)S(1)}, bf16[6,1,1,2048]{3,0,2,1:T(8,128)(2,1)S(1)}, u32[]{:S(2)}, u32[]{:S(2)}) collective-permute-start(bf16[6,1,1,2048]{3,0,2,1:T(8,128)(2,1)S(1)} %get-tuple-element.20), channel_id=1, source_target_pairs={{0,8},{8,16},{16,24},{24,32},{32,40},{40,48},{48,56},{56,64},{64,7... | collective-permute-start | bytes 73736 | tf_op jit(solution)/shard_map/ppermute | solution.py:27
  644.4 6.8 collective-permute-start.27
  776.6 6.2 collective-permute-start.30
  780.7 8.3 %collective-permute-start.31 = (f32[6,2048]{1,0:T(8,128)S(1)}, f32[6,2048]{1,0:T(8,128)S(1)}, u32[]{:S(2)}, u32[]{:S(2)}) collective-permute-start(f32[6,2048]{1,0:T(8,128)S(1)} %get-tuple-element.34), channel_id=1, source_target_pairs={{0,8},{8,16},{16,24},{24,32},{32,40},{40,48},{48,56},{56,64},{64,7... | collective-permute-start | bytes 147464 | tf_op jit(solution)/shard_map/ppermute | solution.py:36
  (14 other events, 315.8 us)

commit v2 on v1

--- a/solution.py
+++ b/solution.py
@@ -5,6 +5,7 @@
 from jax import lax
 from jax.sharding import Mesh
 from jax.sharding import PartitionSpec as P
+
 
 CB = 64
 GB = 64
@@ -36,16 +37,10 @@
     return lax.ppermute(block, axis, route)
 
 
-def one_axis_at_a_time(array, axes):
-    for axis in axes:
-        array = lax.psum(array, axis)
-    return array
-
-
 def momentum_weights(iterations):
     momentum = 1.0
     weights = []
-    for iteration in range(iterations):
+    for _ in range(iterations):
         upcoming = (-momentum * momentum + momentum * math.sqrt(momentum * momentum + 4.0)) / 2.0
         weights.append(momentum * (1.0 - momentum) / (momentum * momentum + upcoming))
         momentum = upcoming
@@ -112,9 +107,8 @@
     for iteration in range(ITERS):
         pushed = backward(extrapolated.astype(jnp.bfloat16))
         moved = inverse_mass * pushed
-        totals = lax.psum(
-            jnp.stack([jnp.sum(extrapolated * extrapolated), jnp.sum(pushed * moved)]), GX_GY
-        )
+        partial = jnp.stack([jnp.sum(extrapolated * extrapolated), jnp.sum(pushed * moved)])
+        totals = lax.psum(jnp.pad(partial, (0, 16384 - 2)), GX_GY)
         size_total, energy_total = totals[0], totals[1]
         gradient = (forward(moved.astype(jnp.bfloat16)) + constraint_bias) * live_mask
         step_size = size_total / (energy_total + epsilon)

time: 799 us -> 1020 us (1.28)
  waiting for transfers between devices: 35 us -> 430 us
  blocking collectives: 189 us -> 0 us
  between operations: 6.4 us -> 19.5 us
    psum x0 -> x3, waiting for transfers between devices: none -> 392 us  [shards(): totals = lax.psum(jnp.pad(partial, (0, 16384 - 2)), GX_GY)]
    psum x3 -> x0, blocking collectives: 189 us -> none  [shards(): lax.psum(jnp.stack([jnp.sum(extrapolated * extrapolated), jnp.sum(pushed...]
  transfers between devices with their start and end apart: 32 -> 35, of which waited for: 12 -> 18; matrix products, arithmetic and copies ran while one was open for 14% -> 11% of each run, Pallas kernels for 0% -> 0%
where the time goes in v2:
time: 1020 us
  waiting for transfers between devices  430 us (42%)
  other arithmetic  306 us (30%)
  local copies, waits for them, and re-layouts  169 us (17%)
  starting transfers between devices  91.4 us (9%)
  between operations  19.5 us (2%)
    psum x3, waiting for transfers between devices, shards(): totals = lax.psum(jnp.pad(partial, (0, 16384 - 2)), GX_GY)  392 us
    scatter-add x4, other arithmetic, backward(): jnp.zeros((6, 9 * grains), jnp.float32).at[:, grain_slots].add(pushes)  194 us
    gather x8, local copies, waits for them, and re-layouts, forward(): picked = jnp.take(nearby, grain_slots, axis=1)  108 us
    unnamed x13, other arithmetic  97.8 us
    ppermute x16, starting transfers between devices, from_behind(): return lax.ppermute(block, axis, route)  46.4 us
    ppermute x16, waiting for transfers between devices, from_behind(): return lax.ppermute(block, axis, route)  30.1 us
    ppermute x8, starting transfers between devices, with_halo(): after = lax.ppermute(leading, axis, down)  23.6 us
    reshape x4, local copies, waits for them, and re-layouts, backward(): nearby = nearby.reshape(6, 3, 3, grains)  22.5 us
  transfers between devices with their start and end apart: 35, of which 18 were waited for; matrix products, arithmetic and copies ran while one was open for 11% of the time, Pallas kernels for 0%

profile of v2, /device:TPU:34, one launch (start us, length us, event | category | flops | bytes accessed | tf_op | source)
XLA Modules:
  0.0 1015.8 jit_solution(6949251054653778411)
XLA Ops:
  17.7 9.1 fusion
  31.5 48.5 %scatter_custom_fusion = f32[6,18432]{0,1:T(8,128)} fusion(s32[8192]{0:T(1024)S(1)} %reshape.145, f32[8192,6]{1,0:T(8,128)} %bitcast.184, f32[]{:T(128)} %constant.14.clone.1), kind=kCustom, calls=%fused_computation.30 | custom fusion | flops 49152 | bytes 442880 | tf_op jit(solution)/shard_map/scatter-add | solution.py:90
  80.0 5.6 copy.50
  95.3 6.0 collective-permute-start.2
  106.9 24.8 %gather_fusion.1 = bf16[8192,6]{1,0:T(8,128)(2,1)S(1)} fusion(bf16[6,18432]{0,1:T(8,128)(2,1)} %bitcast.180, s32[8192]{0:T(1024)S(1)} %broadcast_clamp_fusion), kind=kCustom, calls=%fused_computation.1.clone | custom fusion | bytes 229376 | tf_op jit(solution)/shard_map/jit(_take)/gather | solution.py:81
  134.7 6.0 collective-permute-start.5
  153.6 132.3 %all-reduce.7.cloned.1.call-done = f32[16384]{0:T(1024)} async-done(((f32[16384]{0:T(1024)}), f32[16384]{0:T(1024)}) %all-reduce.7.cloned.1.call-update) | async-done | bytes 65552 | tf_op jit(solution)/shard_map/psum | solution.py:111
  292.1 24.8 %gather_fusion = bf16[8192,6]{1,0:T(8,128)(2,1)S(1)} fusion(bf16[6,18432]{0,1:T(8,128)(2,1)} %bitcast.181, s32[8192]{0:T(1024)S(1)} %broadcast_clamp_fusion), kind=kCustom, calls=%fused_computation.clone | custom fusion | bytes 229376 | tf_op jit(solution)/shard_map/jit(_take)/gather | solution.py:81
  319.6 29.2 %fusion.5 = (f32[128,192]{1,0:T(8,128)S(1)}, f32[128,192]{1,0:T(8,128)S(1)}) fusion(f32[128,384]{1,0:T(8,128)S(1)} %copy.122, bf16[128,192,384]{2,1,0:T(8,128)(2,1)} %param.10, f32[128,384]{1,0:T(8,128)S(1)} %copy.121), kind=kLoop, calls=%fused_computation.21 | loop fusion | flops 47136768 | bytes 19464192
  349.9 9.1 fusion.1
  363.7 48.5 %scatter_custom_fusion.1 = f32[6,18432]{0,1:T(8,128)} fusion(s32[8192]{0:T(1024)S(1)} %reshape.145, f32[8192,6]{1,0:T(8,128)} %bitcast.185, f32[]{:T(128)} %constant.14.clone.1), kind=kCustom, calls=%fused_computation.28 | custom fusion | flops 49152 | bytes 442880 | tf_op jit(solution)/shard_map/scatter-add | solution.py:90
  433.6 5.7 collective-permute-done.15
  454.4 129.8 %all-reduce.9.cloned.1.call-done = f32[16384]{0:T(1024)} async-done(((f32[16384]{0:T(1024)}), f32[16384]{0:T(1024)}) %all-reduce.9.cloned.1.call-update) | async-done | bytes 65552 | tf_op jit(solution)/shard_map/psum | solution.py:111
  590.4 24.8 %gather_fusion.2 = bf16[8192,6]{1,0:T(8,128)(2,1)S(1)} fusion(bf16[6,18432]{0,1:T(8,128)(2,1)} %bitcast.182, s32[8192]{0:T(1024)S(1)} %broadcast_clamp_fusion), kind=kCustom, calls=%fused_computation.2.clone | custom fusion | bytes 229376 | tf_op jit(solution)/shard_map/jit(_take)/gather | solution.py:81
  617.7 15.7 %fusion.6 = f32[128,192]{1,0:T(8,128)S(1)} fusion(f32[128,384]{1,0:T(8,128)S(1)} %copy.124, bf16[128,192,384]{2,1,0:T(8,128)(2,1)} %param.10), kind=kLoop, calls=%fused_computation.22 | loop fusion | flops 28286976 | bytes 19169280
  634.4 9.1 fusion.2
  648.1 48.5 %scatter_custom_fusion.2 = f32[6,18432]{0,1:T(8,128)} fusion(s32[8192]{0:T(1024)S(1)} %reshape.145, f32[8192,6]{1,0:T(8,128)} %bitcast.186, f32[]{:T(128)} %constant.14.clone.1), kind=kCustom, calls=%fused_computation.26 | custom fusion | flops 49152 | bytes 442880 | tf_op jit(solution)/shard_map/scatter-add | solution.py:90
  718.1 5.7 collective-permute-done.23
  739.0 129.8 %all-reduce.11.cloned.1.call-done = f32[16384]{0:T(1024)} async-done(((f32[16384]{0:T(1024)}), f32[16384]{0:T(1024)}) %all-reduce.11.cloned.1.call-update) | async-done | bytes 65552 | tf_op jit(solution)/shard_map/psum | solution.py:111
  874.9 24.8 %gather_fusion.3 = bf16[8192,6]{1,0:T(8,128)(2,1)S(1)} fusion(bf16[6,18432]{0,1:T(8,128)(2,1)} %bitcast.179, s32[8192]{0:T(1024)S(1)} %broadcast_clamp_fusion), kind=kCustom, calls=%fused_computation.3.clone | custom fusion | bytes 229376 | tf_op jit(solution)/shard_map/jit(_take)/gather | solution.py:81
  902.2 15.7 %fusion.7 = f32[128,192]{1,0:T(8,128)S(1)} fusion(f32[128,384]{1,0:T(8,128)S(1)} %copy.126, bf16[128,192,384]{2,1,0:T(8,128)(2,1)} %param.10), kind=kLoop, calls=%fused_computation.23 | loop fusion | flops 28286976 | bytes 19169280
  918.9 9.1 fusion.3
  932.7 48.5 %scatter_custom_fusion.3 = f32[6,18432]{0,1:T(8,128)} fusion(s32[8192]{0:T(1024)S(1)} %reshape.145, f32[8192,6]{1,0:T(8,128)} %bitcast.183, f32[]{:T(128)} %constant.14.clone.1), kind=kCustom, calls=%fused_computation.24 | custom fusion | flops 49152 | bytes 442880 | tf_op jit(solution)/shard_map/scatter-add | solution.py:90
  1002.6 5.7 collective-permute-done.31
  (170 shorter events, 179.1 us)
Async XLA Ops:
  7.2 278.7 %all-reduce.7.cloned.1.call-start = ((), (), s32[]{:S(2)}) async-start(), calls=%async_computation | async-start | bytes 131072 | tf_op jit(solution)/shard_map/psum | solution.py:111
  8.1 82.0 %collective-permute-start.9 = (bf16[6,1,1,2048]{3,0,2,1:T(8,128)(2,1)S(1)}, bf16[6,1,1,2048]{3,0,2,1:T(8,128)(2,1)S(1)}, u32[]{:S(2)}, u32[]{:S(2)}) collective-permute-start(bf16[6,1,1,2048]{3,0,2,1:T(8,128)(2,1)S(1)} %convert_bitcast_fusion), channel_id=1, source_target_pairs={{8,0},{16,8},{24,16},{32,24},{40,32},{48,40},{56,48},{64,56},{72,6... | collective-permute-start | bytes 73736 | tf_op jit(solution)/shard_map/ppermute | solution.py:29
  12.5 77.6 %collective-permute-start.8 = (bf16[6,1,1,2048]{3,0,2,1:T(8,128)(2,1)S(1)}, bf16[6,1,1,2048]{3,0,2,1:T(8,128)(2,1)S(1)}, u32[]{:S(2)}, u32[]{:S(2)}) collective-permute-start(bf16[6,1,1,2048]{3,0,2,1:T(8,128)(2,1)S(1)} %convert_bitcast_fusion), channel_id=1, source_target_pairs={{0,8},{8,16},{16,24},{24,32},{32,40},{40,48},{48,56},{56,64},{64,7... | collective-permute-start | bytes 73736 | tf_op jit(solution)/shard_map/ppermute | solution.py:28
  85.7 9.5 collective-permute-start
  90.1 13.1 %collective-permute-start.11 = (bf16[6,3,1,2048]{3,0,2,1:T(8,128)(2,1)S(1)}, bf16[6,3,1,2048]{3,0,2,1:T(8,128)(2,1)S(1)}, u32[]{:S(2)}, u32[]{:S(2)}) collective-permute-start(bf16[6,3,1,2048]{3,0,2,1:T(8,128)(2,1)S(1)} %pad_maximum_fusion.5), channel_id=1, source_target_pairs={{1,0},{2,1},{3,2},{4,3},{5,4},{6,5},{7,6},{9,8},{10,9},{11,10},{12... | collective-permute-start | bytes 221192 | tf_op jit(solution)/shard_map/ppermute | solution.py:29
  93.3 10.0 collective-permute-start.10
  95.3 38.7 %collective-permute-start.2 = (f32[6,2048]{1,0:T(8,128)S(1)}, f32[6,2048]{1,0:T(8,128)S(1)}, u32[]{:S(2)}, u32[]{:S(2)}) collective-permute-start(f32[6,2048]{1,0:T(8,128)S(1)} %get-tuple-element.39), channel_id=1, source_target_pairs={{8,0},{16,8},{24,16},{32,24},{40,32},{48,40},{56,48},{64,56},{72,6... | collective-permute-start | bytes 147464 | tf_op jit(solution)/shard_map/ppermute | solution.py:37
  101.4 32.6 %collective-permute-start.3 = (f32[6,2048]{1,0:T(8,128)S(1)}, f32[6,2048]{1,0:T(8,128)S(1)}, u32[]{:S(2)}, u32[]{:S(2)}) collective-permute-start(f32[6,2048]{1,0:T(8,128)S(1)} %get-tuple-element.40), channel_id=1, source_target_pairs={{0,8},{8,16},{16,24},{24,32},{32,40},{40,48},{48,56},{56,64},{64,7... | collective-permute-start | bytes 147464 | tf_op jit(solution)/shard_map/ppermute | solution.py:37
  134.7 10.0 collective-permute-start.5
  140.7 8.1 collective-permute-start.4
  144.6 439.6 %all-reduce.9.cloned.1.call-start = ((), (), s32[]{:S(2)}) async-start(), calls=%async_computation.1 | async-start | bytes 131072 | tf_op jit(solution)/shard_map/psum | solution.py:111
  148.8 139.7 %collective-permute-start.7 = (bf16[6,3,1,2048]{3,0,2,1:T(8,128)(2,1)S(1)}, bf16[6,3,1,2048]{3,0,2,1:T(8,128)(2,1)S(1)}, u32[]{:S(2)}, u32[]{:S(2)}) collective-permute-start(bf16[6,3,1,2048]{3,0,2,1:T(8,128)(2,1)S(1)} %pad_maximum_fusion.4), channel_id=1, source_target_pairs={{1,0},{2,1},{3,2},{4,3},{5,4},{6,5},{7,6},{9,8},{10,9},{11,10},{12... | collective-permute-start | bytes 221192 | tf_op jit(solution)/shard_map/ppermute | solution.py:29
  150.9 137.6 %collective-permute-start.6 = (bf16[6,3,1,2048]{3,0,2,1:T(8,128)(2,1)S(1)}, bf16[6,3,1,2048]{3,0,2,1:T(8,128)(2,1)S(1)}, u32[]{:S(2)}, u32[]{:S(2)}) collective-permute-start(bf16[6,3,1,2048]{3,0,2,1:T(8,128)(2,1)S(1)} %pad_maximum_fusion.4), channel_id=1, source_target_pairs={{0,1},{1,2},{2,3},{3,4},{4,5},{5,6},{6,7},{8,9},{9,10},{10,11},{11... | collective-permute-start | bytes 221192 | tf_op jit(solution)/shard_map/ppermute | solution.py:28
  431.1 8.3 collective-permute-start.15
  440.0 7.9 collective-permute-start.17
  442.0 7.9 collective-permute-start.16
  447.9 420.8 %all-reduce.11.cloned.1.call-start = ((), (), s32[]{:S(2)}) async-start(), calls=%async_computation.2 | async-start | bytes 131072 | tf_op jit(solution)/shard_map/psum | solution.py:111
  449.9 136.9 %collective-permute-start.19 = (bf16[6,3,1,2048]{3,0,2,1:T(8,128)(2,1)S(1)}, bf16[6,3,1,2048]{3,0,2,1:T(8,128)(2,1)S(1)}, u32[]{:S(2)}, u32[]{:S(2)}) collective-permute-start(bf16[6,3,1,2048]{3,0,2,1:T(8,128)(2,1)S(1)} %pad_maximum_fusion.6), channel_id=1, source_target_pairs={{1,0},{2,1},{3,2},{4,3},{5,4},{6,5},{7,6},{9,8},{10,9},{11,10},{12... | collective-permute-start | bytes 221192 | tf_op jit(solution)/shard_map/ppermute | solution.py:29
  452.0 134.9 %collective-permute-start.18 = (bf16[6,3,1,2048]{3,0,2,1:T(8,128)(2,1)S(1)}, bf16[6,3,1,2048]{3,0,2,1:T(8,128)(2,1)S(1)}, u32[]{:S(2)}, u32[]{:S(2)}) collective-permute-start(bf16[6,3,1,2048]{3,0,2,1:T(8,128)(2,1)S(1)} %pad_maximum_fusion.6), channel_id=1, source_target_pairs={{0,1},{1,2},{2,3},{3,4},{4,5},{5,6},{6,7},{8,9},{9,10},{10,11},{11... | collective-permute-start | bytes 221192 | tf_op jit(solution)/shard_map/ppermute | solution.py:28
  715.6 8.3 collective-permute-start.23
  726.4 7.9 collective-permute-start.24
  734.4 136.9 %collective-permute-start.27 = (bf16[6,3,1,2048]{3,0,2,1:T(8,128)(2,1)S(1)}, bf16[6,3,1,2048]{3,0,2,1:T(8,128)(2,1)S(1)}, u32[]{:S(2)}, u32[]{:S(2)}) collective-permute-start(bf16[6,3,1,2048]{3,0,2,1:T(8,128)(2,1)S(1)} %pad_maximum_fusion.7), channel_id=1, source_target_pairs={{1,0},{2,1},{3,2},{4,3},{5,4},{6,5},{7,6},{9,8},{10,9},{11,10},{12... | collective-permute-start | bytes 221192 | tf_op jit(solution)/shard_map/ppermute | solution.py:29
  736.3 135.0 %collective-permute-start.26 = (bf16[6,3,1,2048]{3,0,2,1:T(8,128)(2,1)S(1)}, bf16[6,3,1,2048]{3,0,2,1:T(8,128)(2,1)S(1)}, u32[]{:S(2)}, u32[]{:S(2)}) collective-permute-start(bf16[6,3,1,2048]{3,0,2,1:T(8,128)(2,1)S(1)} %pad_maximum_fusion.7), channel_id=1, source_target_pairs={{0,1},{1,2},{2,3},{3,4},{4,5},{5,6},{6,7},{8,9},{9,10},{10,11},{11... | collective-permute-start | bytes 221192 | tf_op jit(solution)/shard_map/ppermute | solution.py:28
  1000.1 8.3 collective-permute-start.31
  (17 other events, 345.9 us)
Sparse Core Ops, SparseCore 0:
  144.8 141.0 all-reduce.6
  448.0 136.1 all-reduce.8
  732.5 136.1 all-reduce.10

commit v3 on v0

--- a/solution.py
+++ b/solution.py
@@ -3,8 +3,78 @@
 import jax
 import jax.numpy as jnp
 from jax import lax
+from jax.experimental import pallas as pl
+from jax.experimental.pallas import tpu as pltpu
 from jax.sharding import Mesh
 from jax.sharding import PartitionSpec as P
+
+TILE = 1024
+
+
+def _gather_kernel(field_ref, idx_ref, out_ref):
+    rows, cols = field_ref.shape
+    idx = idx_ref[...]
+    tile = idx.shape[1]
+    high = lax.shift_right_logical(idx, 7)
+    low = jnp.bitwise_and(idx, 127)
+    pick_col = (lax.broadcasted_iota(jnp.int32, (cols, tile), 0) == high).astype(jnp.bfloat16)
+    pick_lane = (lax.broadcasted_iota(jnp.int32, (128, tile), 0) == low).astype(jnp.float32)
+    spread = jnp.dot(field_ref[...], pick_col, preferred_element_type=jnp.float32)
+    spread = spread.reshape(rows // 128, 128, tile) * pick_lane[None]
+    out_ref[...] = jnp.sum(spread, axis=1).astype(out_ref.dtype)
+
+
+def gather_field(field_t, idx_row):
+    rows, cols = field_t.shape
+    slots = idx_row.shape[1]
+    dofs = rows // 128
+    return pl.pallas_call(
+        _gather_kernel,
+        grid=(slots // TILE,),
+        in_specs=[
+            pl.BlockSpec((rows, cols), lambda i: (0, 0)),
+            pl.BlockSpec((1, TILE), lambda i: (0, i)),
+        ],
+        out_specs=pl.BlockSpec((dofs, TILE), lambda i: (0, i)),
+        out_shape=jax.ShapeDtypeStruct((dofs, slots), field_t.dtype),
+    )(field_t, idx_row)
+
+
+def _scatter_kernel(push_ref, idx_row_ref, idx_col_ref, out_ref):
+    @pl.when(pl.program_id(0) == 0)
+    def _():
+        out_ref[...] = jnp.zeros_like(out_ref)
+
+    rows, cols = out_ref.shape
+    push = push_ref[...]
+    dofs, tile = push.shape
+    low = jnp.bitwise_and(idx_row_ref[...], 127)
+    high = lax.shift_right_logical(idx_col_ref[...], 7)
+    pick_lane = (lax.broadcasted_iota(jnp.int32, (128, tile), 0) == low).astype(jnp.float32)
+    pick_col = (lax.broadcasted_iota(jnp.int32, (tile, cols), 1) == high).astype(jnp.bfloat16)
+    spread = (push[:, None, :] * pick_lane[None]).reshape(rows, tile)
+    upper = spread.astype(jnp.bfloat16)
+    lower = (spread - upper.astype(jnp.float32)).astype(jnp.bfloat16)
+    out_ref[...] += jnp.dot(upper, pick_col, preferred_element_type=jnp.float32) + jnp.dot(
+        lower, pick_col, preferred_element_type=jnp.float32
+    )
+
+
+def scatter_field(push_t, idx_row, idx_col, cols):
+    dofs, slots = push_t.shape
+    rows = dofs * 128
+    return pl.pallas_call(
+        _scatter_kernel,
+        grid=(slots // TILE,),
+        in_specs=[
+            pl.BlockSpec((dofs, TILE), lambda i: (0, i)),
+            pl.BlockSpec((1, TILE), lambda i: (0, i)),
+            pl.BlockSpec((TILE, 1), lambda i: (i, 0)),
+        ],
+        out_specs=pl.BlockSpec((rows, cols), lambda i: (0, 0)),
+        out_shape=jax.ShapeDtypeStruct((rows, cols), jnp.float32),
+        compiler_params=pltpu.CompilerParams(dimension_semantics=("arbitrary",)),
+    )(push_t, idx_row, idx_col)
 
 CB = 64
 GB = 64
@@ -80,29 +150,37 @@
     grains = free_velocity.shape[1]
     live_mask = (jnp.arange(blocks, dtype=jnp.int32) < block_count[0]).astype(jnp.float32)[:, None]
 
+    slot_index = grain_slots.reshape(1, blocks * GB)
+    slot_column = grain_slots.reshape(blocks * GB, 1)
+
+    def to_tiles(grain_field):
+        return jnp.transpose(grain_field.reshape(6, grains // 128, 128), (0, 2, 1))
+
+    def from_tiles(tiles):
+        return jnp.transpose(tiles.reshape(6, 128, grains // 128), (0, 2, 1)).reshape(6, grains)
+
     def forward(grain_field):
-        nearby = with_halo(grain_field.reshape(6, 1, 1, grains), ((GX, 1), (GY, 2)), 1)
-        nearby = nearby.reshape(6, 9 * grains)
-        picked = jnp.take(nearby, grain_slots, axis=1)
-        picked = jnp.transpose(picked, (1, 0, 2)).reshape(blocks, 6 * GB)
+        own = to_tiles(grain_field).reshape(6 * 128, 1, 1, grains // 128)
+        nearby = with_halo(own, ((GX, 1), (GY, 2)), 1)
+        nearby = nearby.reshape(6 * 128, 9 * grains // 128)
+        picked = gather_field(nearby, slot_index)
+        picked = jnp.transpose(picked.reshape(6, blocks, GB), (1, 0, 2)).reshape(blocks, 6 * GB)
         return jnp.einsum("bij,bj->bi", jacobian, picked, preferred_element_type=jnp.float32)
 
     def backward(impulse_field):
         pushes = jnp.einsum(
             "bij,bi->bj", jacobian, impulse_field, preferred_element_type=jnp.float32
         )
-        pushes = jnp.transpose(pushes.reshape(blocks, 6, GB), (1, 0, 2))
-        nearby = jnp.zeros((6, 9 * grains), jnp.float32).at[:, grain_slots].add(pushes)
-        nearby = nearby.reshape(6, 3, 3, grains)
+        pushes = jnp.transpose(pushes.reshape(blocks, 6, GB), (1, 0, 2)).reshape(6, blocks * GB)
+        nearby = scatter_field(pushes, slot_index, slot_column, 9 * grains // 128)
+        nearby = nearby.reshape(6 * 128, 3, 3, grains // 128)
         row_sums = nearby[:, :, 1]
         for step_y in (-1, 1):
-            row_sums = row_sums + from_behind(
-                nearby[:, :, step_y + 1].astype(jnp.bfloat16), GY, step_y
-            ).astype(jnp.float32)
+            row_sums = row_sums + from_behind(nearby[:, :, step_y + 1], GY, step_y)
         summed = row_sums[:, 1]
         for step_x in (-1, 1):
             summed = summed + from_behind(row_sums[:, step_x + 1], GX, step_x)
-        return summed
+        return from_tiles(summed)
 
     constraint_bias = velocity_bias + forward(free_velocity.astype(jnp.bfloat16))
     extrapolated = impulse_start * live_mask

time: 711 us -> 444 us (0.62)
  other arithmetic: 300 us -> 104 us
  local copies, waits for them, and re-layouts: 165 us -> 27.6 us
  Pallas kernels: 0 us -> 69.3 us
  waiting for transfers between devices: 48.8 us -> 36.7 us
  blocking collectives: 88.2 us -> 99.9 us
    scatter-add x4 -> x0, other arithmetic: 194 us -> none  [backward(): jnp.zeros((6, 9 * grains), jnp.float32).at[:, grain_slots].add(pushes)]
    gather x8 -> x0, local copies, waits for them, and re-layouts: 108 us -> none  [forward(): picked = jnp.take(nearby, grain_slots, axis=1)]
    pallas_call x0 -> x8, Pallas kernels: none -> 69.3 us  [the longest x4 42.8 us: scatter_field(): pl.pallas_call(_scatter_kernel, grid=(slots // TILE,), in_specs=[pl.Block...]
    transpose x4 -> x8, local copies, waits for them, and re-layouts: 18 us -> 1.24 us  [the longest x4 0.7 us: backward(): jnp.transpose(pushes.reshape(blocks, 6, GB), (1, 0, 2))]
    concatenate x4, local copies, waits for them, and re-layouts: 13.9 us -> 0.01 us  [with_halo(): array = jnp.concatenate([before, array, after], axis=dim)]
    psum x12, blocking collectives: 88.2 us -> 99.9 us  [one_axis_at_a_time(): array = lax.psum(array, axis)]
    ppermute x8, starting transfers between devices: 19.1 us -> 30.2 us  [with_halo(): after = lax.ppermute(leading, axis, down)]
    ppermute x16, waiting for transfers between devices: 40.8 us -> 32.3 us  [from_behind(): return lax.ppermute(block, axis, route)]
  transfers between devices with their start and end apart: 32 -> 32, of which waited for: 14 -> 18; matrix products, arithmetic and copies ran while one was open for 15% -> 5% of each run, Pallas kernels for 0% -> 4%
where the time goes in v3:
time: 444 us; the launch traced here: 441 us
  other arithmetic  104 us (23%)
  blocking collectives  99.9 us (22%)
  starting transfers between devices  96.8 us (22%)
  Pallas kernels  69.3 us (16%)
  waiting for transfers between devices  36.7 us (8%)
  local copies, waits for them, and re-layouts  27.6 us (6%)
  between operations  6.09 us (1%)
    psum x12, blocking collectives, one_axis_at_a_time(): array = lax.psum(array, axis)  99.9 us
    unnamed x14, other arithmetic  97.8 us
    ppermute x16, starting transfers between devices, from_behind(): return lax.ppermute(block, axis, route)  49.2 us
    pallas_call x4, Pallas kernels, scatter_field(): pl.pallas_call(_scatter_kernel, grid=(slots // TILE,), in_specs=[pl.Block...  42.8 us
    ppermute x16, waiting for transfers between devices, from_behind(): return lax.ppermute(block, axis, route)  32.3 us
    ppermute x8, starting transfers between devices, with_halo(): after = lax.ppermute(leading, axis, down)  30.2 us
    pallas_call x4, Pallas kernels, gather_field(): pl.pallas_call(_gather_kernel, grid=(slots // TILE,), in_specs=[pl.BlockS...  26.5 us
    ppermute x8, starting transfers between devices, with_halo(): before = lax.ppermute(last, axis, up)  17.3 us
  transfers between devices with their start and end apart: 32, of which 18 were waited for; matrix products, arithmetic and copies ran while one was open for 5% of the time, Pallas kernels for 4%

profile of v3, /device:TPU:34, one launch (start us, length us, event | category | flops | bytes accessed | tf_op | source)
XLA Modules:
  0.0 440.8 jit_solution(13860086190756979586)
XLA Ops:
  17.3 9.1 %fusion = f32[128,384]{1,0:T(8,128)S(1)} fusion(bf16[128,192,384]{2,1,0:T(8,128)(2,1)} %param.8, f32[128,192]{1,0:T(8,128)S(1)} %copy.136), kind=kLoop, calls=%fused_computation.8 | loop fusion | flops 28262400 | bytes 19169280
  27.7 10.7 %shard_map.95 = f32[768,144]{1,0:T(8,128)} custom-call(f32[6,8192]{1,0:T(8,128)} %reshape.136.push_ref, s32[1,8192]{1,0:T(1,128)} %reshape.137.idx_row_ref.idx_ref, s32[8192,1]{1,0:T(8,128)} %reshape.193.idx_col_ref), custom_call_target="tpu_custom_call" | custom-call | tf_op jit(solution)/shard_map/pallas_call | solution.py:66
  65.9 6.6 %shard_map.97 = bf16[6,8192]{1,0:T(8,128)(2,1)} custom-call(bf16[768,144]{1,0:T(8,128)(2,1)} %copy.76.field_ref, s32[1,8192]{1,0:T(1,128)} %reshape.137.idx_row_ref.idx_ref), custom_call_target="tpu_custom_call" | custom-call | tf_op jit(solution)/shard_map/pallas_call | solution.py:31
  85.8 9.7 %all-reduce.8 = (f32[]{:T(128)}, f32[]{:T(128)}) all-reduce(f32[]{:T(128)} %get-tuple-element.67, f32[]{:T(128)} %get-tuple-element.65), channel_id=1, replica_groups=mesh['gx_0'=4,'gx_1'=4,'gy_0'=4,'gy_1'=2] {'gx_0'}, use_global_device_ids=true, to_apply=%region_1.0 | all-reduce | flops 2 | bytes 16 | tf_op jit(solution)/shard_map/psum | solution.py:111
  95.5 13.3 %all-reduce.5 = (f32[]{:T(128)}, f32[]{:T(128)}) all-reduce(f32[]{:T(128)} %get-tuple-element.20, f32[]{:T(128)} %get-tuple-element.21), channel_id=1, replica_groups=mesh['gx_0'=4,'gx_1'=4,'gy_0'=4,'gy_1'=2] {'gx_1'}, use_global_device_ids=true, to_apply=%region_2.0 | all-reduce | flops 2 | bytes 16 | tf_op jit(solution)/shard_map/psum | solution.py:111
  108.8 9.2 %all-reduce.2 = (f32[]{:T(128)}, f32[]{:T(128)}) all-reduce(f32[]{:T(128)} %get-tuple-element.14, f32[]{:T(128)} %get-tuple-element.15), channel_id=1, replica_groups=mesh['gx_0'=4,'gx_1'=4,'gy_0'=4,'gy_1'=2] {'gy_0'}, use_global_device_ids=true, to_apply=%region_3.0 | all-reduce | flops 2 | bytes 16 | tf_op jit(solution)/shard_map/psum | solution.py:111
  123.6 6.6 %shard_map.96 = bf16[6,8192]{1,0:T(8,128)(2,1)} custom-call(bf16[768,144]{1,0:T(8,128)(2,1)} %copy.73.field_ref, s32[1,8192]{1,0:T(1,128)} %reshape.137.idx_row_ref.idx_ref), custom_call_target="tpu_custom_call" | custom-call | tf_op jit(solution)/shard_map/pallas_call | solution.py:31
  131.6 29.1 %fusion.5 = (f32[128,192]{1,0:T(8,128)S(1)}, f32[128,192]{1,0:T(8,128)S(1)}) fusion(f32[128,384]{1,0:T(8,128)S(1)} %copy.138, bf16[128,192,384]{2,1,0:T(8,128)(2,1)} %param.8, f32[128,384]{1,0:T(8,128)S(1)} %copy.137), kind=kLoop, calls=%fused_computation.13 | loop fusion | flops 47136768 | bytes 19464192
  161.8 9.1 %fusion.1 = f32[128,384]{1,0:T(8,128)S(1)} fusion(bf16[128,192,384]{2,1,0:T(8,128)(2,1)} %param.8, f32[128,192]{1,0:T(8,128)S(1)} %copy.139), kind=kLoop, calls=%fused_computation.9 | loop fusion | flops 28262400 | bytes 19169280
  172.1 10.7 %shard_map.98 = f32[768,144]{1,0:T(8,128)} custom-call(f32[6,8192]{1,0:T(8,128)} %reshape.153.push_ref, s32[1,8192]{1,0:T(1,128)} %reshape.137.idx_row_ref.idx_ref, s32[8192,1]{1,0:T(8,128)} %reshape.193.idx_col_ref), custom_call_target="tpu_custom_call" | custom-call | tf_op jit(solution)/shard_map/pallas_call | solution.py:66
  219.4 9.0 %all-reduce.7 = (f32[]{:T(128)}, f32[]{:T(128)}) all-reduce(f32[]{:T(128)} %get-tuple-element.36, f32[]{:T(128)} %get-tuple-element.62), channel_id=1, replica_groups=mesh['gx_0'=4,'gx_1'=4,'gy_0'=4,'gy_1'=2] {'gx_0'}, use_global_device_ids=true, to_apply=%region_11.12 | all-reduce | flops 2 | bytes 16 | tf_op jit(solution)/shard_map/psum | solution.py:111
  228.4 12.8 %all-reduce.4 = (f32[]{:T(128)}, f32[]{:T(128)}) all-reduce(f32[]{:T(128)} %get-tuple-element.18, f32[]{:T(128)} %get-tuple-element.19), channel_id=1, replica_groups=mesh['gx_0'=4,'gx_1'=4,'gy_0'=4,'gy_1'=2] {'gx_1'}, use_global_device_ids=true, to_apply=%region_12.13 | all-reduce | flops 2 | bytes 16 | tf_op jit(solution)/shard_map/psum | solution.py:111
  241.1 7.4 %all-reduce.1 = (f32[]{:T(128)}, f32[]{:T(128)}) all-reduce(f32[]{:T(128)} %get-tuple-element.12, f32[]{:T(128)} %get-tuple-element.13), channel_id=1, replica_groups=mesh['gx_0'=4,'gx_1'=4,'gy_0'=4,'gy_1'=2] {'gy_0'}, use_global_device_ids=true, to_apply=%region_13.14 | all-reduce | flops 2 | bytes 16 | tf_op jit(solution)/shard_map/psum | solution.py:111
  254.1 6.6 %shard_map.99 = bf16[6,8192]{1,0:T(8,128)(2,1)} custom-call(bf16[768,144]{1,0:T(8,128)(2,1)} %copy.83.field_ref, s32[1,8192]{1,0:T(1,128)} %reshape.137.idx_row_ref.idx_ref), custom_call_target="tpu_custom_call" | custom-call | tf_op jit(solution)/shard_map/pallas_call | solution.py:31
  262.1 15.7 %fusion.6 = f32[128,192]{1,0:T(8,128)S(1)} fusion(f32[128,384]{1,0:T(8,128)S(1)} %copy.140, bf16[128,192,384]{2,1,0:T(8,128)(2,1)} %param.8), kind=kLoop, calls=%fused_computation.14 | loop fusion | flops 28286976 | bytes 19169280
  278.7 9.1 %fusion.2 = f32[128,384]{1,0:T(8,128)S(1)} fusion(bf16[128,192,384]{2,1,0:T(8,128)(2,1)} %param.8, f32[128,192]{1,0:T(8,128)S(1)} %copy.141), kind=kLoop, calls=%fused_computation.10 | loop fusion | flops 28262400 | bytes 19169280
  289.1 10.7 %shard_map.100 = f32[768,144]{1,0:T(8,128)} custom-call(f32[6,8192]{1,0:T(8,128)} %reshape.163.push_ref, s32[1,8192]{1,0:T(1,128)} %reshape.137.idx_row_ref.idx_ref, s32[8192,1]{1,0:T(8,128)} %reshape.193.idx_col_ref), custom_call_target="tpu_custom_call" | custom-call | tf_op jit(solution)/shard_map/pallas_call | solution.py:66
  337.3 8.6 %all-reduce.6 = (f32[]{:T(128)}, f32[]{:T(128)}) all-reduce(f32[]{:T(128)} %get-tuple-element.32, f32[]{:T(128)} %get-tuple-element.59), channel_id=1, replica_groups=mesh['gx_0'=4,'gx_1'=4,'gy_0'=4,'gy_1'=2] {'gx_0'}, use_global_device_ids=true, to_apply=%region_21.22 | all-reduce | flops 2 | bytes 16 | tf_op jit(solution)/shard_map/psum | solution.py:111
  345.9 13.1 %all-reduce.3 = (f32[]{:T(128)}, f32[]{:T(128)}) all-reduce(f32[]{:T(128)} %get-tuple-element.16, f32[]{:T(128)} %get-tuple-element.17), channel_id=1, replica_groups=mesh['gx_0'=4,'gx_1'=4,'gy_0'=4,'gy_1'=2] {'gx_1'}, use_global_device_ids=true, to_apply=%region_22.23 | all-reduce | flops 2 | bytes 16 | tf_op jit(solution)/shard_map/psum | solution.py:111
  359.0 7.2 %all-reduce = (f32[]{:T(128)}, f32[]{:T(128)}) all-reduce(f32[]{:T(128)} %get-tuple-element.10, f32[]{:T(128)} %get-tuple-element.11), channel_id=1, replica_groups=mesh['gx_0'=4,'gx_1'=4,'gy_0'=4,'gy_1'=2] {'gy_0'}, use_global_device_ids=true, to_apply=%region_23.24 | all-reduce | flops 2 | bytes 16 | tf_op jit(solution)/shard_map/psum | solution.py:111
  371.6 6.6 %shard_map.101 = bf16[6,8192]{1,0:T(8,128)(2,1)} custom-call(bf16[768,144]{1,0:T(8,128)(2,1)} %copy.90.field_ref, s32[1,8192]{1,0:T(1,128)} %reshape.137.idx_row_ref.idx_ref), custom_call_target="tpu_custom_call" | custom-call | tf_op jit(solution)/shard_map/pallas_call | solution.py:31
  379.6 15.7 %fusion.7 = f32[128,192]{1,0:T(8,128)S(1)} fusion(f32[128,384]{1,0:T(8,128)S(1)} %copy.142, bf16[128,192,384]{2,1,0:T(8,128)(2,1)} %param.8), kind=kLoop, calls=%fused_computation.15 | loop fusion | flops 28286976 | bytes 19169280
  396.3 9.1 %fusion.3 = f32[128,384]{1,0:T(8,128)S(1)} fusion(bf16[128,192,384]{2,1,0:T(8,128)(2,1)} %param.8, f32[128,192]{1,0:T(8,128)S(1)} %copy.143), kind=kLoop, calls=%fused_computation.11 | loop fusion | flops 28262400 | bytes 19169280
  406.6 10.7 %shard_map.102 = f32[768,144]{1,0:T(8,128)} custom-call(f32[6,8192]{1,0:T(8,128)} %reshape.173.push_ref, s32[1,8192]{1,0:T(1,128)} %reshape.137.idx_row_ref.idx_ref, s32[8192,1]{1,0:T(8,128)} %reshape.193.idx_col_ref), custom_call_target="tpu_custom_call" | custom-call | tf_op jit(solution)/shard_map/pallas_call | solution.py:66
  (185 shorter events, 178.3 us)
Async XLA Ops:
  1.6 54.6 %collective-permute-start.9 = (bf16[768,1,1,16]{0,3,2,1:T(8,128)(2,1)S(1)}, bf16[768,1,1,16]{0,3,2,1:T(8,128)(2,1)S(1)}, u32[]{:S(2)}, u32[]{:S(2)}) collective-permute-start(bf16[768,1,1,16]{0,3,2,1:T(8,128)(2,1)S(1)} %reshape.148), channel_id=1, source_target_pairs={{8,0},{16,8},{24,16},{32,24},{40,32},{48,40},{56,48},{64,56},{72,6... | collective-permute-start | bytes 73736 | tf_op jit(solution)/shard_map/ppermute | solution.py:98
  6.0 38.1 %collective-permute-start.8 = (bf16[768,1,1,16]{0,3,2,1:T(8,128)(2,1)S(1)}, bf16[768,1,1,16]{0,3,2,1:T(8,128)(2,1)S(1)}, u32[]{:S(2)}, u32[]{:S(2)}) collective-permute-start(bf16[768,1,1,16]{0,3,2,1:T(8,128)(2,1)S(1)} %reshape.148), channel_id=1, source_target_pairs={{0,8},{8,16},{16,24},{24,32},{32,40},{40,48},{48,56},{56,64},{64,7... | collective-permute-start | bytes 73736 | tf_op jit(solution)/shard_map/ppermute | solution.py:97
  48.2 12.3 %collective-permute-start.2 = (f32[768,16]{0,1:T(8,128)S(1)}, f32[768,16]{0,1:T(8,128)S(1)}, u32[]{:S(2)}, u32[]{:S(2)}) collective-permute-start(f32[768,16]{0,1:T(8,128)S(1)} %get-tuple-element.56), channel_id=1, source_target_pairs={{8,0},{16,8},{24,16},{32,24},{40,32},{48,40},{56,48},{64,56},{72,6... | collective-permute-start | bytes 147464 | tf_op jit(solution)/shard_map/ppermute | solution.py:106
  54.2 8.1 %collective-permute-start.3 = (f32[768,16]{0,1:T(8,128)S(1)}, f32[768,16]{0,1:T(8,128)S(1)}, u32[]{:S(2)}, u32[]{:S(2)}) collective-permute-start(f32[768,16]{0,1:T(8,128)S(1)} %get-tuple-element.57), channel_id=1, source_target_pairs={{0,8},{8,16},{16,24},{24,32},{32,40},{40,48},{48,56},{56,64},{64,7... | collective-permute-start | bytes 147464 | tf_op jit(solution)/shard_map/ppermute | solution.py:106
  56.2 8.8 %collective-permute-start.11 = (bf16[768,3,1,16]{0,3,2,1:T(8,128)(2,1)S(1)}, bf16[768,3,1,16]{0,3,2,1:T(8,128)(2,1)S(1)}, u32[]{:S(2)}, u32[]{:S(2)}) collective-permute-start(bf16[768,3,1,16]{0,3,2,1:T(8,128)(2,1)S(1)} %constant_dynamic-update-slice_fusion.3), channel_id=1, source_target_pairs={{1,0},{2,1},{3,2},{4,3},{5,4},{6,5},{7,6},{9,8},{10,9},{11,10},{12... | collective-permute-start | bytes 221192 | tf_op jit(solution)/shard_map/ppermute | solution.py:98
  58.1 6.8 %collective-permute-start.10 = (bf16[768,3,1,16]{0,3,2,1:T(8,128)(2,1)S(1)}, bf16[768,3,1,16]{0,3,2,1:T(8,128)(2,1)S(1)}, u32[]{:S(2)}, u32[]{:S(2)}) collective-permute-start(bf16[768,3,1,16]{0,3,2,1:T(8,128)(2,1)S(1)} %constant_dynamic-update-slice_fusion.3), channel_id=1, source_target_pairs={{0,1},{1,2},{2,3},{3,4},{4,5},{5,6},{6,7},{8,9},{9,10},{10,11},{11... | collective-permute-start | bytes 221192 | tf_op jit(solution)/shard_map/ppermute | solution.py:97
  63.0 16.8 %collective-permute-start.4 = (bf16[768,1,1,16]{0,3,2,1:T(8,128)(2,1)S(1)}, bf16[768,1,1,16]{0,3,2,1:T(8,128)(2,1)S(1)}, u32[]{:S(2)}, u32[]{:S(2)}) collective-permute-start(bf16[768,1,1,16]{0,3,2,1:T(8,128)(2,1)S(1)} %reshape.143), channel_id=1, source_target_pairs={{0,8},{8,16},{16,24},{24,32},{32,40},{40,48},{48,56},{56,64},{64,7... | collective-permute-start | bytes 73736 | tf_op jit(solution)/shard_map/ppermute | solution.py:97
  73.8 7.5 %collective-permute-start.5 = (bf16[768,1,1,16]{0,3,2,1:T(8,128)(2,1)S(1)}, bf16[768,1,1,16]{0,3,2,1:T(8,128)(2,1)S(1)}, u32[]{:S(2)}, u32[]{:S(2)}) collective-permute-start(bf16[768,1,1,16]{0,3,2,1:T(8,128)(2,1)S(1)} %reshape.143), channel_id=1, source_target_pairs={{8,0},{16,8},{24,16},{32,24},{40,32},{48,40},{56,48},{64,56},{72,6... | collective-permute-start | bytes 73736 | tf_op jit(solution)/shard_map/ppermute | solution.py:98
  81.4 41.2 %collective-permute-start.7 = (bf16[768,3,1,16]{0,3,2,1:T(8,128)(2,1)S(1)}, bf16[768,3,1,16]{0,3,2,1:T(8,128)(2,1)S(1)}, u32[]{:S(2)}, u32[]{:S(2)}) collective-permute-start(bf16[768,3,1,16]{0,3,2,1:T(8,128)(2,1)S(1)} %constant_dynamic-update-slice_fusion), channel_id=1, source_target_pairs={{1,0},{2,1},{3,2},{4,3},{5,4},{6,5},{7,6},{9,8},{10,9},{11,10},{12... | collective-permute-start | bytes 221192 | tf_op jit(solution)/shard_map/ppermute | solution.py:98
  83.3 39.3 %collective-permute-start.6 = (bf16[768,3,1,16]{0,3,2,1:T(8,128)(2,1)S(1)}, bf16[768,3,1,16]{0,3,2,1:T(8,128)(2,1)S(1)}, u32[]{:S(2)}, u32[]{:S(2)}) collective-permute-start(bf16[768,3,1,16]{0,3,2,1:T(8,128)(2,1)S(1)} %constant_dynamic-update-slice_fusion), channel_id=1, source_target_pairs={{0,1},{1,2},{2,3},{3,4},{4,5},{5,6},{6,7},{8,9},{9,10},{10,11},{11... | collective-permute-start | bytes 221192 | tf_op jit(solution)/shard_map/ppermute | solution.py:97
  184.2 6.7 %collective-permute-start.12 = (f32[768,3,16]{0,2,1:T(8,128)S(1)}, f32[768,3,16]{0,2,1:T(8,128)S(1)}, u32[]{:S(2)}, u32[]{:S(2)}) collective-permute-start(f32[768,3,16]{0,2,1:T(8,128)S(1)} %get-tuple-element.46), channel_id=1, source_target_pairs={{1,0},{2,1},{3,2},{4,3},{5,4},{6,5},{7,6},{9,8},{10,9},{11,10},{12... | collective-permute-start | bytes 442376 | tf_op jit(solution)/shard_map/ppermute | solution.py:106
  196.8 8.1 %collective-permute-start.15 = (f32[768,16]{0,1:T(8,128)S(1)}, f32[768,16]{0,1:T(8,128)S(1)}, u32[]{:S(2)}, u32[]{:S(2)}) collective-permute-start(f32[768,16]{0,1:T(8,128)S(1)} %get-tuple-element.55), channel_id=1, source_target_pairs={{0,8},{8,16},{16,24},{24,32},{32,40},{40,48},{48,56},{56,64},{64,7... | collective-permute-start | bytes 147464 | tf_op jit(solution)/shard_map/ppermute | solution.py:106
  205.6 8.0 %collective-permute-start.16 = (bf16[768,1,1,16]{0,3,2,1:T(8,128)(2,1)S(1)}, bf16[768,1,1,16]{0,3,2,1:T(8,128)(2,1)S(1)}, u32[]{:S(2)}, u32[]{:S(2)}) collective-permute-start(bf16[768,1,1,16]{0,3,2,1:T(8,128)(2,1)S(1)} %reshape.158), channel_id=1, source_target_pairs={{0,8},{8,16},{16,24},{24,32},{32,40},{40,48},{48,56},{56,64},{64,7... | collective-permute-start | bytes 73736 | tf_op jit(solution)/shard_map/ppermute | solution.py:97
  207.5 7.5 %collective-permute-start.17 = (bf16[768,1,1,16]{0,3,2,1:T(8,128)(2,1)S(1)}, bf16[768,1,1,16]{0,3,2,1:T(8,128)(2,1)S(1)}, u32[]{:S(2)}, u32[]{:S(2)}) collective-permute-start(bf16[768,1,1,16]{0,3,2,1:T(8,128)(2,1)S(1)} %reshape.158), channel_id=1, source_target_pairs={{8,0},{16,8},{24,16},{32,24},{40,32},{48,40},{56,48},{64,56},{72,6... | collective-permute-start | bytes 73736 | tf_op jit(solution)/shard_map/ppermute | solution.py:98
  215.1 38.0 %collective-permute-start.19 = (bf16[768,3,1,16]{0,3,2,1:T(8,128)(2,1)S(1)}, bf16[768,3,1,16]{0,3,2,1:T(8,128)(2,1)S(1)}, u32[]{:S(2)}, u32[]{:S(2)}) collective-permute-start(bf16[768,3,1,16]{0,3,2,1:T(8,128)(2,1)S(1)} %constant_dynamic-update-slice_fusion.6), channel_id=1, source_target_pairs={{1,0},{2,1},{3,2},{4,3},{5,4},{6,5},{7,6},{9,8},{10,9},{11,10},{12... | collective-permute-start | bytes 221192 | tf_op jit(solution)/shard_map/ppermute | solution.py:98
  217.0 36.1 %collective-permute-start.18 = (bf16[768,3,1,16]{0,3,2,1:T(8,128)(2,1)S(1)}, bf16[768,3,1,16]{0,3,2,1:T(8,128)(2,1)S(1)}, u32[]{:S(2)}, u32[]{:S(2)}) collective-permute-start(bf16[768,3,1,16]{0,3,2,1:T(8,128)(2,1)S(1)} %constant_dynamic-update-slice_fusion.6), channel_id=1, source_target_pairs={{0,1},{1,2},{2,3},{3,4},{4,5},{5,6},{6,7},{8,9},{9,10},{10,11},{11... | collective-permute-start | bytes 221192 | tf_op jit(solution)/shard_map/ppermute | solution.py:97
  301.2 7.4 %collective-permute-start.20 = (f32[768,3,16]{0,2,1:T(8,128)S(1)}, f32[768,3,16]{0,2,1:T(8,128)S(1)}, u32[]{:S(2)}, u32[]{:S(2)}) collective-permute-start(f32[768,3,16]{0,2,1:T(8,128)S(1)} %get-tuple-element.44), channel_id=1, source_target_pairs={{1,0},{2,1},{3,2},{4,3},{5,4},{6,5},{7,6},{9,8},{10,9},{11,10},{12... | collective-permute-start | bytes 442376 | tf_op jit(solution)/shard_map/ppermute | solution.py:106
  314.7 8.1 %collective-permute-start.23 = (f32[768,16]{0,1:T(8,128)S(1)}, f32[768,16]{0,1:T(8,128)S(1)}, u32[]{:S(2)}, u32[]{:S(2)}) collective-permute-start(f32[768,16]{0,1:T(8,128)S(1)} %get-tuple-element.53), channel_id=1, source_target_pairs={{0,8},{8,16},{16,24},{24,32},{32,40},{40,48},{48,56},{56,64},{64,7... | collective-permute-start | bytes 147464 | tf_op jit(solution)/shard_map/ppermute | solution.py:106
  323.5 8.0 %collective-permute-start.24 = (bf16[768,1,1,16]{0,3,2,1:T(8,128)(2,1)S(1)}, bf16[768,1,1,16]{0,3,2,1:T(8,128)(2,1)S(1)}, u32[]{:S(2)}, u32[]{:S(2)}) collective-permute-start(bf16[768,1,1,16]{0,3,2,1:T(8,128)(2,1)S(1)} %reshape.168), channel_id=1, source_target_pairs={{0,8},{8,16},{16,24},{24,32},{32,40},{40,48},{48,56},{56,64},{64,7... | collective-permute-start | bytes 73736 | tf_op jit(solution)/shard_map/ppermute | solution.py:97
  325.4 7.5 %collective-permute-start.25 = (bf16[768,1,1,16]{0,3,2,1:T(8,128)(2,1)S(1)}, bf16[768,1,1,16]{0,3,2,1:T(8,128)(2,1)S(1)}, u32[]{:S(2)}, u32[]{:S(2)}) collective-permute-start(bf16[768,1,1,16]{0,3,2,1:T(8,128)(2,1)S(1)} %reshape.168), channel_id=1, source_target_pairs={{8,0},{16,8},{24,16},{32,24},{40,32},{48,40},{56,48},{64,56},{72,6... | collective-permute-start | bytes 73736 | tf_op jit(solution)/shard_map/ppermute | solution.py:98
  333.0 37.6 %collective-permute-start.27 = (bf16[768,3,1,16]{0,3,2,1:T(8,128)(2,1)S(1)}, bf16[768,3,1,16]{0,3,2,1:T(8,128)(2,1)S(1)}, u32[]{:S(2)}, u32[]{:S(2)}) collective-permute-start(bf16[768,3,1,16]{0,3,2,1:T(8,128)(2,1)S(1)} %constant_dynamic-update-slice_fusion.9), channel_id=1, source_target_pairs={{1,0},{2,1},{3,2},{4,3},{5,4},{6,5},{7,6},{9,8},{10,9},{11,10},{12... | collective-permute-start | bytes 221192 | tf_op jit(solution)/shard_map/ppermute | solution.py:98
  334.9 35.7 %collective-permute-start.26 = (bf16[768,3,1,16]{0,3,2,1:T(8,128)(2,1)S(1)}, bf16[768,3,1,16]{0,3,2,1:T(8,128)(2,1)S(1)}, u32[]{:S(2)}, u32[]{:S(2)}) collective-permute-start(bf16[768,3,1,16]{0,3,2,1:T(8,128)(2,1)S(1)} %constant_dynamic-update-slice_fusion.9), channel_id=1, source_target_pairs={{0,1},{1,2},{2,3},{3,4},{4,5},{5,6},{6,7},{8,9},{9,10},{10,11},{11... | collective-permute-start | bytes 221192 | tf_op jit(solution)/shard_map/ppermute | solution.py:97
  418.7 7.6 %collective-permute-start.28 = (f32[768,3,16]{0,2,1:T(8,128)S(1)}, f32[768,3,16]{0,2,1:T(8,128)S(1)}, u32[]{:S(2)}, u32[]{:S(2)}) collective-permute-start(f32[768,3,16]{0,2,1:T(8,128)S(1)} %get-tuple-element.42), channel_id=1, source_target_pairs={{1,0},{2,1},{3,2},{4,3},{5,4},{6,5},{7,6},{9,8},{10,9},{11,10},{12... | collective-permute-start | bytes 442376 | tf_op jit(solution)/shard_map/ppermute | solution.py:106
  432.0 8.1 %collective-permute-start.31 = (f32[768,16]{0,1:T(8,128)S(1)}, f32[768,16]{0,1:T(8,128)S(1)}, u32[]{:S(2)}, u32[]{:S(2)}) collective-permute-start(f32[768,16]{0,1:T(8,128)S(1)} %get-tuple-element.51), channel_id=1, source_target_pairs={{0,8},{8,16},{16,24},{24,32},{32,40},{40,48},{48,56},{56,64},{64,7... | collective-permute-start | bytes 147464 | tf_op jit(solution)/shard_map/ppermute | solution.py:106
  (13 other events, 558.5 us)

commit v4 on v3

--- a/solution.py
+++ b/solution.py
@@ -40,7 +40,7 @@
     )(field_t, idx_row)
 
 
-def _scatter_kernel(push_ref, idx_row_ref, idx_col_ref, out_ref):
+def _scatter_kernel(push_ref, idx_ref, out_ref):
     @pl.when(pl.program_id(0) == 0)
     def _():
         out_ref[...] = jnp.zeros_like(out_ref)
@@ -48,19 +48,21 @@
     rows, cols = out_ref.shape
     push = push_ref[...]
     dofs, tile = push.shape
-    low = jnp.bitwise_and(idx_row_ref[...], 127)
-    high = lax.shift_right_logical(idx_col_ref[...], 7)
+    idx = idx_ref[...]
+    low = jnp.bitwise_and(idx, 127)
+    high = lax.shift_right_logical(idx, 7)
     pick_lane = (lax.broadcasted_iota(jnp.int32, (128, tile), 0) == low).astype(jnp.float32)
-    pick_col = (lax.broadcasted_iota(jnp.int32, (tile, cols), 1) == high).astype(jnp.bfloat16)
+    pick_col = (lax.broadcasted_iota(jnp.int32, (cols, tile), 0) == high).astype(jnp.bfloat16)
     spread = (push[:, None, :] * pick_lane[None]).reshape(rows, tile)
     upper = spread.astype(jnp.bfloat16)
     lower = (spread - upper.astype(jnp.float32)).astype(jnp.bfloat16)
-    out_ref[...] += jnp.dot(upper, pick_col, preferred_element_type=jnp.float32) + jnp.dot(
-        lower, pick_col, preferred_element_type=jnp.float32
-    )
-
-
-def scatter_field(push_t, idx_row, idx_col, cols):
+    over_slots = (((1,), (1,)), ((), ()))
+    out_ref[...] += lax.dot_general(
+        upper, pick_col, over_slots, preferred_element_type=jnp.float32
+    ) + lax.dot_general(lower, pick_col, over_slots, preferred_element_type=jnp.float32)
+
+
+def scatter_field(push_t, idx_row, cols):
     dofs, slots = push_t.shape
     rows = dofs * 128
     return pl.pallas_call(
@@ -69,19 +71,19 @@
         in_specs=[
             pl.BlockSpec((dofs, TILE), lambda i: (0, i)),
             pl.BlockSpec((1, TILE), lambda i: (0, i)),
-            pl.BlockSpec((TILE, 1), lambda i: (i, 0)),
         ],
         out_specs=pl.BlockSpec((rows, cols), lambda i: (0, 0)),
         out_shape=jax.ShapeDtypeStruct((rows, cols), jnp.float32),
         compiler_params=pltpu.CompilerParams(dimension_semantics=("arbitrary",)),
-    )(push_t, idx_row, idx_col)
+    )(push_t, idx_row)
+
 
 CB = 64
 GB = 64
 ITERS = 3
-GX_GY = ("gx_0", "gx_1", "gy_0", "gy_1")
-GX = ("gx_0", "gx_1")
-GY = ("gy_0", "gy_1")
+GX = ("gx_0", "gx_1", "gx_2", "gx_3")
+GY = ("gy_0", "gy_1", "gy_2")
+GX_GY = GX + GY
 
 
 epsilon = 1e-06
@@ -151,7 +153,6 @@
     live_mask = (jnp.arange(blocks, dtype=jnp.int32) < block_count[0]).astype(jnp.float32)[:, None]
 
     slot_index = grain_slots.reshape(1, blocks * GB)
-    slot_column = grain_slots.reshape(blocks * GB, 1)
 
     def to_tiles(grain_field):
         return jnp.transpose(grain_field.reshape(6, grains // 128, 128), (0, 2, 1))
@@ -172,7 +173,7 @@
             "bij,bi->bj", jacobian, impulse_field, preferred_element_type=jnp.float32
         )
         pushes = jnp.transpose(pushes.reshape(blocks, 6, GB), (1, 0, 2)).reshape(6, blocks * GB)
-        nearby = scatter_field(pushes, slot_index, slot_column, 9 * grains // 128)
+        nearby = scatter_field(pushes, slot_index, 9 * grains // 128)
         nearby = nearby.reshape(6 * 128, 3, 3, grains // 128)
         row_sums = nearby[:, :, 1]
         for step_y in (-1, 1):
@@ -204,7 +205,7 @@
 
 
 def solution(mesh):
-    finer = Mesh(mesh.devices.reshape(4, 4, 4, 2), ("gx_0", "gx_1", "gy_0", "gy_1"))
+    finer = Mesh(mesh.devices.reshape((2,) * len(GX_GY)), GX_GY)
     placed = (
         P(GX_GY, None, None),
         P(GX_GY, None),

time: 444 us -> 466 us (1.050)
  blocking collectives: 99.9 us -> 124 us
  local copies, waits for them, and re-layouts: 27.6 us -> 22 us
    psum x12 -> x21, blocking collectives: 99.9 us -> 124 us  [one_axis_at_a_time(): array = lax.psum(array, axis)]
    reshape x1 -> x0, local copies, waits for them, and re-layouts: 5.48 us -> none  [shards(): slot_column = grain_slots.reshape(blocks * GB, 1)]
  transfers between devices with their start and end apart: 32 -> 32, of which waited for: 18 -> 15; matrix products, arithmetic and copies ran while one was open for 5% -> 4% of each run, Pallas kernels for 4% -> 4%
where the time goes in v4:
time: 466 us; the launch traced here: 461 us
  blocking collectives  124 us (27%)
  other arithmetic  105 us (23%)
  starting transfers between devices  97.7 us (21%)
  Pallas kernels  65.7 us (14%)
  waiting for transfers between devices  40.9 us (9%)
  local copies, waits for them, and re-layouts  22 us (5%)
  between operations  6.36 us (1%)
    psum x21, blocking collectives, one_axis_at_a_time(): array = lax.psum(array, axis)  124 us
    unnamed x14, other arithmetic  97.8 us
    ppermute x16, starting transfers between devices, from_behind(): return lax.ppermute(block, axis, route)  50.2 us
    pallas_call x4, Pallas kernels, scatter_field(): pl.pallas_call(_scatter_kernel, grid=(slots // TILE,), in_specs=[pl.Block...  39.2 us
    ppermute x16, waiting for transfers between devices, from_behind(): return lax.ppermute(block, axis, route)  36.5 us
    ppermute x8, starting transfers between devices, with_halo(): after = lax.ppermute(leading, axis, down)  30.2 us
    pallas_call x4, Pallas kernels, gather_field(): pl.pallas_call(_gather_kernel, grid=(slots // TILE,), in_specs=[pl.BlockS...  26.5 us
    ppermute x8, starting transfers between devices, with_halo(): before = lax.ppermute(last, axis, up)  17.3 us
  transfers between devices with their start and end apart: 32, of which 15 were waited for; matrix products, arithmetic and copies ran while one was open for 4% of the time, Pallas kernels for 4%

profile of v4, /device:TPU:34, one launch (start us, length us, event | category | flops | bytes accessed | tf_op | source)
XLA Modules:
  0.0 461.5 jit_solution(765395019588504662)
XLA Ops:
  11.8 9.1 %fusion = f32[128,384]{1,0:T(8,128)S(1)} fusion(bf16[128,192,384]{2,1,0:T(8,128)(2,1)} %param.8, f32[128,192]{1,0:T(8,128)S(1)} %copy.125), kind=kLoop, calls=%fused_computation.8 | loop fusion | flops 28262400 | bytes 19169280
  22.2 9.8 %shard_map.95 = f32[768,144]{1,0:T(8,128)} custom-call(f32[6,8192]{1,0:T(8,128)} %reshape.133.push_ref, s32[1,8192]{1,0:T(1,128)} %reshape.134.idx_ref), custom_call_target="tpu_custom_call" | custom-call | tf_op jit(solution)/shard_map/pallas_call | solution.py:68
  59.6 6.6 %shard_map.97 = bf16[6,8192]{1,0:T(8,128)(2,1)} custom-call(bf16[768,144]{1,0:T(8,128)(2,1)} %copy.68.field_ref, s32[1,8192]{1,0:T(1,128)} %reshape.134.idx_ref), custom_call_target="tpu_custom_call" | custom-call | tf_op jit(solution)/shard_map/pallas_call | solution.py:31
  79.5 7.2 %all-reduce.20 = (f32[]{:T(128)}, f32[]{:T(128)}) all-reduce(f32[]{:T(128)} %get-tuple-element.85, f32[]{:T(128)} %get-tuple-element.83), channel_id=1, replica_groups=mesh['gx_0'=2,'gx_1'=2,'gx_2'=2,'gx_3'=2,'gy_0'=2,'gy_1'=2,'gy_2'=2] {'g..., use_global_device_ids=true, to_apply=%region_1.0 | all-reduce | flops 2 | bytes 16 | tf_op jit(solution)/shard_map/psum | solution.py:113
  92.3 7.1 %all-reduce.14 = (f32[]{:T(128)}, f32[]{:T(128)}) all-reduce(f32[]{:T(128)} %get-tuple-element.38, f32[]{:T(128)} %get-tuple-element.39), channel_id=1, replica_groups=mesh['gx_0'=2,'gx_1'=2,'gx_2'=2,'gx_3'=2,'gy_0'=2,'gy_1'=2,'gy_2'=2] {'g..., use_global_device_ids=true, to_apply=%region_3.0 | all-reduce | flops 2 | bytes 16 | tf_op jit(solution)/shard_map/psum | solution.py:113
  105.1 7.1 %all-reduce.8 = (f32[]{:T(128)}, f32[]{:T(128)}) all-reduce(f32[]{:T(128)} %get-tuple-element.26, f32[]{:T(128)} %get-tuple-element.27), channel_id=1, replica_groups=mesh['gx_0'=2,'gx_1'=2,'gx_2'=2,'gx_3'=2,'gy_0'=2,'gy_1'=2,'gy_2'=2] {'g..., use_global_device_ids=true, to_apply=%region_5.0 | all-reduce | flops 2 | bytes 16 | tf_op jit(solution)/shard_map/psum | solution.py:113
  123.4 6.6 %shard_map.96 = bf16[6,8192]{1,0:T(8,128)(2,1)} custom-call(bf16[768,144]{1,0:T(8,128)(2,1)} %copy.65.field_ref, s32[1,8192]{1,0:T(1,128)} %reshape.134.idx_ref), custom_call_target="tpu_custom_call" | custom-call | tf_op jit(solution)/shard_map/pallas_call | solution.py:31
  131.5 29.1 %fusion.5 = (f32[128,192]{1,0:T(8,128)S(1)}, f32[128,192]{1,0:T(8,128)S(1)}) fusion(f32[128,384]{1,0:T(8,128)S(1)} %copy.127, bf16[128,192,384]{2,1,0:T(8,128)(2,1)} %param.8, f32[128,384]{1,0:T(8,128)S(1)} %copy.126), kind=kLoop, calls=%fused_computation.13 | loop fusion | flops 47136768 | bytes 19464192
  161.7 9.1 %fusion.1 = f32[128,384]{1,0:T(8,128)S(1)} fusion(bf16[128,192,384]{2,1,0:T(8,128)(2,1)} %param.8, f32[128,192]{1,0:T(8,128)S(1)} %copy.128), kind=kLoop, calls=%fused_computation.9 | loop fusion | flops 28262400 | bytes 19169280
  172.0 9.8 %shard_map.98 = f32[768,144]{1,0:T(8,128)} custom-call(f32[6,8192]{1,0:T(8,128)} %reshape.149.push_ref, s32[1,8192]{1,0:T(1,128)} %reshape.134.idx_ref), custom_call_target="tpu_custom_call" | custom-call | tf_op jit(solution)/shard_map/pallas_call | solution.py:68
  220.7 7.2 %all-reduce.19 = (f32[]{:T(128)}, f32[]{:T(128)}) all-reduce(f32[]{:T(128)} %get-tuple-element.54, f32[]{:T(128)} %get-tuple-element.80), channel_id=1, replica_groups=mesh['gx_0'=2,'gx_1'=2,'gx_2'=2,'gx_3'=2,'gy_0'=2,'gy_1'=2,'gy_2'=2] {'g..., use_global_device_ids=true, to_apply=%region_17.18 | all-reduce | flops 2 | bytes 16 | tf_op jit(solution)/shard_map/psum | solution.py:113
  233.4 7.1 %all-reduce.13 = (f32[]{:T(128)}, f32[]{:T(128)}) all-reduce(f32[]{:T(128)} %get-tuple-element.36, f32[]{:T(128)} %get-tuple-element.37), channel_id=1, replica_groups=mesh['gx_0'=2,'gx_1'=2,'gx_2'=2,'gx_3'=2,'gy_0'=2,'gy_1'=2,'gy_2'=2] {'g..., use_global_device_ids=true, to_apply=%region_19.20 | all-reduce | flops 2 | bytes 16 | tf_op jit(solution)/shard_map/psum | solution.py:113
  246.1 7.1 %all-reduce.7 = (f32[]{:T(128)}, f32[]{:T(128)}) all-reduce(f32[]{:T(128)} %get-tuple-element.24, f32[]{:T(128)} %get-tuple-element.25), channel_id=1, replica_groups=mesh['gx_0'=2,'gx_1'=2,'gx_2'=2,'gx_3'=2,'gy_0'=2,'gy_1'=2,'gy_2'=2] {'g..., use_global_device_ids=true, to_apply=%region_21.22 | all-reduce | flops 2 | bytes 16 | tf_op jit(solution)/shard_map/psum | solution.py:113
  264.5 6.6 %shard_map.99 = bf16[6,8192]{1,0:T(8,128)(2,1)} custom-call(bf16[768,144]{1,0:T(8,128)(2,1)} %copy.74.field_ref, s32[1,8192]{1,0:T(1,128)} %reshape.134.idx_ref), custom_call_target="tpu_custom_call" | custom-call | tf_op jit(solution)/shard_map/pallas_call | solution.py:31
  272.6 15.7 %fusion.6 = f32[128,192]{1,0:T(8,128)S(1)} fusion(f32[128,384]{1,0:T(8,128)S(1)} %copy.129, bf16[128,192,384]{2,1,0:T(8,128)(2,1)} %param.8), kind=kLoop, calls=%fused_computation.14 | loop fusion | flops 28286976 | bytes 19169280
  289.2 9.1 %fusion.2 = f32[128,384]{1,0:T(8,128)S(1)} fusion(bf16[128,192,384]{2,1,0:T(8,128)(2,1)} %param.8, f32[128,192]{1,0:T(8,128)S(1)} %copy.130), kind=kLoop, calls=%fused_computation.10 | loop fusion | flops 28262400 | bytes 19169280
  299.5 9.8 %shard_map.100 = f32[768,144]{1,0:T(8,128)} custom-call(f32[6,8192]{1,0:T(8,128)} %reshape.159.push_ref, s32[1,8192]{1,0:T(1,128)} %reshape.134.idx_ref), custom_call_target="tpu_custom_call" | custom-call | tf_op jit(solution)/shard_map/pallas_call | solution.py:68
  348.1 7.2 %all-reduce.18 = (f32[]{:T(128)}, f32[]{:T(128)}) all-reduce(f32[]{:T(128)} %get-tuple-element.50, f32[]{:T(128)} %get-tuple-element.77), channel_id=1, replica_groups=mesh['gx_0'=2,'gx_1'=2,'gx_2'=2,'gx_3'=2,'gy_0'=2,'gy_1'=2,'gy_2'=2] {'g..., use_global_device_ids=true, to_apply=%region_33.34 | all-reduce | flops 2 | bytes 16 | tf_op jit(solution)/shard_map/psum | solution.py:113
  360.8 7.1 %all-reduce.12 = (f32[]{:T(128)}, f32[]{:T(128)}) all-reduce(f32[]{:T(128)} %get-tuple-element.34, f32[]{:T(128)} %get-tuple-element.35), channel_id=1, replica_groups=mesh['gx_0'=2,'gx_1'=2,'gx_2'=2,'gx_3'=2,'gy_0'=2,'gy_1'=2,'gy_2'=2] {'g..., use_global_device_ids=true, to_apply=%region_35.36 | all-reduce | flops 2 | bytes 16 | tf_op jit(solution)/shard_map/psum | solution.py:113
  373.5 7.1 %all-reduce.6 = (f32[]{:T(128)}, f32[]{:T(128)}) all-reduce(f32[]{:T(128)} %get-tuple-element.22, f32[]{:T(128)} %get-tuple-element.23), channel_id=1, replica_groups=mesh['gx_0'=2,'gx_1'=2,'gx_2'=2,'gx_3'=2,'gy_0'=2,'gy_1'=2,'gy_2'=2] {'g..., use_global_device_ids=true, to_apply=%region_37.38 | all-reduce | flops 2 | bytes 16 | tf_op jit(solution)/shard_map/psum | solution.py:113
  391.7 6.6 %shard_map.101 = bf16[6,8192]{1,0:T(8,128)(2,1)} custom-call(bf16[768,144]{1,0:T(8,128)(2,1)} %copy.80.field_ref, s32[1,8192]{1,0:T(1,128)} %reshape.134.idx_ref), custom_call_target="tpu_custom_call" | custom-call | tf_op jit(solution)/shard_map/pallas_call | solution.py:31
  399.7 15.7 %fusion.7 = f32[128,192]{1,0:T(8,128)S(1)} fusion(f32[128,384]{1,0:T(8,128)S(1)} %copy.131, bf16[128,192,384]{2,1,0:T(8,128)(2,1)} %param.8), kind=kLoop, calls=%fused_computation.15 | loop fusion | flops 28286976 | bytes 19169280
  416.4 9.1 %fusion.3 = f32[128,384]{1,0:T(8,128)S(1)} fusion(bf16[128,192,384]{2,1,0:T(8,128)(2,1)} %param.8, f32[128,192]{1,0:T(8,128)S(1)} %copy.132), kind=kLoop, calls=%fused_computation.11 | loop fusion | flops 28262400 | bytes 19169280
  426.7 9.8 %shard_map.102 = f32[768,144]{1,0:T(8,128)} custom-call(f32[6,8192]{1,0:T(8,128)} %reshape.169.push_ref, s32[1,8192]{1,0:T(1,128)} %reshape.134.idx_ref), custom_call_target="tpu_custom_call" | custom-call | tf_op jit(solution)/shard_map/pallas_call | solution.py:68
  (193 shorter events, 228.1 us)
Async XLA Ops:
  1.6 48.2 %collective-permute-start.9 = (bf16[768,1,1,16]{0,3,2,1:T(8,128)(2,1)S(1)}, bf16[768,1,1,16]{0,3,2,1:T(8,128)(2,1)S(1)}, u32[]{:S(2)}, u32[]{:S(2)}) collective-permute-start(bf16[768,1,1,16]{0,3,2,1:T(8,128)(2,1)S(1)} %reshape.144), channel_id=1, source_target_pairs={{8,0},{16,8},{24,16},{32,24},{40,32},{48,40},{56,48},{64,56},{72,6... | collective-permute-start | bytes 73736 | tf_op jit(solution)/shard_map/ppermute | solution.py:100
  6.0 31.7 %collective-permute-start.8 = (bf16[768,1,1,16]{0,3,2,1:T(8,128)(2,1)S(1)}, bf16[768,1,1,16]{0,3,2,1:T(8,128)(2,1)S(1)}, u32[]{:S(2)}, u32[]{:S(2)}) collective-permute-start(bf16[768,1,1,16]{0,3,2,1:T(8,128)(2,1)S(1)} %reshape.144), channel_id=1, source_target_pairs={{0,8},{8,16},{16,24},{24,32},{32,40},{40,48},{48,56},{56,64},{64,7... | collective-permute-start | bytes 73736 | tf_op jit(solution)/shard_map/ppermute | solution.py:99
  41.8 12.3 %collective-permute-start.2 = (f32[768,16]{0,1:T(8,128)S(1)}, f32[768,16]{0,1:T(8,128)S(1)}, u32[]{:S(2)}, u32[]{:S(2)}) collective-permute-start(f32[768,16]{0,1:T(8,128)S(1)} %get-tuple-element.74), channel_id=1, source_target_pairs={{8,0},{16,8},{24,16},{32,24},{40,32},{48,40},{56,48},{64,56},{72,6... | collective-permute-start | bytes 147464 | tf_op jit(solution)/shard_map/ppermute | solution.py:108
  47.8 8.1 %collective-permute-start.3 = (f32[768,16]{0,1:T(8,128)S(1)}, f32[768,16]{0,1:T(8,128)S(1)}, u32[]{:S(2)}, u32[]{:S(2)}) collective-permute-start(f32[768,16]{0,1:T(8,128)S(1)} %get-tuple-element.75), channel_id=1, source_target_pairs={{0,8},{8,16},{16,24},{24,32},{32,40},{40,48},{48,56},{56,64},{64,7... | collective-permute-start | bytes 147464 | tf_op jit(solution)/shard_map/ppermute | solution.py:108
  49.8 8.9 %collective-permute-start.11 = (bf16[768,3,1,16]{0,3,2,1:T(8,128)(2,1)S(1)}, bf16[768,3,1,16]{0,3,2,1:T(8,128)(2,1)S(1)}, u32[]{:S(2)}, u32[]{:S(2)}) collective-permute-start(bf16[768,3,1,16]{0,3,2,1:T(8,128)(2,1)S(1)} %constant_dynamic-update-slice_fusion.3), channel_id=1, source_target_pairs={{1,0},{2,1},{3,2},{4,3},{5,4},{6,5},{7,6},{9,8},{10,9},{11,10},{12... | collective-permute-start | bytes 221192 | tf_op jit(solution)/shard_map/ppermute | solution.py:100
  51.7 7.0 %collective-permute-start.10 = (bf16[768,3,1,16]{0,3,2,1:T(8,128)(2,1)S(1)}, bf16[768,3,1,16]{0,3,2,1:T(8,128)(2,1)S(1)}, u32[]{:S(2)}, u32[]{:S(2)}) collective-permute-start(bf16[768,3,1,16]{0,3,2,1:T(8,128)(2,1)S(1)} %constant_dynamic-update-slice_fusion.3), channel_id=1, source_target_pairs={{0,1},{1,2},{2,3},{3,4},{4,5},{5,6},{6,7},{8,9},{9,10},{10,11},{11... | collective-permute-start | bytes 221192 | tf_op jit(solution)/shard_map/ppermute | solution.py:99
  56.7 16.8 %collective-permute-start.4 = (bf16[768,1,1,16]{0,3,2,1:T(8,128)(2,1)S(1)}, bf16[768,1,1,16]{0,3,2,1:T(8,128)(2,1)S(1)}, u32[]{:S(2)}, u32[]{:S(2)}) collective-permute-start(bf16[768,1,1,16]{0,3,2,1:T(8,128)(2,1)S(1)} %reshape.139), channel_id=1, source_target_pairs={{0,8},{8,16},{16,24},{24,32},{32,40},{40,48},{48,56},{56,64},{64,7... | collective-permute-start | bytes 73736 | tf_op jit(solution)/shard_map/ppermute | solution.py:99
  67.5 7.5 %collective-permute-start.5 = (bf16[768,1,1,16]{0,3,2,1:T(8,128)(2,1)S(1)}, bf16[768,1,1,16]{0,3,2,1:T(8,128)(2,1)S(1)}, u32[]{:S(2)}, u32[]{:S(2)}) collective-permute-start(bf16[768,1,1,16]{0,3,2,1:T(8,128)(2,1)S(1)} %reshape.139), channel_id=1, source_target_pairs={{8,0},{16,8},{24,16},{32,24},{40,32},{48,40},{56,48},{64,56},{72,6... | collective-permute-start | bytes 73736 | tf_op jit(solution)/shard_map/ppermute | solution.py:100
  75.1 47.4 %collective-permute-start.7 = (bf16[768,3,1,16]{0,3,2,1:T(8,128)(2,1)S(1)}, bf16[768,3,1,16]{0,3,2,1:T(8,128)(2,1)S(1)}, u32[]{:S(2)}, u32[]{:S(2)}) collective-permute-start(bf16[768,3,1,16]{0,3,2,1:T(8,128)(2,1)S(1)} %constant_dynamic-update-slice_fusion), channel_id=1, source_target_pairs={{1,0},{2,1},{3,2},{4,3},{5,4},{6,5},{7,6},{9,8},{10,9},{11,10},{12... | collective-permute-start | bytes 221192 | tf_op jit(solution)/shard_map/ppermute | solution.py:100
  77.0 45.5 %collective-permute-start.6 = (bf16[768,3,1,16]{0,3,2,1:T(8,128)(2,1)S(1)}, bf16[768,3,1,16]{0,3,2,1:T(8,128)(2,1)S(1)}, u32[]{:S(2)}, u32[]{:S(2)}) collective-permute-start(bf16[768,3,1,16]{0,3,2,1:T(8,128)(2,1)S(1)} %constant_dynamic-update-slice_fusion), channel_id=1, source_target_pairs={{0,1},{1,2},{2,3},{3,4},{4,5},{5,6},{6,7},{8,9},{9,10},{10,11},{11... | collective-permute-start | bytes 221192 | tf_op jit(solution)/shard_map/ppermute | solution.py:99
  191.6 8.4 %collective-permute-start.14 = (f32[768,16]{0,1:T(8,128)S(1)}, f32[768,16]{0,1:T(8,128)S(1)}, u32[]{:S(2)}, u32[]{:S(2)}) collective-permute-start(f32[768,16]{0,1:T(8,128)S(1)} %get-tuple-element.72), channel_id=1, source_target_pairs={{8,0},{16,8},{24,16},{32,24},{40,32},{48,40},{56,48},{64,56},{72,6... | collective-permute-start | bytes 147464 | tf_op jit(solution)/shard_map/ppermute | solution.py:108
  198.1 8.1 %collective-permute-start.15 = (f32[768,16]{0,1:T(8,128)S(1)}, f32[768,16]{0,1:T(8,128)S(1)}, u32[]{:S(2)}, u32[]{:S(2)}) collective-permute-start(f32[768,16]{0,1:T(8,128)S(1)} %get-tuple-element.73), channel_id=1, source_target_pairs={{0,8},{8,16},{16,24},{24,32},{32,40},{40,48},{48,56},{56,64},{64,7... | collective-permute-start | bytes 147464 | tf_op jit(solution)/shard_map/ppermute | solution.py:108
  206.9 8.0 %collective-permute-start.16 = (bf16[768,1,1,16]{0,3,2,1:T(8,128)(2,1)S(1)}, bf16[768,1,1,16]{0,3,2,1:T(8,128)(2,1)S(1)}, u32[]{:S(2)}, u32[]{:S(2)}) collective-permute-start(bf16[768,1,1,16]{0,3,2,1:T(8,128)(2,1)S(1)} %reshape.154), channel_id=1, source_target_pairs={{0,8},{8,16},{16,24},{24,32},{32,40},{40,48},{48,56},{56,64},{64,7... | collective-permute-start | bytes 73736 | tf_op jit(solution)/shard_map/ppermute | solution.py:99
  208.9 7.5 %collective-permute-start.17 = (bf16[768,1,1,16]{0,3,2,1:T(8,128)(2,1)S(1)}, bf16[768,1,1,16]{0,3,2,1:T(8,128)(2,1)S(1)}, u32[]{:S(2)}, u32[]{:S(2)}) collective-permute-start(bf16[768,1,1,16]{0,3,2,1:T(8,128)(2,1)S(1)} %reshape.154), channel_id=1, source_target_pairs={{8,0},{16,8},{24,16},{32,24},{40,32},{48,40},{56,48},{64,56},{72,6... | collective-permute-start | bytes 73736 | tf_op jit(solution)/shard_map/ppermute | solution.py:100
  216.4 47.1 %collective-permute-start.19 = (bf16[768,3,1,16]{0,3,2,1:T(8,128)(2,1)S(1)}, bf16[768,3,1,16]{0,3,2,1:T(8,128)(2,1)S(1)}, u32[]{:S(2)}, u32[]{:S(2)}) collective-permute-start(bf16[768,3,1,16]{0,3,2,1:T(8,128)(2,1)S(1)} %constant_dynamic-update-slice_fusion.6), channel_id=1, source_target_pairs={{1,0},{2,1},{3,2},{4,3},{5,4},{6,5},{7,6},{9,8},{10,9},{11,10},{12... | collective-permute-start | bytes 221192 | tf_op jit(solution)/shard_map/ppermute | solution.py:100
  218.3 45.2 %collective-permute-start.18 = (bf16[768,3,1,16]{0,3,2,1:T(8,128)(2,1)S(1)}, bf16[768,3,1,16]{0,3,2,1:T(8,128)(2,1)S(1)}, u32[]{:S(2)}, u32[]{:S(2)}) collective-permute-start(bf16[768,3,1,16]{0,3,2,1:T(8,128)(2,1)S(1)} %constant_dynamic-update-slice_fusion.6), channel_id=1, source_target_pairs={{0,1},{1,2},{2,3},{3,4},{4,5},{5,6},{6,7},{8,9},{9,10},{10,11},{11... | collective-permute-start | bytes 221192 | tf_op jit(solution)/shard_map/ppermute | solution.py:99
  319.2 8.3 %collective-permute-start.22 = (f32[768,16]{0,1:T(8,128)S(1)}, f32[768,16]{0,1:T(8,128)S(1)}, u32[]{:S(2)}, u32[]{:S(2)}) collective-permute-start(f32[768,16]{0,1:T(8,128)S(1)} %get-tuple-element.70), channel_id=1, source_target_pairs={{8,0},{16,8},{24,16},{32,24},{40,32},{48,40},{56,48},{64,56},{72,6... | collective-permute-start | bytes 147464 | tf_op jit(solution)/shard_map/ppermute | solution.py:108
  325.5 8.1 %collective-permute-start.23 = (f32[768,16]{0,1:T(8,128)S(1)}, f32[768,16]{0,1:T(8,128)S(1)}, u32[]{:S(2)}, u32[]{:S(2)}) collective-permute-start(f32[768,16]{0,1:T(8,128)S(1)} %get-tuple-element.71), channel_id=1, source_target_pairs={{0,8},{8,16},{16,24},{24,32},{32,40},{40,48},{48,56},{56,64},{64,7... | collective-permute-start | bytes 147464 | tf_op jit(solution)/shard_map/ppermute | solution.py:108
  334.3 8.0 %collective-permute-start.24 = (bf16[768,1,1,16]{0,3,2,1:T(8,128)(2,1)S(1)}, bf16[768,1,1,16]{0,3,2,1:T(8,128)(2,1)S(1)}, u32[]{:S(2)}, u32[]{:S(2)}) collective-permute-start(bf16[768,1,1,16]{0,3,2,1:T(8,128)(2,1)S(1)} %reshape.164), channel_id=1, source_target_pairs={{0,8},{8,16},{16,24},{24,32},{32,40},{40,48},{48,56},{56,64},{64,7... | collective-permute-start | bytes 73736 | tf_op jit(solution)/shard_map/ppermute | solution.py:99
  336.3 7.5 %collective-permute-start.25 = (bf16[768,1,1,16]{0,3,2,1:T(8,128)(2,1)S(1)}, bf16[768,1,1,16]{0,3,2,1:T(8,128)(2,1)S(1)}, u32[]{:S(2)}, u32[]{:S(2)}) collective-permute-start(bf16[768,1,1,16]{0,3,2,1:T(8,128)(2,1)S(1)} %reshape.164), channel_id=1, source_target_pairs={{8,0},{16,8},{24,16},{32,24},{40,32},{48,40},{56,48},{64,56},{72,6... | collective-permute-start | bytes 73736 | tf_op jit(solution)/shard_map/ppermute | solution.py:100
  343.8 46.9 %collective-permute-start.27 = (bf16[768,3,1,16]{0,3,2,1:T(8,128)(2,1)S(1)}, bf16[768,3,1,16]{0,3,2,1:T(8,128)(2,1)S(1)}, u32[]{:S(2)}, u32[]{:S(2)}) collective-permute-start(bf16[768,3,1,16]{0,3,2,1:T(8,128)(2,1)S(1)} %constant_dynamic-update-slice_fusion.9), channel_id=1, source_target_pairs={{1,0},{2,1},{3,2},{4,3},{5,4},{6,5},{7,6},{9,8},{10,9},{11,10},{12... | collective-permute-start | bytes 221192 | tf_op jit(solution)/shard_map/ppermute | solution.py:100
  345.7 45.0 %collective-permute-start.26 = (bf16[768,3,1,16]{0,3,2,1:T(8,128)(2,1)S(1)}, bf16[768,3,1,16]{0,3,2,1:T(8,128)(2,1)S(1)}, u32[]{:S(2)}, u32[]{:S(2)}) collective-permute-start(bf16[768,3,1,16]{0,3,2,1:T(8,128)(2,1)S(1)} %constant_dynamic-update-slice_fusion.9), channel_id=1, source_target_pairs={{0,1},{1,2},{2,3},{3,4},{4,5},{5,6},{6,7},{8,9},{9,10},{10,11},{11... | collective-permute-start | bytes 221192 | tf_op jit(solution)/shard_map/ppermute | solution.py:99
  446.3 8.3 %collective-permute-start.30 = (f32[768,16]{0,1:T(8,128)S(1)}, f32[768,16]{0,1:T(8,128)S(1)}, u32[]{:S(2)}, u32[]{:S(2)}) collective-permute-start(f32[768,16]{0,1:T(8,128)S(1)} %get-tuple-element.68), channel_id=1, source_target_pairs={{8,0},{16,8},{24,16},{32,24},{40,32},{48,40},{56,48},{64,56},{72,6... | collective-permute-start | bytes 147464 | tf_op jit(solution)/shard_map/ppermute | solution.py:108
  452.7 8.1 %collective-permute-start.31 = (f32[768,16]{0,1:T(8,128)S(1)}, f32[768,16]{0,1:T(8,128)S(1)}, u32[]{:S(2)}, u32[]{:S(2)}) collective-permute-start(f32[768,16]{0,1:T(8,128)S(1)} %get-tuple-element.69), channel_id=1, source_target_pairs={{0,8},{8,16},{16,24},{24,32},{32,40},{40,48},{48,56},{56,64},{64,7... | collective-permute-start | bytes 147464 | tf_op jit(solution)/shard_map/ppermute | solution.py:108
  (13 other events, 580.4 us)

commit v5 on v4

--- a/solution.py
+++ b/solution.py
@@ -81,9 +81,9 @@
 CB = 64
 GB = 64
 ITERS = 3
-GX = ("gx_0", "gx_1", "gx_2", "gx_3")
-GY = ("gy_0", "gy_1", "gy_2")
-GX_GY = GX + GY
+GX_GY = ("gx_0", "gx_1", "gy_0", "gy_1")
+GX = ("gx_0", "gx_1")
+GY = ("gy_0", "gy_1")
 
 
 epsilon = 1e-06
@@ -205,7 +205,7 @@
 
 
 def solution(mesh):
-    finer = Mesh(mesh.devices.reshape((2,) * len(GX_GY)), GX_GY)
+    finer = Mesh(mesh.devices.reshape(4, 4, 4, 2), ("gx_0", "gx_1", "gy_0", "gy_1"))
     placed = (
         P(GX_GY, None, None),
         P(GX_GY, None),

time: 466 us -> 435 us (0.933)
  blocking collectives: 124 us -> 100 us
    psum x21 -> x12, blocking collectives: 124 us -> 100 us  [one_axis_at_a_time(): array = lax.psum(array, axis)]
  transfers between devices with their start and end apart: 32 -> 32, of which waited for: 15 -> 18; matrix products, arithmetic and copies ran while one was open for 4% -> 4% of each run, Pallas kernels for 4% -> 4%
where the time goes in v5:
time: 435 us; the launch traced here: 432 us
  other arithmetic  105 us (24%)
  blocking collectives  100 us (23%)
  starting transfers between devices  96.8 us (22%)
  Pallas kernels  65.7 us (15%)
  waiting for transfers between devices  36.7 us (8%)
  local copies, waits for them, and re-layouts  22 us (5%)
  between operations  5.94 us (1%)
    psum x12, blocking collectives, one_axis_at_a_time(): array = lax.psum(array, axis)  100 us
    unnamed x14, other arithmetic  97.8 us
    ppermute x16, starting transfers between devices, from_behind(): return lax.ppermute(block, axis, route)  49.3 us
    pallas_call x4, Pallas kernels, scatter_field(): pl.pallas_call(_scatter_kernel, grid=(slots // TILE,), in_specs=[pl.Block...  39.2 us
    ppermute x16, waiting for transfers between devices, from_behind(): return lax.ppermute(block, axis, route)  32.3 us
    ppermute x8, starting transfers between devices, with_halo(): after = lax.ppermute(leading, axis, down)  30.2 us
    pallas_call x4, Pallas kernels, gather_field(): pl.pallas_call(_gather_kernel, grid=(slots // TILE,), in_specs=[pl.BlockS...  26.5 us
    ppermute x8, starting transfers between devices, with_halo(): before = lax.ppermute(last, axis, up)  17.3 us
  transfers between devices with their start and end apart: 32, of which 18 were waited for; matrix products, arithmetic and copies ran while one was open for 4% of the time, Pallas kernels for 4%

profile of v5, /device:TPU:34, one launch (start us, length us, event | category | flops | bytes accessed | tf_op | source)
XLA Modules:
  0.0 431.7 jit_solution(16726738096472064666)
XLA Ops:
  11.8 9.1 %fusion = f32[128,384]{1,0:T(8,128)S(1)} fusion(bf16[128,192,384]{2,1,0:T(8,128)(2,1)} %param.8, f32[128,192]{1,0:T(8,128)S(1)} %copy.125), kind=kLoop, calls=%fused_computation.8 | loop fusion | flops 28262400 | bytes 19169280
  22.2 9.8 %shard_map.95 = f32[768,144]{1,0:T(8,128)} custom-call(f32[6,8192]{1,0:T(8,128)} %reshape.133.push_ref, s32[1,8192]{1,0:T(1,128)} %reshape.134.idx_ref), custom_call_target="tpu_custom_call" | custom-call | tf_op jit(solution)/shard_map/pallas_call | solution.py:68
  59.6 6.6 %shard_map.97 = bf16[6,8192]{1,0:T(8,128)(2,1)} custom-call(bf16[768,144]{1,0:T(8,128)(2,1)} %copy.68.field_ref, s32[1,8192]{1,0:T(1,128)} %reshape.134.idx_ref), custom_call_target="tpu_custom_call" | custom-call | tf_op jit(solution)/shard_map/pallas_call | solution.py:31
  79.5 9.8 %all-reduce.8 = (f32[]{:T(128)}, f32[]{:T(128)}) all-reduce(f32[]{:T(128)} %get-tuple-element.67, f32[]{:T(128)} %get-tuple-element.65), channel_id=1, replica_groups=mesh['gx_0'=4,'gx_1'=4,'gy_0'=4,'gy_1'=2] {'gx_0'}, use_global_device_ids=true, to_apply=%region_1.0 | all-reduce | flops 2 | bytes 16 | tf_op jit(solution)/shard_map/psum | solution.py:113
  89.3 13.2 %all-reduce.5 = (f32[]{:T(128)}, f32[]{:T(128)}) all-reduce(f32[]{:T(128)} %get-tuple-element.20, f32[]{:T(128)} %get-tuple-element.21), channel_id=1, replica_groups=mesh['gx_0'=4,'gx_1'=4,'gy_0'=4,'gy_1'=2] {'gx_1'}, use_global_device_ids=true, to_apply=%region_2.0 | all-reduce | flops 2 | bytes 16 | tf_op jit(solution)/shard_map/psum | solution.py:113
  102.5 9.3 %all-reduce.2 = (f32[]{:T(128)}, f32[]{:T(128)}) all-reduce(f32[]{:T(128)} %get-tuple-element.14, f32[]{:T(128)} %get-tuple-element.15), channel_id=1, replica_groups=mesh['gx_0'=4,'gx_1'=4,'gy_0'=4,'gy_1'=2] {'gy_0'}, use_global_device_ids=true, to_apply=%region_3.0 | all-reduce | flops 2 | bytes 16 | tf_op jit(solution)/shard_map/psum | solution.py:113
  117.3 6.6 %shard_map.96 = bf16[6,8192]{1,0:T(8,128)(2,1)} custom-call(bf16[768,144]{1,0:T(8,128)(2,1)} %copy.65.field_ref, s32[1,8192]{1,0:T(1,128)} %reshape.134.idx_ref), custom_call_target="tpu_custom_call" | custom-call | tf_op jit(solution)/shard_map/pallas_call | solution.py:31
  125.3 29.1 %fusion.5 = (f32[128,192]{1,0:T(8,128)S(1)}, f32[128,192]{1,0:T(8,128)S(1)}) fusion(f32[128,384]{1,0:T(8,128)S(1)} %copy.127, bf16[128,192,384]{2,1,0:T(8,128)(2,1)} %param.8, f32[128,384]{1,0:T(8,128)S(1)} %copy.126), kind=kLoop, calls=%fused_computation.13 | loop fusion | flops 47136768 | bytes 19464192
  155.5 9.1 %fusion.1 = f32[128,384]{1,0:T(8,128)S(1)} fusion(bf16[128,192,384]{2,1,0:T(8,128)(2,1)} %param.8, f32[128,192]{1,0:T(8,128)S(1)} %copy.128), kind=kLoop, calls=%fused_computation.9 | loop fusion | flops 28262400 | bytes 19169280
  165.8 9.8 %shard_map.98 = f32[768,144]{1,0:T(8,128)} custom-call(f32[6,8192]{1,0:T(8,128)} %reshape.149.push_ref, s32[1,8192]{1,0:T(1,128)} %reshape.134.idx_ref), custom_call_target="tpu_custom_call" | custom-call | tf_op jit(solution)/shard_map/pallas_call | solution.py:68
  212.2 9.1 %all-reduce.7 = (f32[]{:T(128)}, f32[]{:T(128)}) all-reduce(f32[]{:T(128)} %get-tuple-element.36, f32[]{:T(128)} %get-tuple-element.62), channel_id=1, replica_groups=mesh['gx_0'=4,'gx_1'=4,'gy_0'=4,'gy_1'=2] {'gx_0'}, use_global_device_ids=true, to_apply=%region_11.12 | all-reduce | flops 2 | bytes 16 | tf_op jit(solution)/shard_map/psum | solution.py:113
  221.2 12.7 %all-reduce.4 = (f32[]{:T(128)}, f32[]{:T(128)}) all-reduce(f32[]{:T(128)} %get-tuple-element.18, f32[]{:T(128)} %get-tuple-element.19), channel_id=1, replica_groups=mesh['gx_0'=4,'gx_1'=4,'gy_0'=4,'gy_1'=2] {'gx_1'}, use_global_device_ids=true, to_apply=%region_12.13 | all-reduce | flops 2 | bytes 16 | tf_op jit(solution)/shard_map/psum | solution.py:113
  233.9 7.4 %all-reduce.1 = (f32[]{:T(128)}, f32[]{:T(128)}) all-reduce(f32[]{:T(128)} %get-tuple-element.12, f32[]{:T(128)} %get-tuple-element.13), channel_id=1, replica_groups=mesh['gx_0'=4,'gx_1'=4,'gy_0'=4,'gy_1'=2] {'gy_0'}, use_global_device_ids=true, to_apply=%region_13.14 | all-reduce | flops 2 | bytes 16 | tf_op jit(solution)/shard_map/psum | solution.py:113
  246.8 6.6 %shard_map.99 = bf16[6,8192]{1,0:T(8,128)(2,1)} custom-call(bf16[768,144]{1,0:T(8,128)(2,1)} %copy.74.field_ref, s32[1,8192]{1,0:T(1,128)} %reshape.134.idx_ref), custom_call_target="tpu_custom_call" | custom-call | tf_op jit(solution)/shard_map/pallas_call | solution.py:31
  254.9 15.7 %fusion.6 = f32[128,192]{1,0:T(8,128)S(1)} fusion(f32[128,384]{1,0:T(8,128)S(1)} %copy.129, bf16[128,192,384]{2,1,0:T(8,128)(2,1)} %param.8), kind=kLoop, calls=%fused_computation.14 | loop fusion | flops 28286976 | bytes 19169280
  271.5 9.1 %fusion.2 = f32[128,384]{1,0:T(8,128)S(1)} fusion(bf16[128,192,384]{2,1,0:T(8,128)(2,1)} %param.8, f32[128,192]{1,0:T(8,128)S(1)} %copy.130), kind=kLoop, calls=%fused_computation.10 | loop fusion | flops 28262400 | bytes 19169280
  281.8 9.8 %shard_map.100 = f32[768,144]{1,0:T(8,128)} custom-call(f32[6,8192]{1,0:T(8,128)} %reshape.159.push_ref, s32[1,8192]{1,0:T(1,128)} %reshape.134.idx_ref), custom_call_target="tpu_custom_call" | custom-call | tf_op jit(solution)/shard_map/pallas_call | solution.py:68
  329.1 8.7 %all-reduce.6 = (f32[]{:T(128)}, f32[]{:T(128)}) all-reduce(f32[]{:T(128)} %get-tuple-element.32, f32[]{:T(128)} %get-tuple-element.59), channel_id=1, replica_groups=mesh['gx_0'=4,'gx_1'=4,'gy_0'=4,'gy_1'=2] {'gx_0'}, use_global_device_ids=true, to_apply=%region_21.22 | all-reduce | flops 2 | bytes 16 | tf_op jit(solution)/shard_map/psum | solution.py:113
  337.8 13.1 %all-reduce.3 = (f32[]{:T(128)}, f32[]{:T(128)}) all-reduce(f32[]{:T(128)} %get-tuple-element.16, f32[]{:T(128)} %get-tuple-element.17), channel_id=1, replica_groups=mesh['gx_0'=4,'gx_1'=4,'gy_0'=4,'gy_1'=2] {'gx_1'}, use_global_device_ids=true, to_apply=%region_22.23 | all-reduce | flops 2 | bytes 16 | tf_op jit(solution)/shard_map/psum | solution.py:113
  350.9 7.2 %all-reduce = (f32[]{:T(128)}, f32[]{:T(128)}) all-reduce(f32[]{:T(128)} %get-tuple-element.10, f32[]{:T(128)} %get-tuple-element.11), channel_id=1, replica_groups=mesh['gx_0'=4,'gx_1'=4,'gy_0'=4,'gy_1'=2] {'gy_0'}, use_global_device_ids=true, to_apply=%region_23.24 | all-reduce | flops 2 | bytes 16 | tf_op jit(solution)/shard_map/psum | solution.py:113
  363.4 6.6 %shard_map.101 = bf16[6,8192]{1,0:T(8,128)(2,1)} custom-call(bf16[768,144]{1,0:T(8,128)(2,1)} %copy.80.field_ref, s32[1,8192]{1,0:T(1,128)} %reshape.134.idx_ref), custom_call_target="tpu_custom_call" | custom-call | tf_op jit(solution)/shard_map/pallas_call | solution.py:31
  371.5 15.7 %fusion.7 = f32[128,192]{1,0:T(8,128)S(1)} fusion(f32[128,384]{1,0:T(8,128)S(1)} %copy.131, bf16[128,192,384]{2,1,0:T(8,128)(2,1)} %param.8), kind=kLoop, calls=%fused_computation.15 | loop fusion | flops 28286976 | bytes 19169280
  388.1 9.1 %fusion.3 = f32[128,384]{1,0:T(8,128)S(1)} fusion(bf16[128,192,384]{2,1,0:T(8,128)(2,1)} %param.8, f32[128,192]{1,0:T(8,128)S(1)} %copy.132), kind=kLoop, calls=%fused_computation.11 | loop fusion | flops 28262400 | bytes 19169280
  398.4 9.8 %shard_map.102 = f32[768,144]{1,0:T(8,128)} custom-call(f32[6,8192]{1,0:T(8,128)} %reshape.169.push_ref, s32[1,8192]{1,0:T(1,128)} %reshape.134.idx_ref), custom_call_target="tpu_custom_call" | custom-call | tf_op jit(solution)/shard_map/pallas_call | solution.py:68
  (184 shorter events, 172.6 us)
Async XLA Ops:
  1.6 48.2 %collective-permute-start.9 = (bf16[768,1,1,16]{0,3,2,1:T(8,128)(2,1)S(1)}, bf16[768,1,1,16]{0,3,2,1:T(8,128)(2,1)S(1)}, u32[]{:S(2)}, u32[]{:S(2)}) collective-permute-start(bf16[768,1,1,16]{0,3,2,1:T(8,128)(2,1)S(1)} %reshape.144), channel_id=1, source_target_pairs={{8,0},{16,8},{24,16},{32,24},{40,32},{48,40},{56,48},{64,56},{72,6... | collective-permute-start | bytes 73736 | tf_op jit(solution)/shard_map/ppermute | solution.py:100
  6.0 31.7 %collective-permute-start.8 = (bf16[768,1,1,16]{0,3,2,1:T(8,128)(2,1)S(1)}, bf16[768,1,1,16]{0,3,2,1:T(8,128)(2,1)S(1)}, u32[]{:S(2)}, u32[]{:S(2)}) collective-permute-start(bf16[768,1,1,16]{0,3,2,1:T(8,128)(2,1)S(1)} %reshape.144), channel_id=1, source_target_pairs={{0,8},{8,16},{16,24},{24,32},{32,40},{40,48},{48,56},{56,64},{64,7... | collective-permute-start | bytes 73736 | tf_op jit(solution)/shard_map/ppermute | solution.py:99
  41.8 12.3 %collective-permute-start.2 = (f32[768,16]{0,1:T(8,128)S(1)}, f32[768,16]{0,1:T(8,128)S(1)}, u32[]{:S(2)}, u32[]{:S(2)}) collective-permute-start(f32[768,16]{0,1:T(8,128)S(1)} %get-tuple-element.56), channel_id=1, source_target_pairs={{8,0},{16,8},{24,16},{32,24},{40,32},{48,40},{56,48},{64,56},{72,6... | collective-permute-start | bytes 147464 | tf_op jit(solution)/shard_map/ppermute | solution.py:108
  47.8 8.1 %collective-permute-start.3 = (f32[768,16]{0,1:T(8,128)S(1)}, f32[768,16]{0,1:T(8,128)S(1)}, u32[]{:S(2)}, u32[]{:S(2)}) collective-permute-start(f32[768,16]{0,1:T(8,128)S(1)} %get-tuple-element.57), channel_id=1, source_target_pairs={{0,8},{8,16},{16,24},{24,32},{32,40},{40,48},{48,56},{56,64},{64,7... | collective-permute-start | bytes 147464 | tf_op jit(solution)/shard_map/ppermute | solution.py:108
  49.8 8.9 %collective-permute-start.11 = (bf16[768,3,1,16]{0,3,2,1:T(8,128)(2,1)S(1)}, bf16[768,3,1,16]{0,3,2,1:T(8,128)(2,1)S(1)}, u32[]{:S(2)}, u32[]{:S(2)}) collective-permute-start(bf16[768,3,1,16]{0,3,2,1:T(8,128)(2,1)S(1)} %constant_dynamic-update-slice_fusion.3), channel_id=1, source_target_pairs={{1,0},{2,1},{3,2},{4,3},{5,4},{6,5},{7,6},{9,8},{10,9},{11,10},{12... | collective-permute-start | bytes 221192 | tf_op jit(solution)/shard_map/ppermute | solution.py:100
  51.7 7.0 %collective-permute-start.10 = (bf16[768,3,1,16]{0,3,2,1:T(8,128)(2,1)S(1)}, bf16[768,3,1,16]{0,3,2,1:T(8,128)(2,1)S(1)}, u32[]{:S(2)}, u32[]{:S(2)}) collective-permute-start(bf16[768,3,1,16]{0,3,2,1:T(8,128)(2,1)S(1)} %constant_dynamic-update-slice_fusion.3), channel_id=1, source_target_pairs={{0,1},{1,2},{2,3},{3,4},{4,5},{5,6},{6,7},{8,9},{9,10},{10,11},{11... | collective-permute-start | bytes 221192 | tf_op jit(solution)/shard_map/ppermute | solution.py:99
  56.7 16.8 %collective-permute-start.4 = (bf16[768,1,1,16]{0,3,2,1:T(8,128)(2,1)S(1)}, bf16[768,1,1,16]{0,3,2,1:T(8,128)(2,1)S(1)}, u32[]{:S(2)}, u32[]{:S(2)}) collective-permute-start(bf16[768,1,1,16]{0,3,2,1:T(8,128)(2,1)S(1)} %reshape.139), channel_id=1, source_target_pairs={{0,8},{8,16},{16,24},{24,32},{32,40},{40,48},{48,56},{56,64},{64,7... | collective-permute-start | bytes 73736 | tf_op jit(solution)/shard_map/ppermute | solution.py:99
  67.5 7.5 %collective-permute-start.5 = (bf16[768,1,1,16]{0,3,2,1:T(8,128)(2,1)S(1)}, bf16[768,1,1,16]{0,3,2,1:T(8,128)(2,1)S(1)}, u32[]{:S(2)}, u32[]{:S(2)}) collective-permute-start(bf16[768,1,1,16]{0,3,2,1:T(8,128)(2,1)S(1)} %reshape.139), channel_id=1, source_target_pairs={{8,0},{16,8},{24,16},{32,24},{40,32},{48,40},{56,48},{64,56},{72,6... | collective-permute-start | bytes 73736 | tf_op jit(solution)/shard_map/ppermute | solution.py:100
  75.1 41.2 %collective-permute-start.7 = (bf16[768,3,1,16]{0,3,2,1:T(8,128)(2,1)S(1)}, bf16[768,3,1,16]{0,3,2,1:T(8,128)(2,1)S(1)}, u32[]{:S(2)}, u32[]{:S(2)}) collective-permute-start(bf16[768,3,1,16]{0,3,2,1:T(8,128)(2,1)S(1)} %constant_dynamic-update-slice_fusion), channel_id=1, source_target_pairs={{1,0},{2,1},{3,2},{4,3},{5,4},{6,5},{7,6},{9,8},{10,9},{11,10},{12... | collective-permute-start | bytes 221192 | tf_op jit(solution)/shard_map/ppermute | solution.py:100
  77.0 39.3 %collective-permute-start.6 = (bf16[768,3,1,16]{0,3,2,1:T(8,128)(2,1)S(1)}, bf16[768,3,1,16]{0,3,2,1:T(8,128)(2,1)S(1)}, u32[]{:S(2)}, u32[]{:S(2)}) collective-permute-start(bf16[768,3,1,16]{0,3,2,1:T(8,128)(2,1)S(1)} %constant_dynamic-update-slice_fusion), channel_id=1, source_target_pairs={{0,1},{1,2},{2,3},{3,4},{4,5},{5,6},{6,7},{8,9},{9,10},{10,11},{11... | collective-permute-start | bytes 221192 | tf_op jit(solution)/shard_map/ppermute | solution.py:99
  177.0 6.7 %collective-permute-start.12 = (f32[768,3,16]{0,2,1:T(8,128)S(1)}, f32[768,3,16]{0,2,1:T(8,128)S(1)}, u32[]{:S(2)}, u32[]{:S(2)}) collective-permute-start(f32[768,3,16]{0,2,1:T(8,128)S(1)} %get-tuple-element.46), channel_id=1, source_target_pairs={{1,0},{2,1},{3,2},{4,3},{5,4},{6,5},{7,6},{9,8},{10,9},{11,10},{12... | collective-permute-start | bytes 442376 | tf_op jit(solution)/shard_map/ppermute | solution.py:108
  189.6 8.1 %collective-permute-start.15 = (f32[768,16]{0,1:T(8,128)S(1)}, f32[768,16]{0,1:T(8,128)S(1)}, u32[]{:S(2)}, u32[]{:S(2)}) collective-permute-start(f32[768,16]{0,1:T(8,128)S(1)} %get-tuple-element.55), channel_id=1, source_target_pairs={{0,8},{8,16},{16,24},{24,32},{32,40},{40,48},{48,56},{56,64},{64,7... | collective-permute-start | bytes 147464 | tf_op jit(solution)/shard_map/ppermute | solution.py:108
  198.4 8.0 %collective-permute-start.16 = (bf16[768,1,1,16]{0,3,2,1:T(8,128)(2,1)S(1)}, bf16[768,1,1,16]{0,3,2,1:T(8,128)(2,1)S(1)}, u32[]{:S(2)}, u32[]{:S(2)}) collective-permute-start(bf16[768,1,1,16]{0,3,2,1:T(8,128)(2,1)S(1)} %reshape.154), channel_id=1, source_target_pairs={{0,8},{8,16},{16,24},{24,32},{32,40},{40,48},{48,56},{56,64},{64,7... | collective-permute-start | bytes 73736 | tf_op jit(solution)/shard_map/ppermute | solution.py:99
  200.3 7.5 %collective-permute-start.17 = (bf16[768,1,1,16]{0,3,2,1:T(8,128)(2,1)S(1)}, bf16[768,1,1,16]{0,3,2,1:T(8,128)(2,1)S(1)}, u32[]{:S(2)}, u32[]{:S(2)}) collective-permute-start(bf16[768,1,1,16]{0,3,2,1:T(8,128)(2,1)S(1)} %reshape.154), channel_id=1, source_target_pairs={{8,0},{16,8},{24,16},{32,24},{40,32},{48,40},{56,48},{64,56},{72,6... | collective-permute-start | bytes 73736 | tf_op jit(solution)/shard_map/ppermute | solution.py:100
  207.8 38.0 %collective-permute-start.19 = (bf16[768,3,1,16]{0,3,2,1:T(8,128)(2,1)S(1)}, bf16[768,3,1,16]{0,3,2,1:T(8,128)(2,1)S(1)}, u32[]{:S(2)}, u32[]{:S(2)}) collective-permute-start(bf16[768,3,1,16]{0,3,2,1:T(8,128)(2,1)S(1)} %constant_dynamic-update-slice_fusion.6), channel_id=1, source_target_pairs={{1,0},{2,1},{3,2},{4,3},{5,4},{6,5},{7,6},{9,8},{10,9},{11,10},{12... | collective-permute-start | bytes 221192 | tf_op jit(solution)/shard_map/ppermute | solution.py:100
  209.7 36.1 %collective-permute-start.18 = (bf16[768,3,1,16]{0,3,2,1:T(8,128)(2,1)S(1)}, bf16[768,3,1,16]{0,3,2,1:T(8,128)(2,1)S(1)}, u32[]{:S(2)}, u32[]{:S(2)}) collective-permute-start(bf16[768,3,1,16]{0,3,2,1:T(8,128)(2,1)S(1)} %constant_dynamic-update-slice_fusion.6), channel_id=1, source_target_pairs={{0,1},{1,2},{2,3},{3,4},{4,5},{5,6},{6,7},{8,9},{9,10},{10,11},{11... | collective-permute-start | bytes 221192 | tf_op jit(solution)/shard_map/ppermute | solution.py:99
  293.0 7.4 %collective-permute-start.20 = (f32[768,3,16]{0,2,1:T(8,128)S(1)}, f32[768,3,16]{0,2,1:T(8,128)S(1)}, u32[]{:S(2)}, u32[]{:S(2)}) collective-permute-start(f32[768,3,16]{0,2,1:T(8,128)S(1)} %get-tuple-element.44), channel_id=1, source_target_pairs={{1,0},{2,1},{3,2},{4,3},{5,4},{6,5},{7,6},{9,8},{10,9},{11,10},{12... | collective-permute-start | bytes 442376 | tf_op jit(solution)/shard_map/ppermute | solution.py:108
  306.5 8.1 %collective-permute-start.23 = (f32[768,16]{0,1:T(8,128)S(1)}, f32[768,16]{0,1:T(8,128)S(1)}, u32[]{:S(2)}, u32[]{:S(2)}) collective-permute-start(f32[768,16]{0,1:T(8,128)S(1)} %get-tuple-element.53), channel_id=1, source_target_pairs={{0,8},{8,16},{16,24},{24,32},{32,40},{40,48},{48,56},{56,64},{64,7... | collective-permute-start | bytes 147464 | tf_op jit(solution)/shard_map/ppermute | solution.py:108
  315.3 8.0 %collective-permute-start.24 = (bf16[768,1,1,16]{0,3,2,1:T(8,128)(2,1)S(1)}, bf16[768,1,1,16]{0,3,2,1:T(8,128)(2,1)S(1)}, u32[]{:S(2)}, u32[]{:S(2)}) collective-permute-start(bf16[768,1,1,16]{0,3,2,1:T(8,128)(2,1)S(1)} %reshape.164), channel_id=1, source_target_pairs={{0,8},{8,16},{16,24},{24,32},{32,40},{40,48},{48,56},{56,64},{64,7... | collective-permute-start | bytes 73736 | tf_op jit(solution)/shard_map/ppermute | solution.py:99
  317.3 7.5 %collective-permute-start.25 = (bf16[768,1,1,16]{0,3,2,1:T(8,128)(2,1)S(1)}, bf16[768,1,1,16]{0,3,2,1:T(8,128)(2,1)S(1)}, u32[]{:S(2)}, u32[]{:S(2)}) collective-permute-start(bf16[768,1,1,16]{0,3,2,1:T(8,128)(2,1)S(1)} %reshape.164), channel_id=1, source_target_pairs={{8,0},{16,8},{24,16},{32,24},{40,32},{48,40},{56,48},{64,56},{72,6... | collective-permute-start | bytes 73736 | tf_op jit(solution)/shard_map/ppermute | solution.py:100
  324.8 37.6 %collective-permute-start.27 = (bf16[768,3,1,16]{0,3,2,1:T(8,128)(2,1)S(1)}, bf16[768,3,1,16]{0,3,2,1:T(8,128)(2,1)S(1)}, u32[]{:S(2)}, u32[]{:S(2)}) collective-permute-start(bf16[768,3,1,16]{0,3,2,1:T(8,128)(2,1)S(1)} %constant_dynamic-update-slice_fusion.9), channel_id=1, source_target_pairs={{1,0},{2,1},{3,2},{4,3},{5,4},{6,5},{7,6},{9,8},{10,9},{11,10},{12... | collective-permute-start | bytes 221192 | tf_op jit(solution)/shard_map/ppermute | solution.py:100
  326.7 35.7 %collective-permute-start.26 = (bf16[768,3,1,16]{0,3,2,1:T(8,128)(2,1)S(1)}, bf16[768,3,1,16]{0,3,2,1:T(8,128)(2,1)S(1)}, u32[]{:S(2)}, u32[]{:S(2)}) collective-permute-start(bf16[768,3,1,16]{0,3,2,1:T(8,128)(2,1)S(1)} %constant_dynamic-update-slice_fusion.9), channel_id=1, source_target_pairs={{0,1},{1,2},{2,3},{3,4},{4,5},{5,6},{6,7},{8,9},{9,10},{10,11},{11... | collective-permute-start | bytes 221192 | tf_op jit(solution)/shard_map/ppermute | solution.py:99
  409.6 7.6 %collective-permute-start.28 = (f32[768,3,16]{0,2,1:T(8,128)S(1)}, f32[768,3,16]{0,2,1:T(8,128)S(1)}, u32[]{:S(2)}, u32[]{:S(2)}) collective-permute-start(f32[768,3,16]{0,2,1:T(8,128)S(1)} %get-tuple-element.42), channel_id=1, source_target_pairs={{1,0},{2,1},{3,2},{4,3},{5,4},{6,5},{7,6},{9,8},{10,9},{11,10},{12... | collective-permute-start | bytes 442376 | tf_op jit(solution)/shard_map/ppermute | solution.py:108
  423.0 8.1 %collective-permute-start.31 = (f32[768,16]{0,1:T(8,128)S(1)}, f32[768,16]{0,1:T(8,128)S(1)}, u32[]{:S(2)}, u32[]{:S(2)}) collective-permute-start(f32[768,16]{0,1:T(8,128)S(1)} %get-tuple-element.51), channel_id=1, source_target_pairs={{0,8},{8,16},{16,24},{24,32},{32,40},{40,48},{48,56},{56,64},{64,7... | collective-permute-start | bytes 147464 | tf_op jit(solution)/shard_map/ppermute | solution.py:108
  (13 other events, 564.5 us)

commit v6 on v5

--- a/solution.py
+++ b/solution.py
@@ -108,9 +108,14 @@
     return lax.ppermute(block, axis, route)
 
 
-def one_axis_at_a_time(array, axes):
+def butterfly_sum(array, axes):
+    size = 1
     for axis in axes:
-        array = lax.psum(array, axis)
+        size *= lax.axis_size(axis)
+    step = 1
+    while step < size:
+        array = array + lax.ppermute(array, axes, [(i, i ^ step) for i in range(size)])
+        step *= 2
     return array
 
 
@@ -191,10 +196,10 @@
     for iteration in range(ITERS):
         pushed = backward(extrapolated.astype(jnp.bfloat16))
         moved = inverse_mass * pushed
-        size_total, energy_total = (
-            one_axis_at_a_time(jnp.sum(extrapolated * extrapolated), GX_GY),
-            one_axis_at_a_time(jnp.sum(pushed * moved), GX_GY),
+        totals = butterfly_sum(
+            jnp.stack([jnp.sum(extrapolated * extrapolated), jnp.sum(pushed * moved)]), GX_GY
         )
+        size_total, energy_total = totals[0], totals[1]
         gradient = (forward(moved.astype(jnp.bfloat16)) + constraint_bias) * live_mask
         step_size = size_total / (energy_total + epsilon)
         current = project_cone(extrapolated - step_size * gradient, friction) * live_mask

time: 435 us -> 423 us (0.972)
  blocking collectives: 100 us -> 0 us
  waiting for transfers between devices: 36.7 us -> 101 us
  other arithmetic: 105 us -> 117 us
  starting transfers between devices: 96.8 us -> 107 us
    psum x12 -> x0, blocking collectives: 100 us -> none  [one_axis_at_a_time(): array = lax.psum(array, axis)]
    ppermute x0 -> x21, waiting for transfers between devices: none -> 60.5 us  [butterfly_sum(): lax.ppermute(array, axes, [(i, i ^ step) for i in range(size)])]
    ppermute x0 -> x21, starting transfers between devices: none -> 20.9 us  [butterfly_sum(): lax.ppermute(array, axes, [(i, i ^ step) for i in range(size)])]
    ppermute x8, starting transfers between devices: 30.2 us -> 17.9 us  [with_halo(): after = lax.ppermute(leading, axis, down)]
    add x0 -> x21, other arithmetic: none -> 8.1 us  [butterfly_sum(): array + lax.ppermute(array, axes, [(i, i ^ step) for i in range(size)])]
    ppermute x8, starting transfers between devices: 17.3 us -> 24 us  [with_halo(): before = lax.ppermute(last, axis, up)]
    ppermute x16, starting transfers between devices: 49.3 us -> 44.2 us  [from_behind(): return lax.ppermute(block, axis, route)]
    ppermute x16, waiting for transfers between devices: 32.3 us -> 37.1 us  [from_behind(): return lax.ppermute(block, axis, route)]
  transfers between devices with their start and end apart: 32 -> 53, of which waited for: 18 -> 34; matrix products, arithmetic and copies ran while one was open for 4% -> 7% of each run, Pallas kernels for 4% -> 4%
where the time goes in v6:
time: 423 us; the launch traced here: 420 us
  other arithmetic  117 us (28%)
  starting transfers between devices  107 us (25%)
  waiting for transfers between devices  101 us (24%)
  Pallas kernels  65.7 us (16%)
  local copies, waits for them, and re-layouts  23 us (5%)
  between operations  6.19 us (1%)
    unnamed x14, other arithmetic  97.8 us
    ppermute x21, waiting for transfers between devices, butterfly_sum(): lax.ppermute(array, axes, [(i, i ^ step) for i in range(size)])  60.5 us
    ppermute x16, starting transfers between devices, from_behind(): return lax.ppermute(block, axis, route)  44.2 us
    pallas_call x4, Pallas kernels, scatter_field(): pl.pallas_call(_scatter_kernel, grid=(slots // TILE,), in_specs=[pl.Block...  39.2 us
    ppermute x16, waiting for transfers between devices, from_behind(): return lax.ppermute(block, axis, route)  37.1 us
    pallas_call x4, Pallas kernels, gather_field(): pl.pallas_call(_gather_kernel, grid=(slots // TILE,), in_specs=[pl.BlockS...  26.5 us
    ppermute x8, starting transfers between devices, with_halo(): before = lax.ppermute(last, axis, up)  24 us
    ppermute x21, starting transfers between devices, butterfly_sum(): lax.ppermute(array, axes, [(i, i ^ step) for i in range(size)])  20.9 us
  transfers between devices with their start and end apart: 53, of which 34 were waited for; matrix products, arithmetic and copies ran while one was open for 7% of the time, Pallas kernels for 4%

profile of v6, /device:TPU:34, one launch (start us, length us, event | category | flops | bytes accessed | tf_op | source)
XLA Modules:
  0.0 419.8 jit_solution(17932491344870685507)
XLA Ops:
  1.6 4.5 %collective-permute-start.16 = (bf16[768,1,1,16]{0,3,2,1:T(8,128)(2,1)S(1)}, bf16[768,1,1,16]{0,3,2,1:T(8,128)(2,1)S(1)}, u32[]{:S(2)}, u32[]{:S(2)}) collective-permute-start(bf16[768,1,1,16]{0,3,2,1:T(8,128)(2,1)S(1)} %reshape.153), channel_id=1, source_target_pairs={{8,0},{16,8},{24,16},{32,24},{40,32},{48,40},{56,48},{64,56},{72,6... | collective-permute-start | bytes 73736 | tf_op jit(solution)/shard_map/ppermute | solution.py:100
  10.3 9.1 %fusion = f32[128,384]{1,0:T(8,128)S(1)} fusion(bf16[128,192,384]{2,1,0:T(8,128)(2,1)} %param.8, f32[128,192]{1,0:T(8,128)S(1)} %copy.125), kind=kLoop, calls=%fused_computation.8 | loop fusion | flops 28262400 | bytes 19169280
  21.4 9.8 %shard_map.95 = f32[768,144]{1,0:T(8,128)} custom-call(f32[6,8192]{1,0:T(8,128)} %reshape.142.push_ref, s32[1,8192]{1,0:T(1,128)} %reshape.143.idx_ref), custom_call_target="tpu_custom_call" | custom-call | tf_op jit(solution)/shard_map/pallas_call | solution.py:68
  43.1 6.6 %shard_map.97 = bf16[6,8192]{1,0:T(8,128)(2,1)} custom-call(bf16[768,144]{1,0:T(8,128)(2,1)} %copy.68.field_ref, s32[1,8192]{1,0:T(1,128)} %reshape.143.idx_ref), custom_call_target="tpu_custom_call" | custom-call | tf_op jit(solution)/shard_map/pallas_call | solution.py:31
  51.1 6.0 %collective-permute-start.2 = (f32[768,16]{0,1:T(8,128)S(1)}, f32[768,16]{0,1:T(8,128)S(1)}, u32[]{:S(2)}, u32[]{:S(2)}) collective-permute-start(f32[768,16]{0,1:T(8,128)S(1)} %get-tuple-element.32), channel_id=1, source_target_pairs={{8,0},{16,8},{24,16},{32,24},{40,32},{48,40},{56,48},{64,56},{72,6... | collective-permute-start | bytes 147464 | tf_op jit(solution)/shard_map/ppermute | solution.py:108
  59.2 6.2 %collective-permute-done.3 = f32[768,16]{0,1:T(8,128)S(1)} collective-permute-done((f32[768,16]{0,1:T(8,128)S(1)}, f32[768,16]{0,1:T(8,128)S(1)}, u32[]{:S(2)}, u32[]{:S(2)}) %collective-permute-start.3) | collective-permute-done | bytes 49184 | tf_op jit(solution)/shard_map/ppermute | solution.py:108
  111.8 6.6 %shard_map.96 = bf16[6,8192]{1,0:T(8,128)(2,1)} custom-call(bf16[768,144]{1,0:T(8,128)(2,1)} %copy.65.field_ref, s32[1,8192]{1,0:T(1,128)} %reshape.143.idx_ref), custom_call_target="tpu_custom_call" | custom-call | tf_op jit(solution)/shard_map/pallas_call | solution.py:31
  119.8 29.1 %fusion.5 = (f32[128,192]{1,0:T(8,128)S(1)}, f32[128,192]{1,0:T(8,128)S(1)}) fusion(f32[128,384]{1,0:T(8,128)S(1)} %copy.127, bf16[128,192,384]{2,1,0:T(8,128)(2,1)} %param.8, f32[128,384]{1,0:T(8,128)S(1)} %copy.126), kind=kLoop, calls=%fused_computation.13 | loop fusion | flops 47136768 | bytes 19464192
  150.1 9.1 %fusion.1 = f32[128,384]{1,0:T(8,128)S(1)} fusion(bf16[128,192,384]{2,1,0:T(8,128)(2,1)} %param.8, f32[128,192]{1,0:T(8,128)S(1)} %copy.128), kind=kLoop, calls=%fused_computation.9 | loop fusion | flops 28262400 | bytes 19169280
  160.4 9.8 %shard_map.98 = f32[768,144]{1,0:T(8,128)} custom-call(f32[6,8192]{1,0:T(8,128)} %reshape.158.push_ref, s32[1,8192]{1,0:T(1,128)} %reshape.143.idx_ref), custom_call_target="tpu_custom_call" | custom-call | tf_op jit(solution)/shard_map/pallas_call | solution.py:68
  180.0 4.4 %collective-permute-start.21 = (f32[768,16]{0,1:T(8,128)S(1)}, f32[768,16]{0,1:T(8,128)S(1)}, u32[]{:S(2)}, u32[]{:S(2)}) collective-permute-start(f32[768,16]{0,1:T(8,128)S(1)} %get-tuple-element.30), channel_id=1, source_target_pairs={{8,0},{16,8},{24,16},{32,24},{40,32},{48,40},{56,48},{64,56},{72,6... | collective-permute-start | bytes 147464 | tf_op jit(solution)/shard_map/ppermute | solution.py:108
  186.4 6.2 %collective-permute-done.22 = f32[768,16]{0,1:T(8,128)S(1)} collective-permute-done((f32[768,16]{0,1:T(8,128)S(1)}, f32[768,16]{0,1:T(8,128)S(1)}, u32[]{:S(2)}, u32[]{:S(2)}) %collective-permute-start.22) | collective-permute-done | bytes 49184 | tf_op jit(solution)/shard_map/ppermute | solution.py:108
  238.9 6.6 %shard_map.99 = bf16[6,8192]{1,0:T(8,128)(2,1)} custom-call(bf16[768,144]{1,0:T(8,128)(2,1)} %copy.74.field_ref, s32[1,8192]{1,0:T(1,128)} %reshape.143.idx_ref), custom_call_target="tpu_custom_call" | custom-call | tf_op jit(solution)/shard_map/pallas_call | solution.py:31
  247.0 15.7 %fusion.6 = f32[128,192]{1,0:T(8,128)S(1)} fusion(f32[128,384]{1,0:T(8,128)S(1)} %copy.129, bf16[128,192,384]{2,1,0:T(8,128)(2,1)} %param.8), kind=kLoop, calls=%fused_computation.14 | loop fusion | flops 28286976 | bytes 19169280
  263.6 9.1 %fusion.2 = f32[128,384]{1,0:T(8,128)S(1)} fusion(bf16[128,192,384]{2,1,0:T(8,128)(2,1)} %param.8, f32[128,192]{1,0:T(8,128)S(1)} %copy.130), kind=kLoop, calls=%fused_computation.10 | loop fusion | flops 28262400 | bytes 19169280
  273.9 9.8 %shard_map.100 = f32[768,144]{1,0:T(8,128)} custom-call(f32[6,8192]{1,0:T(8,128)} %reshape.168.push_ref, s32[1,8192]{1,0:T(1,128)} %reshape.143.idx_ref), custom_call_target="tpu_custom_call" | custom-call | tf_op jit(solution)/shard_map/pallas_call | solution.py:68
  293.6 4.0 collective-permute-start.36
  299.6 6.1 %collective-permute-done.37 = f32[768,16]{0,1:T(8,128)S(1)} collective-permute-done((f32[768,16]{0,1:T(8,128)S(1)}, f32[768,16]{0,1:T(8,128)S(1)}, u32[]{:S(2)}, u32[]{:S(2)}) %collective-permute-start.37) | collective-permute-done | bytes 49184 | tf_op jit(solution)/shard_map/ppermute | solution.py:108
  352.2 6.6 %shard_map.101 = bf16[6,8192]{1,0:T(8,128)(2,1)} custom-call(bf16[768,144]{1,0:T(8,128)(2,1)} %copy.80.field_ref, s32[1,8192]{1,0:T(1,128)} %reshape.143.idx_ref), custom_call_target="tpu_custom_call" | custom-call | tf_op jit(solution)/shard_map/pallas_call | solution.py:31
  360.2 15.7 %fusion.7 = f32[128,192]{1,0:T(8,128)S(1)} fusion(f32[128,384]{1,0:T(8,128)S(1)} %copy.131, bf16[128,192,384]{2,1,0:T(8,128)(2,1)} %param.8), kind=kLoop, calls=%fused_computation.15 | loop fusion | flops 28286976 | bytes 19169280
  376.9 9.1 %fusion.3 = f32[128,384]{1,0:T(8,128)S(1)} fusion(bf16[128,192,384]{2,1,0:T(8,128)(2,1)} %param.8, f32[128,192]{1,0:T(8,128)S(1)} %copy.132), kind=kLoop, calls=%fused_computation.11 | loop fusion | flops 28262400 | bytes 19169280
  387.2 9.8 %shard_map.102 = f32[768,144]{1,0:T(8,128)} custom-call(f32[6,8192]{1,0:T(8,128)} %reshape.178.push_ref, s32[1,8192]{1,0:T(1,128)} %reshape.143.idx_ref), custom_call_target="tpu_custom_call" | custom-call | tf_op jit(solution)/shard_map/pallas_call | solution.py:68
  407.0 4.0 collective-permute-start.51
  412.9 6.2 %collective-permute-done.52 = f32[768,16]{0,1:T(8,128)S(1)} collective-permute-done((f32[768,16]{0,1:T(8,128)S(1)}, f32[768,16]{0,1:T(8,128)S(1)}, u32[]{:S(2)}, u32[]{:S(2)}) %collective-permute-start.52) | collective-permute-done | bytes 49184 | tf_op jit(solution)/shard_map/ppermute | solution.py:108
  (243 shorter events, 203.3 us)
Async XLA Ops:
  1.6 31.0 %collective-permute-start.16 = (bf16[768,1,1,16]{0,3,2,1:T(8,128)(2,1)S(1)}, bf16[768,1,1,16]{0,3,2,1:T(8,128)(2,1)S(1)}, u32[]{:S(2)}, u32[]{:S(2)}) collective-permute-start(bf16[768,1,1,16]{0,3,2,1:T(8,128)(2,1)S(1)} %reshape.153), channel_id=1, source_target_pairs={{8,0},{16,8},{24,16},{32,24},{40,32},{48,40},{56,48},{64,56},{72,6... | collective-permute-start | bytes 73736 | tf_op jit(solution)/shard_map/ppermute | solution.py:100
  6.1 26.5 %collective-permute-start.15 = (bf16[768,1,1,16]{0,3,2,1:T(8,128)(2,1)S(1)}, bf16[768,1,1,16]{0,3,2,1:T(8,128)(2,1)S(1)}, u32[]{:S(2)}, u32[]{:S(2)}) collective-permute-start(bf16[768,1,1,16]{0,3,2,1:T(8,128)(2,1)S(1)} %reshape.153), channel_id=1, source_target_pairs={{0,8},{8,16},{16,24},{24,32},{32,40},{40,48},{48,56},{56,64},{64,7... | collective-permute-start | bytes 73736 | tf_op jit(solution)/shard_map/ppermute | solution.py:99
  32.6 9.5 %collective-permute-start.18 = (bf16[768,3,1,16]{0,3,2,1:T(8,128)(2,1)S(1)}, bf16[768,3,1,16]{0,3,2,1:T(8,128)(2,1)S(1)}, u32[]{:S(2)}, u32[]{:S(2)}) collective-permute-start(bf16[768,3,1,16]{0,3,2,1:T(8,128)(2,1)S(1)} %constant_dynamic-update-slice_fusion.3), channel_id=1, source_target_pairs={{1,0},{2,1},{3,2},{4,3},{5,4},{6,5},{7,6},{9,8},{10,9},{11,10},{12... | collective-permute-start | bytes 221192 | tf_op jit(solution)/shard_map/ppermute | solution.py:100
  34.6 7.5 %collective-permute-start.17 = (bf16[768,3,1,16]{0,3,2,1:T(8,128)(2,1)S(1)}, bf16[768,3,1,16]{0,3,2,1:T(8,128)(2,1)S(1)}, u32[]{:S(2)}, u32[]{:S(2)}) collective-permute-start(bf16[768,3,1,16]{0,3,2,1:T(8,128)(2,1)S(1)} %constant_dynamic-update-slice_fusion.3), channel_id=1, source_target_pairs={{0,1},{1,2},{2,3},{3,4},{4,5},{5,6},{6,7},{8,9},{9,10},{10,11},{11... | collective-permute-start | bytes 221192 | tf_op jit(solution)/shard_map/ppermute | solution.py:99
  37.0 14.0 %collective-permute-start = (f32[768,3,16]{0,2,1:T(8,128)S(1)}, f32[768,3,16]{0,2,1:T(8,128)S(1)}, u32[]{:S(2)}, u32[]{:S(2)}) collective-permute-start(f32[768,3,16]{0,2,1:T(8,128)S(1)} %get-tuple-element.24), channel_id=1, source_target_pairs={{1,0},{2,1},{3,2},{4,3},{5,4},{6,5},{7,6},{9,8},{10,9},{11,10},{12... | collective-permute-start | bytes 442376 | tf_op jit(solution)/shard_map/ppermute | solution.py:108
  40.2 10.8 %collective-permute-start.1 = (f32[768,3,16]{0,2,1:T(8,128)S(1)}, f32[768,3,16]{0,2,1:T(8,128)S(1)}, u32[]{:S(2)}, u32[]{:S(2)}) collective-permute-start(f32[768,3,16]{0,2,1:T(8,128)S(1)} %get-tuple-element.25), channel_id=1, source_target_pairs={{0,1},{1,2},{2,3},{3,4},{4,5},{5,6},{6,7},{8,9},{9,10},{10,11},{11... | collective-permute-start | bytes 442376 | tf_op jit(solution)/shard_map/ppermute | solution.py:108
  51.1 8.1 %collective-permute-start.2 = (f32[768,16]{0,1:T(8,128)S(1)}, f32[768,16]{0,1:T(8,128)S(1)}, u32[]{:S(2)}, u32[]{:S(2)}) collective-permute-start(f32[768,16]{0,1:T(8,128)S(1)} %get-tuple-element.32), channel_id=1, source_target_pairs={{8,0},{16,8},{24,16},{32,24},{40,32},{48,40},{56,48},{64,56},{72,6... | collective-permute-start | bytes 147464 | tf_op jit(solution)/shard_map/ppermute | solution.py:108
  57.1 8.3 %collective-permute-start.3 = (f32[768,16]{0,1:T(8,128)S(1)}, f32[768,16]{0,1:T(8,128)S(1)}, u32[]{:S(2)}, u32[]{:S(2)}) collective-permute-start(f32[768,16]{0,1:T(8,128)S(1)} %get-tuple-element.33), channel_id=1, source_target_pairs={{0,8},{8,16},{16,24},{24,32},{32,40},{40,48},{48,56},{56,64},{64,7... | collective-permute-start | bytes 147464 | tf_op jit(solution)/shard_map/ppermute | solution.py:108
  66.1 37.1 %collective-permute-start.12 = (bf16[768,1,1,16]{0,3,2,1:T(8,128)(2,1)S(1)}, bf16[768,1,1,16]{0,3,2,1:T(8,128)(2,1)S(1)}, u32[]{:S(2)}, u32[]{:S(2)}) collective-permute-start(bf16[768,1,1,16]{0,3,2,1:T(8,128)(2,1)S(1)} %reshape.148), channel_id=1, source_target_pairs={{8,0},{16,8},{24,16},{32,24},{40,32},{48,40},{56,48},{64,56},{72,6... | collective-permute-start | bytes 73736 | tf_op jit(solution)/shard_map/ppermute | solution.py:100
  68.1 35.1 %collective-permute-start.11 = (bf16[768,1,1,16]{0,3,2,1:T(8,128)(2,1)S(1)}, bf16[768,1,1,16]{0,3,2,1:T(8,128)(2,1)S(1)}, u32[]{:S(2)}, u32[]{:S(2)}) collective-permute-start(bf16[768,1,1,16]{0,3,2,1:T(8,128)(2,1)S(1)} %reshape.148), channel_id=1, source_target_pairs={{0,8},{8,16},{16,24},{24,32},{32,40},{40,48},{48,56},{56,64},{64,7... | collective-permute-start | bytes 73736 | tf_op jit(solution)/shard_map/ppermute | solution.py:99
  103.2 6.4 %collective-permute-start.14 = (bf16[768,3,1,16]{0,3,2,1:T(8,128)(2,1)S(1)}, bf16[768,3,1,16]{0,3,2,1:T(8,128)(2,1)S(1)}, u32[]{:S(2)}, u32[]{:S(2)}) collective-permute-start(bf16[768,3,1,16]{0,3,2,1:T(8,128)(2,1)S(1)} %constant_dynamic-update-slice_fusion), channel_id=1, source_target_pairs={{1,0},{2,1},{3,2},{4,3},{5,4},{6,5},{7,6},{9,8},{10,9},{11,10},{12... | collective-permute-start | bytes 221192 | tf_op jit(solution)/shard_map/ppermute | solution.py:100
  173.5 6.5 %collective-permute-start.20 = (f32[768,3,16]{0,2,1:T(8,128)S(1)}, f32[768,3,16]{0,2,1:T(8,128)S(1)}, u32[]{:S(2)}, u32[]{:S(2)}) collective-permute-start(f32[768,3,16]{0,2,1:T(8,128)S(1)} %get-tuple-element.23), channel_id=1, source_target_pairs={{0,1},{1,2},{2,3},{3,4},{4,5},{5,6},{6,7},{8,9},{9,10},{10,11},{11... | collective-permute-start | bytes 442376 | tf_op jit(solution)/shard_map/ppermute | solution.py:108
  180.0 6.3 %collective-permute-start.21 = (f32[768,16]{0,1:T(8,128)S(1)}, f32[768,16]{0,1:T(8,128)S(1)}, u32[]{:S(2)}, u32[]{:S(2)}) collective-permute-start(f32[768,16]{0,1:T(8,128)S(1)} %get-tuple-element.30), channel_id=1, source_target_pairs={{8,0},{16,8},{24,16},{32,24},{40,32},{48,40},{56,48},{64,56},{72,6... | collective-permute-start | bytes 147464 | tf_op jit(solution)/shard_map/ppermute | solution.py:108
  184.4 8.1 %collective-permute-start.22 = (f32[768,16]{0,1:T(8,128)S(1)}, f32[768,16]{0,1:T(8,128)S(1)}, u32[]{:S(2)}, u32[]{:S(2)}) collective-permute-start(f32[768,16]{0,1:T(8,128)S(1)} %get-tuple-element.31), channel_id=1, source_target_pairs={{0,8},{8,16},{16,24},{24,32},{32,40},{40,48},{48,56},{56,64},{64,7... | collective-permute-start | bytes 147464 | tf_op jit(solution)/shard_map/ppermute | solution.py:108
  193.3 37.1 %collective-permute-start.31 = (bf16[768,1,1,16]{0,3,2,1:T(8,128)(2,1)S(1)}, bf16[768,1,1,16]{0,3,2,1:T(8,128)(2,1)S(1)}, u32[]{:S(2)}, u32[]{:S(2)}) collective-permute-start(bf16[768,1,1,16]{0,3,2,1:T(8,128)(2,1)S(1)} %reshape.163), channel_id=1, source_target_pairs={{8,0},{16,8},{24,16},{32,24},{40,32},{48,40},{56,48},{64,56},{72,6... | collective-permute-start | bytes 73736 | tf_op jit(solution)/shard_map/ppermute | solution.py:100
  195.2 35.1 %collective-permute-start.30 = (bf16[768,1,1,16]{0,3,2,1:T(8,128)(2,1)S(1)}, bf16[768,1,1,16]{0,3,2,1:T(8,128)(2,1)S(1)}, u32[]{:S(2)}, u32[]{:S(2)}) collective-permute-start(bf16[768,1,1,16]{0,3,2,1:T(8,128)(2,1)S(1)} %reshape.163), channel_id=1, source_target_pairs={{0,8},{8,16},{16,24},{24,32},{32,40},{40,48},{48,56},{56,64},{64,7... | collective-permute-start | bytes 73736 | tf_op jit(solution)/shard_map/ppermute | solution.py:99
  230.4 6.4 %collective-permute-start.33 = (bf16[768,3,1,16]{0,3,2,1:T(8,128)(2,1)S(1)}, bf16[768,3,1,16]{0,3,2,1:T(8,128)(2,1)S(1)}, u32[]{:S(2)}, u32[]{:S(2)}) collective-permute-start(bf16[768,3,1,16]{0,3,2,1:T(8,128)(2,1)S(1)} %constant_dynamic-update-slice_fusion.6), channel_id=1, source_target_pairs={{1,0},{2,1},{3,2},{4,3},{5,4},{6,5},{7,6},{9,8},{10,9},{11,10},{12... | collective-permute-start | bytes 221192 | tf_op jit(solution)/shard_map/ppermute | solution.py:100
  287.1 6.5 %collective-permute-start.35 = (f32[768,3,16]{0,2,1:T(8,128)S(1)}, f32[768,3,16]{0,2,1:T(8,128)S(1)}, u32[]{:S(2)}, u32[]{:S(2)}) collective-permute-start(f32[768,3,16]{0,2,1:T(8,128)S(1)} %get-tuple-element.21), channel_id=1, source_target_pairs={{0,1},{1,2},{2,3},{3,4},{4,5},{5,6},{6,7},{8,9},{9,10},{10,11},{11... | collective-permute-start | bytes 442376 | tf_op jit(solution)/shard_map/ppermute | solution.py:108
  297.7 8.1 %collective-permute-start.37 = (f32[768,16]{0,1:T(8,128)S(1)}, f32[768,16]{0,1:T(8,128)S(1)}, u32[]{:S(2)}, u32[]{:S(2)}) collective-permute-start(f32[768,16]{0,1:T(8,128)S(1)} %get-tuple-element.29), channel_id=1, source_target_pairs={{0,8},{8,16},{16,24},{24,32},{32,40},{40,48},{48,56},{56,64},{64,7... | collective-permute-start | bytes 147464 | tf_op jit(solution)/shard_map/ppermute | solution.py:108
  306.5 37.1 %collective-permute-start.46 = (bf16[768,1,1,16]{0,3,2,1:T(8,128)(2,1)S(1)}, bf16[768,1,1,16]{0,3,2,1:T(8,128)(2,1)S(1)}, u32[]{:S(2)}, u32[]{:S(2)}) collective-permute-start(bf16[768,1,1,16]{0,3,2,1:T(8,128)(2,1)S(1)} %reshape.173), channel_id=1, source_target_pairs={{8,0},{16,8},{24,16},{32,24},{40,32},{48,40},{56,48},{64,56},{72,6... | collective-permute-start | bytes 73736 | tf_op jit(solution)/shard_map/ppermute | solution.py:100
  308.4 35.1 %collective-permute-start.45 = (bf16[768,1,1,16]{0,3,2,1:T(8,128)(2,1)S(1)}, bf16[768,1,1,16]{0,3,2,1:T(8,128)(2,1)S(1)}, u32[]{:S(2)}, u32[]{:S(2)}) collective-permute-start(bf16[768,1,1,16]{0,3,2,1:T(8,128)(2,1)S(1)} %reshape.173), channel_id=1, source_target_pairs={{0,8},{8,16},{16,24},{24,32},{32,40},{40,48},{48,56},{56,64},{64,7... | collective-permute-start | bytes 73736 | tf_op jit(solution)/shard_map/ppermute | solution.py:99
  343.6 6.5 %collective-permute-start.48 = (bf16[768,3,1,16]{0,3,2,1:T(8,128)(2,1)S(1)}, bf16[768,3,1,16]{0,3,2,1:T(8,128)(2,1)S(1)}, u32[]{:S(2)}, u32[]{:S(2)}) collective-permute-start(bf16[768,3,1,16]{0,3,2,1:T(8,128)(2,1)S(1)} %constant_dynamic-update-slice_fusion.9), channel_id=1, source_target_pairs={{1,0},{2,1},{3,2},{4,3},{5,4},{6,5},{7,6},{9,8},{10,9},{11,10},{12... | collective-permute-start | bytes 221192 | tf_op jit(solution)/shard_map/ppermute | solution.py:100
  400.4 6.5 %collective-permute-start.50 = (f32[768,3,16]{0,2,1:T(8,128)S(1)}, f32[768,3,16]{0,2,1:T(8,128)S(1)}, u32[]{:S(2)}, u32[]{:S(2)}) collective-permute-start(f32[768,3,16]{0,2,1:T(8,128)S(1)} %get-tuple-element.19), channel_id=1, source_target_pairs={{0,1},{1,2},{2,3},{3,4},{4,5},{5,6},{6,7},{8,9},{9,10},{10,11},{11... | collective-permute-start | bytes 442376 | tf_op jit(solution)/shard_map/ppermute | solution.py:108
  411.0 8.1 %collective-permute-start.52 = (f32[768,16]{0,1:T(8,128)S(1)}, f32[768,16]{0,1:T(8,128)S(1)}, u32[]{:S(2)}, u32[]{:S(2)}) collective-permute-start(f32[768,16]{0,1:T(8,128)S(1)} %get-tuple-element.27), channel_id=1, source_target_pairs={{0,8},{8,16},{16,24},{24,32},{32,40},{40,48},{48,56},{56,64},{64,7... | collective-permute-start | bytes 147464 | tf_op jit(solution)/shard_map/ppermute | solution.py:108
  (35 other events, 656.2 us)

commit v7 on v6

--- a/solution.py
+++ b/solution.py
@@ -7,6 +7,7 @@
 from jax.experimental.pallas import tpu as pltpu
 from jax.sharding import Mesh
 from jax.sharding import PartitionSpec as P
+
 
 TILE = 1024
 
@@ -47,7 +48,7 @@
 
     rows, cols = out_ref.shape
     push = push_ref[...]
-    dofs, tile = push.shape
+    _, tile = push.shape
     idx = idx_ref[...]
     low = jnp.bitwise_and(idx, 127)
     high = lax.shift_right_logical(idx, 7)
@@ -115,14 +116,14 @@
     step = 1
     while step < size:
         array = array + lax.ppermute(array, axes, [(i, i ^ step) for i in range(size)])
-        step *= 2
+        step = step * 2
     return array
 
 
 def momentum_weights(iterations):
     momentum = 1.0
     weights = []
-    for iteration in range(iterations):
+    for _ in range(iterations):
         upcoming = (-momentum * momentum + momentum * math.sqrt(momentum * momentum + 4.0)) / 2.0
         weights.append(momentum * (1.0 - momentum) / (momentum * momentum + upcoming))
         momentum = upcoming
@@ -197,7 +198,8 @@
         pushed = backward(extrapolated.astype(jnp.bfloat16))
         moved = inverse_mass * pushed
         totals = butterfly_sum(
-            jnp.stack([jnp.sum(extrapolated * extrapolated), jnp.sum(pushed * moved)]), GX_GY
+            jnp.stack([jnp.sum(extrapolated * extrapolated), jnp.sum(pushed * moved)]),
+            GX_GY,
         )
         size_total, energy_total = totals[0], totals[1]
         gradient = (forward(moved.astype(jnp.bfloat16)) + constraint_bias) * live_mask

time: 423 us -> 423 us (level)
  no operation moved by 1% of the time
where the time goes in v7:
time: 423 us; the launch traced here: 420 us
  other arithmetic  117 us (28%)
  starting transfers between devices  107 us (25%)
  waiting for transfers between devices  101 us (24%)
  Pallas kernels  65.7 us (16%)
  local copies, waits for them, and re-layouts  23 us (5%)
  between operations  6.19 us (1%)
    unnamed x14, other arithmetic  97.8 us
    ppermute x21, waiting for transfers between devices, butterfly_sum(): lax.ppermute(array, axes, [(i, i ^ step) for i in range(size)])  60.5 us
    ppermute x16, starting transfers between devices, from_behind(): return lax.ppermute(block, axis, route)  44.2 us
    pallas_call x4, Pallas kernels, scatter_field(): pl.pallas_call(_scatter_kernel, grid=(slots // TILE,), in_specs=[pl.Block...  39.2 us
    ppermute x16, waiting for transfers between devices, from_behind(): return lax.ppermute(block, axis, route)  37.1 us
    pallas_call x4, Pallas kernels, gather_field(): pl.pallas_call(_gather_kernel, grid=(slots // TILE,), in_specs=[pl.BlockS...  26.5 us
    ppermute x8, starting transfers between devices, with_halo(): before = lax.ppermute(last, axis, up)  24 us
    ppermute x21, starting transfers between devices, butterfly_sum(): lax.ppermute(array, axes, [(i, i ^ step) for i in range(size)])  20.9 us
  transfers between devices with their start and end apart: 53, of which 34 were waited for; matrix products, arithmetic and copies ran while one was open for 7% of the time, Pallas kernels for 4%

profile of v7, /device:TPU:34, one launch (start us, length us, event | category | flops | bytes accessed | tf_op | source)
XLA Modules:
  0.0 419.8 jit_solution(17932491344870685507)
XLA Ops:
  1.6 4.5 %collective-permute-start.16 = (bf16[768,1,1,16]{0,3,2,1:T(8,128)(2,1)S(1)}, bf16[768,1,1,16]{0,3,2,1:T(8,128)(2,1)S(1)}, u32[]{:S(2)}, u32[]{:S(2)}) collective-permute-start(bf16[768,1,1,16]{0,3,2,1:T(8,128)(2,1)S(1)} %reshape.153), channel_id=1, source_target_pairs={{8,0},{16,8},{24,16},{32,24},{40,32},{48,40},{56,48},{64,56},{72,6... | collective-permute-start | bytes 73736 | tf_op jit(solution)/shard_map/ppermute | solution.py:101
  10.3 9.1 %fusion = f32[128,384]{1,0:T(8,128)S(1)} fusion(bf16[128,192,384]{2,1,0:T(8,128)(2,1)} %param.8, f32[128,192]{1,0:T(8,128)S(1)} %copy.125), kind=kLoop, calls=%fused_computation.8 | loop fusion | flops 28262400 | bytes 19169280
  21.4 9.8 %shard_map.95 = f32[768,144]{1,0:T(8,128)} custom-call(f32[6,8192]{1,0:T(8,128)} %reshape.142.push_ref, s32[1,8192]{1,0:T(1,128)} %reshape.143.idx_ref), custom_call_target="tpu_custom_call" | custom-call | tf_op jit(solution)/shard_map/pallas_call | solution.py:69
  43.1 6.6 %shard_map.97 = bf16[6,8192]{1,0:T(8,128)(2,1)} custom-call(bf16[768,144]{1,0:T(8,128)(2,1)} %copy.68.field_ref, s32[1,8192]{1,0:T(1,128)} %reshape.143.idx_ref), custom_call_target="tpu_custom_call" | custom-call | tf_op jit(solution)/shard_map/pallas_call | solution.py:32
  51.1 6.0 %collective-permute-start.2 = (f32[768,16]{0,1:T(8,128)S(1)}, f32[768,16]{0,1:T(8,128)S(1)}, u32[]{:S(2)}, u32[]{:S(2)}) collective-permute-start(f32[768,16]{0,1:T(8,128)S(1)} %get-tuple-element.32), channel_id=1, source_target_pairs={{8,0},{16,8},{24,16},{32,24},{40,32},{48,40},{56,48},{64,56},{72,6... | collective-permute-start | bytes 147464 | tf_op jit(solution)/shard_map/ppermute | solution.py:109
  59.2 6.2 %collective-permute-done.3 = f32[768,16]{0,1:T(8,128)S(1)} collective-permute-done((f32[768,16]{0,1:T(8,128)S(1)}, f32[768,16]{0,1:T(8,128)S(1)}, u32[]{:S(2)}, u32[]{:S(2)}) %collective-permute-start.3) | collective-permute-done | bytes 49184 | tf_op jit(solution)/shard_map/ppermute | solution.py:109
  111.8 6.6 %shard_map.96 = bf16[6,8192]{1,0:T(8,128)(2,1)} custom-call(bf16[768,144]{1,0:T(8,128)(2,1)} %copy.65.field_ref, s32[1,8192]{1,0:T(1,128)} %reshape.143.idx_ref), custom_call_target="tpu_custom_call" | custom-call | tf_op jit(solution)/shard_map/pallas_call | solution.py:32
  119.8 29.1 %fusion.5 = (f32[128,192]{1,0:T(8,128)S(1)}, f32[128,192]{1,0:T(8,128)S(1)}) fusion(f32[128,384]{1,0:T(8,128)S(1)} %copy.127, bf16[128,192,384]{2,1,0:T(8,128)(2,1)} %param.8, f32[128,384]{1,0:T(8,128)S(1)} %copy.126), kind=kLoop, calls=%fused_computation.13 | loop fusion | flops 47136768 | bytes 19464192
  150.1 9.1 %fusion.1 = f32[128,384]{1,0:T(8,128)S(1)} fusion(bf16[128,192,384]{2,1,0:T(8,128)(2,1)} %param.8, f32[128,192]{1,0:T(8,128)S(1)} %copy.128), kind=kLoop, calls=%fused_computation.9 | loop fusion | flops 28262400 | bytes 19169280
  160.4 9.8 %shard_map.98 = f32[768,144]{1,0:T(8,128)} custom-call(f32[6,8192]{1,0:T(8,128)} %reshape.158.push_ref, s32[1,8192]{1,0:T(1,128)} %reshape.143.idx_ref), custom_call_target="tpu_custom_call" | custom-call | tf_op jit(solution)/shard_map/pallas_call | solution.py:69
  180.0 4.4 %collective-permute-start.21 = (f32[768,16]{0,1:T(8,128)S(1)}, f32[768,16]{0,1:T(8,128)S(1)}, u32[]{:S(2)}, u32[]{:S(2)}) collective-permute-start(f32[768,16]{0,1:T(8,128)S(1)} %get-tuple-element.30), channel_id=1, source_target_pairs={{8,0},{16,8},{24,16},{32,24},{40,32},{48,40},{56,48},{64,56},{72,6... | collective-permute-start | bytes 147464 | tf_op jit(solution)/shard_map/ppermute | solution.py:109
  186.4 6.2 %collective-permute-done.22 = f32[768,16]{0,1:T(8,128)S(1)} collective-permute-done((f32[768,16]{0,1:T(8,128)S(1)}, f32[768,16]{0,1:T(8,128)S(1)}, u32[]{:S(2)}, u32[]{:S(2)}) %collective-permute-start.22) | collective-permute-done | bytes 49184 | tf_op jit(solution)/shard_map/ppermute | solution.py:109
  238.9 6.6 %shard_map.99 = bf16[6,8192]{1,0:T(8,128)(2,1)} custom-call(bf16[768,144]{1,0:T(8,128)(2,1)} %copy.74.field_ref, s32[1,8192]{1,0:T(1,128)} %reshape.143.idx_ref), custom_call_target="tpu_custom_call" | custom-call | tf_op jit(solution)/shard_map/pallas_call | solution.py:32
  247.0 15.7 %fusion.6 = f32[128,192]{1,0:T(8,128)S(1)} fusion(f32[128,384]{1,0:T(8,128)S(1)} %copy.129, bf16[128,192,384]{2,1,0:T(8,128)(2,1)} %param.8), kind=kLoop, calls=%fused_computation.14 | loop fusion | flops 28286976 | bytes 19169280
  263.6 9.1 %fusion.2 = f32[128,384]{1,0:T(8,128)S(1)} fusion(bf16[128,192,384]{2,1,0:T(8,128)(2,1)} %param.8, f32[128,192]{1,0:T(8,128)S(1)} %copy.130), kind=kLoop, calls=%fused_computation.10 | loop fusion | flops 28262400 | bytes 19169280
  273.9 9.8 %shard_map.100 = f32[768,144]{1,0:T(8,128)} custom-call(f32[6,8192]{1,0:T(8,128)} %reshape.168.push_ref, s32[1,8192]{1,0:T(1,128)} %reshape.143.idx_ref), custom_call_target="tpu_custom_call" | custom-call | tf_op jit(solution)/shard_map/pallas_call | solution.py:69
  293.6 4.0 collective-permute-start.36
  299.6 6.1 %collective-permute-done.37 = f32[768,16]{0,1:T(8,128)S(1)} collective-permute-done((f32[768,16]{0,1:T(8,128)S(1)}, f32[768,16]{0,1:T(8,128)S(1)}, u32[]{:S(2)}, u32[]{:S(2)}) %collective-permute-start.37) | collective-permute-done | bytes 49184 | tf_op jit(solution)/shard_map/ppermute | solution.py:109
  352.2 6.6 %shard_map.101 = bf16[6,8192]{1,0:T(8,128)(2,1)} custom-call(bf16[768,144]{1,0:T(8,128)(2,1)} %copy.80.field_ref, s32[1,8192]{1,0:T(1,128)} %reshape.143.idx_ref), custom_call_target="tpu_custom_call" | custom-call | tf_op jit(solution)/shard_map/pallas_call | solution.py:32
  360.2 15.7 %fusion.7 = f32[128,192]{1,0:T(8,128)S(1)} fusion(f32[128,384]{1,0:T(8,128)S(1)} %copy.131, bf16[128,192,384]{2,1,0:T(8,128)(2,1)} %param.8), kind=kLoop, calls=%fused_computation.15 | loop fusion | flops 28286976 | bytes 19169280
  376.9 9.1 %fusion.3 = f32[128,384]{1,0:T(8,128)S(1)} fusion(bf16[128,192,384]{2,1,0:T(8,128)(2,1)} %param.8, f32[128,192]{1,0:T(8,128)S(1)} %copy.132), kind=kLoop, calls=%fused_computation.11 | loop fusion | flops 28262400 | bytes 19169280
  387.2 9.8 %shard_map.102 = f32[768,144]{1,0:T(8,128)} custom-call(f32[6,8192]{1,0:T(8,128)} %reshape.178.push_ref, s32[1,8192]{1,0:T(1,128)} %reshape.143.idx_ref), custom_call_target="tpu_custom_call" | custom-call | tf_op jit(solution)/shard_map/pallas_call | solution.py:69
  407.0 4.0 collective-permute-start.51
  412.9 6.2 %collective-permute-done.52 = f32[768,16]{0,1:T(8,128)S(1)} collective-permute-done((f32[768,16]{0,1:T(8,128)S(1)}, f32[768,16]{0,1:T(8,128)S(1)}, u32[]{:S(2)}, u32[]{:S(2)}) %collective-permute-start.52) | collective-permute-done | bytes 49184 | tf_op jit(solution)/shard_map/ppermute | solution.py:109
  (243 shorter events, 203.3 us)
Async XLA Ops:
  1.6 31.0 %collective-permute-start.16 = (bf16[768,1,1,16]{0,3,2,1:T(8,128)(2,1)S(1)}, bf16[768,1,1,16]{0,3,2,1:T(8,128)(2,1)S(1)}, u32[]{:S(2)}, u32[]{:S(2)}) collective-permute-start(bf16[768,1,1,16]{0,3,2,1:T(8,128)(2,1)S(1)} %reshape.153), channel_id=1, source_target_pairs={{8,0},{16,8},{24,16},{32,24},{40,32},{48,40},{56,48},{64,56},{72,6... | collective-permute-start | bytes 73736 | tf_op jit(solution)/shard_map/ppermute | solution.py:101
  6.1 26.5 %collective-permute-start.15 = (bf16[768,1,1,16]{0,3,2,1:T(8,128)(2,1)S(1)}, bf16[768,1,1,16]{0,3,2,1:T(8,128)(2,1)S(1)}, u32[]{:S(2)}, u32[]{:S(2)}) collective-permute-start(bf16[768,1,1,16]{0,3,2,1:T(8,128)(2,1)S(1)} %reshape.153), channel_id=1, source_target_pairs={{0,8},{8,16},{16,24},{24,32},{32,40},{40,48},{48,56},{56,64},{64,7... | collective-permute-start | bytes 73736 | tf_op jit(solution)/shard_map/ppermute | solution.py:100
  32.6 9.5 %collective-permute-start.18 = (bf16[768,3,1,16]{0,3,2,1:T(8,128)(2,1)S(1)}, bf16[768,3,1,16]{0,3,2,1:T(8,128)(2,1)S(1)}, u32[]{:S(2)}, u32[]{:S(2)}) collective-permute-start(bf16[768,3,1,16]{0,3,2,1:T(8,128)(2,1)S(1)} %constant_dynamic-update-slice_fusion.3), channel_id=1, source_target_pairs={{1,0},{2,1},{3,2},{4,3},{5,4},{6,5},{7,6},{9,8},{10,9},{11,10},{12... | collective-permute-start | bytes 221192 | tf_op jit(solution)/shard_map/ppermute | solution.py:101
  34.6 7.5 %collective-permute-start.17 = (bf16[768,3,1,16]{0,3,2,1:T(8,128)(2,1)S(1)}, bf16[768,3,1,16]{0,3,2,1:T(8,128)(2,1)S(1)}, u32[]{:S(2)}, u32[]{:S(2)}) collective-permute-start(bf16[768,3,1,16]{0,3,2,1:T(8,128)(2,1)S(1)} %constant_dynamic-update-slice_fusion.3), channel_id=1, source_target_pairs={{0,1},{1,2},{2,3},{3,4},{4,5},{5,6},{6,7},{8,9},{9,10},{10,11},{11... | collective-permute-start | bytes 221192 | tf_op jit(solution)/shard_map/ppermute | solution.py:100
  37.0 14.0 %collective-permute-start = (f32[768,3,16]{0,2,1:T(8,128)S(1)}, f32[768,3,16]{0,2,1:T(8,128)S(1)}, u32[]{:S(2)}, u32[]{:S(2)}) collective-permute-start(f32[768,3,16]{0,2,1:T(8,128)S(1)} %get-tuple-element.24), channel_id=1, source_target_pairs={{1,0},{2,1},{3,2},{4,3},{5,4},{6,5},{7,6},{9,8},{10,9},{11,10},{12... | collective-permute-start | bytes 442376 | tf_op jit(solution)/shard_map/ppermute | solution.py:109
  40.2 10.8 %collective-permute-start.1 = (f32[768,3,16]{0,2,1:T(8,128)S(1)}, f32[768,3,16]{0,2,1:T(8,128)S(1)}, u32[]{:S(2)}, u32[]{:S(2)}) collective-permute-start(f32[768,3,16]{0,2,1:T(8,128)S(1)} %get-tuple-element.25), channel_id=1, source_target_pairs={{0,1},{1,2},{2,3},{3,4},{4,5},{5,6},{6,7},{8,9},{9,10},{10,11},{11... | collective-permute-start | bytes 442376 | tf_op jit(solution)/shard_map/ppermute | solution.py:109
  51.1 8.1 %collective-permute-start.2 = (f32[768,16]{0,1:T(8,128)S(1)}, f32[768,16]{0,1:T(8,128)S(1)}, u32[]{:S(2)}, u32[]{:S(2)}) collective-permute-start(f32[768,16]{0,1:T(8,128)S(1)} %get-tuple-element.32), channel_id=1, source_target_pairs={{8,0},{16,8},{24,16},{32,24},{40,32},{48,40},{56,48},{64,56},{72,6... | collective-permute-start | bytes 147464 | tf_op jit(solution)/shard_map/ppermute | solution.py:109
  57.1 8.3 %collective-permute-start.3 = (f32[768,16]{0,1:T(8,128)S(1)}, f32[768,16]{0,1:T(8,128)S(1)}, u32[]{:S(2)}, u32[]{:S(2)}) collective-permute-start(f32[768,16]{0,1:T(8,128)S(1)} %get-tuple-element.33), channel_id=1, source_target_pairs={{0,8},{8,16},{16,24},{24,32},{32,40},{40,48},{48,56},{56,64},{64,7... | collective-permute-start | bytes 147464 | tf_op jit(solution)/shard_map/ppermute | solution.py:109
  66.1 37.1 %collective-permute-start.12 = (bf16[768,1,1,16]{0,3,2,1:T(8,128)(2,1)S(1)}, bf16[768,1,1,16]{0,3,2,1:T(8,128)(2,1)S(1)}, u32[]{:S(2)}, u32[]{:S(2)}) collective-permute-start(bf16[768,1,1,16]{0,3,2,1:T(8,128)(2,1)S(1)} %reshape.148), channel_id=1, source_target_pairs={{8,0},{16,8},{24,16},{32,24},{40,32},{48,40},{56,48},{64,56},{72,6... | collective-permute-start | bytes 73736 | tf_op jit(solution)/shard_map/ppermute | solution.py:101
  68.1 35.1 %collective-permute-start.11 = (bf16[768,1,1,16]{0,3,2,1:T(8,128)(2,1)S(1)}, bf16[768,1,1,16]{0,3,2,1:T(8,128)(2,1)S(1)}, u32[]{:S(2)}, u32[]{:S(2)}) collective-permute-start(bf16[768,1,1,16]{0,3,2,1:T(8,128)(2,1)S(1)} %reshape.148), channel_id=1, source_target_pairs={{0,8},{8,16},{16,24},{24,32},{32,40},{40,48},{48,56},{56,64},{64,7... | collective-permute-start | bytes 73736 | tf_op jit(solution)/shard_map/ppermute | solution.py:100
  103.2 6.4 %collective-permute-start.14 = (bf16[768,3,1,16]{0,3,2,1:T(8,128)(2,1)S(1)}, bf16[768,3,1,16]{0,3,2,1:T(8,128)(2,1)S(1)}, u32[]{:S(2)}, u32[]{:S(2)}) collective-permute-start(bf16[768,3,1,16]{0,3,2,1:T(8,128)(2,1)S(1)} %constant_dynamic-update-slice_fusion), channel_id=1, source_target_pairs={{1,0},{2,1},{3,2},{4,3},{5,4},{6,5},{7,6},{9,8},{10,9},{11,10},{12... | collective-permute-start | bytes 221192 | tf_op jit(solution)/shard_map/ppermute | solution.py:101
  173.5 6.5 %collective-permute-start.20 = (f32[768,3,16]{0,2,1:T(8,128)S(1)}, f32[768,3,16]{0,2,1:T(8,128)S(1)}, u32[]{:S(2)}, u32[]{:S(2)}) collective-permute-start(f32[768,3,16]{0,2,1:T(8,128)S(1)} %get-tuple-element.23), channel_id=1, source_target_pairs={{0,1},{1,2},{2,3},{3,4},{4,5},{5,6},{6,7},{8,9},{9,10},{10,11},{11... | collective-permute-start | bytes 442376 | tf_op jit(solution)/shard_map/ppermute | solution.py:109
  180.0 6.3 %collective-permute-start.21 = (f32[768,16]{0,1:T(8,128)S(1)}, f32[768,16]{0,1:T(8,128)S(1)}, u32[]{:S(2)}, u32[]{:S(2)}) collective-permute-start(f32[768,16]{0,1:T(8,128)S(1)} %get-tuple-element.30), channel_id=1, source_target_pairs={{8,0},{16,8},{24,16},{32,24},{40,32},{48,40},{56,48},{64,56},{72,6... | collective-permute-start | bytes 147464 | tf_op jit(solution)/shard_map/ppermute | solution.py:109
  184.4 8.1 %collective-permute-start.22 = (f32[768,16]{0,1:T(8,128)S(1)}, f32[768,16]{0,1:T(8,128)S(1)}, u32[]{:S(2)}, u32[]{:S(2)}) collective-permute-start(f32[768,16]{0,1:T(8,128)S(1)} %get-tuple-element.31), channel_id=1, source_target_pairs={{0,8},{8,16},{16,24},{24,32},{32,40},{40,48},{48,56},{56,64},{64,7... | collective-permute-start | bytes 147464 | tf_op jit(solution)/shard_map/ppermute | solution.py:109
  193.3 37.1 %collective-permute-start.31 = (bf16[768,1,1,16]{0,3,2,1:T(8,128)(2,1)S(1)}, bf16[768,1,1,16]{0,3,2,1:T(8,128)(2,1)S(1)}, u32[]{:S(2)}, u32[]{:S(2)}) collective-permute-start(bf16[768,1,1,16]{0,3,2,1:T(8,128)(2,1)S(1)} %reshape.163), channel_id=1, source_target_pairs={{8,0},{16,8},{24,16},{32,24},{40,32},{48,40},{56,48},{64,56},{72,6... | collective-permute-start | bytes 73736 | tf_op jit(solution)/shard_map/ppermute | solution.py:101
  195.2 35.1 %collective-permute-start.30 = (bf16[768,1,1,16]{0,3,2,1:T(8,128)(2,1)S(1)}, bf16[768,1,1,16]{0,3,2,1:T(8,128)(2,1)S(1)}, u32[]{:S(2)}, u32[]{:S(2)}) collective-permute-start(bf16[768,1,1,16]{0,3,2,1:T(8,128)(2,1)S(1)} %reshape.163), channel_id=1, source_target_pairs={{0,8},{8,16},{16,24},{24,32},{32,40},{40,48},{48,56},{56,64},{64,7... | collective-permute-start | bytes 73736 | tf_op jit(solution)/shard_map/ppermute | solution.py:100
  230.4 6.4 %collective-permute-start.33 = (bf16[768,3,1,16]{0,3,2,1:T(8,128)(2,1)S(1)}, bf16[768,3,1,16]{0,3,2,1:T(8,128)(2,1)S(1)}, u32[]{:S(2)}, u32[]{:S(2)}) collective-permute-start(bf16[768,3,1,16]{0,3,2,1:T(8,128)(2,1)S(1)} %constant_dynamic-update-slice_fusion.6), channel_id=1, source_target_pairs={{1,0},{2,1},{3,2},{4,3},{5,4},{6,5},{7,6},{9,8},{10,9},{11,10},{12... | collective-permute-start | bytes 221192 | tf_op jit(solution)/shard_map/ppermute | solution.py:101
  287.1 6.5 %collective-permute-start.35 = (f32[768,3,16]{0,2,1:T(8,128)S(1)}, f32[768,3,16]{0,2,1:T(8,128)S(1)}, u32[]{:S(2)}, u32[]{:S(2)}) collective-permute-start(f32[768,3,16]{0,2,1:T(8,128)S(1)} %get-tuple-element.21), channel_id=1, source_target_pairs={{0,1},{1,2},{2,3},{3,4},{4,5},{5,6},{6,7},{8,9},{9,10},{10,11},{11... | collective-permute-start | bytes 442376 | tf_op jit(solution)/shard_map/ppermute | solution.py:109
  297.7 8.1 %collective-permute-start.37 = (f32[768,16]{0,1:T(8,128)S(1)}, f32[768,16]{0,1:T(8,128)S(1)}, u32[]{:S(2)}, u32[]{:S(2)}) collective-permute-start(f32[768,16]{0,1:T(8,128)S(1)} %get-tuple-element.29), channel_id=1, source_target_pairs={{0,8},{8,16},{16,24},{24,32},{32,40},{40,48},{48,56},{56,64},{64,7... | collective-permute-start | bytes 147464 | tf_op jit(solution)/shard_map/ppermute | solution.py:109
  306.5 37.1 %collective-permute-start.46 = (bf16[768,1,1,16]{0,3,2,1:T(8,128)(2,1)S(1)}, bf16[768,1,1,16]{0,3,2,1:T(8,128)(2,1)S(1)}, u32[]{:S(2)}, u32[]{:S(2)}) collective-permute-start(bf16[768,1,1,16]{0,3,2,1:T(8,128)(2,1)S(1)} %reshape.173), channel_id=1, source_target_pairs={{8,0},{16,8},{24,16},{32,24},{40,32},{48,40},{56,48},{64,56},{72,6... | collective-permute-start | bytes 73736 | tf_op jit(solution)/shard_map/ppermute | solution.py:101
  308.4 35.1 %collective-permute-start.45 = (bf16[768,1,1,16]{0,3,2,1:T(8,128)(2,1)S(1)}, bf16[768,1,1,16]{0,3,2,1:T(8,128)(2,1)S(1)}, u32[]{:S(2)}, u32[]{:S(2)}) collective-permute-start(bf16[768,1,1,16]{0,3,2,1:T(8,128)(2,1)S(1)} %reshape.173), channel_id=1, source_target_pairs={{0,8},{8,16},{16,24},{24,32},{32,40},{40,48},{48,56},{56,64},{64,7... | collective-permute-start | bytes 73736 | tf_op jit(solution)/shard_map/ppermute | solution.py:100
  343.6 6.5 %collective-permute-start.48 = (bf16[768,3,1,16]{0,3,2,1:T(8,128)(2,1)S(1)}, bf16[768,3,1,16]{0,3,2,1:T(8,128)(2,1)S(1)}, u32[]{:S(2)}, u32[]{:S(2)}) collective-permute-start(bf16[768,3,1,16]{0,3,2,1:T(8,128)(2,1)S(1)} %constant_dynamic-update-slice_fusion.9), channel_id=1, source_target_pairs={{1,0},{2,1},{3,2},{4,3},{5,4},{6,5},{7,6},{9,8},{10,9},{11,10},{12... | collective-permute-start | bytes 221192 | tf_op jit(solution)/shard_map/ppermute | solution.py:101
  400.4 6.5 %collective-permute-start.50 = (f32[768,3,16]{0,2,1:T(8,128)S(1)}, f32[768,3,16]{0,2,1:T(8,128)S(1)}, u32[]{:S(2)}, u32[]{:S(2)}) collective-permute-start(f32[768,3,16]{0,2,1:T(8,128)S(1)} %get-tuple-element.19), channel_id=1, source_target_pairs={{0,1},{1,2},{2,3},{3,4},{4,5},{5,6},{6,7},{8,9},{9,10},{10,11},{11... | collective-permute-start | bytes 442376 | tf_op jit(solution)/shard_map/ppermute | solution.py:109
  411.0 8.1 %collective-permute-start.52 = (f32[768,16]{0,1:T(8,128)S(1)}, f32[768,16]{0,1:T(8,128)S(1)}, u32[]{:S(2)}, u32[]{:S(2)}) collective-permute-start(f32[768,16]{0,1:T(8,128)S(1)} %get-tuple-element.27), channel_id=1, source_target_pairs={{0,8},{8,16},{16,24},{24,32},{32,40},{40,48},{48,56},{56,64},{64,7... | collective-permute-start | bytes 147464 | tf_op jit(solution)/shard_map/ppermute | solution.py:109
  (35 other events, 656.2 us)

commit v8 on v7

--- a/solution.py
+++ b/solution.py
@@ -109,14 +109,23 @@
     return lax.ppermute(block, axis, route)
 
 
-def butterfly_sum(array, axes):
-    size = 1
+def exchange_sum(array, axes):
     for axis in axes:
-        size *= lax.axis_size(axis)
-    step = 1
-    while step < size:
-        array = array + lax.ppermute(array, axes, [(i, i ^ step) for i in range(size)])
-        step = step * 2
+        size = lax.axis_size(axis)
+        parts = [array] + [
+            lax.ppermute(array, axis, [(i, (i + k) % size) for i in range(size)])
+            for k in range(1, size)
+        ]
+        own = lax.axis_index(axis)
+        ordered = []
+        for position in range(size):
+            chosen = parts[0]
+            for k in range(1, size):
+                chosen = jnp.where((own - k) % size == position, parts[k], chosen)
+            ordered.append(chosen)
+        while len(ordered) > 1:
+            ordered = [ordered[i] + ordered[i + 1] for i in range(0, len(ordered), 2)]
+        array = ordered[0]
     return array
 
 
@@ -197,9 +206,9 @@
     for iteration in range(ITERS):
         pushed = backward(extrapolated.astype(jnp.bfloat16))
         moved = inverse_mass * pushed
-        totals = butterfly_sum(
+        totals = exchange_sum(
             jnp.stack([jnp.sum(extrapolated * extrapolated), jnp.sum(pushed * moved)]),
-            GX_GY,
+            ("gy_1", "gy_0", "gx_1", "gx_0"),
         )
         size_total, energy_total = totals[0], totals[1]
         gradient = (forward(moved.astype(jnp.bfloat16)) + constraint_bias) * live_mask

time: 423 us -> 405 us (0.957)
  waiting for transfers between devices: 101 us -> 69.3 us
  starting transfers between devices: 107 us -> 123 us
    ppermute x21 -> x30, waiting for transfers between devices: 60.5 us -> 28.5 us  [exchange_sum(): lax.ppermute(array, axis, [(i, (i + k) % size) for i in range(size)])]
    ppermute x21 -> x30, starting transfers between devices: 20.9 us -> 36.9 us  [exchange_sum(): lax.ppermute(array, axis, [(i, (i + k) % size) for i in range(size)])]
  transfers between devices with their start and end apart: 53 -> 62, of which waited for: 34 -> 36; matrix products, arithmetic and copies ran while one was open for 7% -> 7% of each run, Pallas kernels for 4% -> 4%
where the time goes in v8:
time: 405 us; the launch traced here: 400 us
  starting transfers between devices  123 us (30%)
  other arithmetic  113 us (28%)
  waiting for transfers between devices  69.3 us (17%)
  Pallas kernels  65.8 us (16%)
  local copies, waits for them, and re-layouts  22.9 us (6%)
  between operations  6.53 us (2%)
    unnamed x14, other arithmetic  97.8 us
    ppermute x16, starting transfers between devices, from_behind(): return lax.ppermute(block, axis, route)  44.1 us
    pallas_call x4, Pallas kernels, scatter_field(): pl.pallas_call(_scatter_kernel, grid=(slots // TILE,), in_specs=[pl.Block...  39.2 us
    ppermute x30, starting transfers between devices, exchange_sum(): lax.ppermute(array, axis, [(i, (i + k) % size) for i in range(size)])  36.9 us
    ppermute x16, waiting for transfers between devices, from_behind(): return lax.ppermute(block, axis, route)  36.6 us
    ppermute x30, waiting for transfers between devices, exchange_sum(): lax.ppermute(array, axis, [(i, (i + k) % size) for i in range(size)])  28.5 us
    pallas_call x4, Pallas kernels, gather_field(): pl.pallas_call(_gather_kernel, grid=(slots // TILE,), in_specs=[pl.BlockS...  26.5 us
    ppermute x8, starting transfers between devices, with_halo(): before = lax.ppermute(last, axis, up)  24 us
  transfers between devices with their start and end apart: 62, of which 36 were waited for; matrix products, arithmetic and copies ran while one was open for 7% of the time, Pallas kernels for 4%

profile of v8, /device:TPU:34, one launch (start us, length us, event | category | flops | bytes accessed | tf_op | source)
XLA Modules:
  0.0 400.3 jit_solution(12456158263602328935)
XLA Ops:
  1.6 4.5 %collective-permute-start.19 = (bf16[768,1,1,16]{0,3,2,1:T(8,128)(2,1)S(1)}, bf16[768,1,1,16]{0,3,2,1:T(8,128)(2,1)S(1)}, u32[]{:S(2)}, u32[]{:S(2)}) collective-permute-start(bf16[768,1,1,16]{0,3,2,1:T(8,128)(2,1)S(1)} %reshape.153), channel_id=1, source_target_pairs={{8,0},{16,8},{24,16},{32,24},{40,32},{48,40},{56,48},{64,56},{72,6... | collective-permute-start | bytes 73736 | tf_op jit(solution)/shard_map/ppermute | solution.py:101
  10.3 9.1 %fusion = f32[128,384]{1,0:T(8,128)S(1)} fusion(bf16[128,192,384]{2,1,0:T(8,128)(2,1)} %param.8, f32[128,192]{1,0:T(8,128)S(1)} %copy.125), kind=kLoop, calls=%fused_computation.8 | loop fusion | flops 28262400 | bytes 19169280
  21.4 9.8 %shard_map.95 = f32[768,144]{1,0:T(8,128)} custom-call(f32[6,8192]{1,0:T(8,128)} %reshape.142.push_ref, s32[1,8192]{1,0:T(1,128)} %reshape.143.idx_ref), custom_call_target="tpu_custom_call" | custom-call | tf_op jit(solution)/shard_map/pallas_call | solution.py:69
  43.3 6.6 %shard_map.97 = bf16[6,8192]{1,0:T(8,128)(2,1)} custom-call(bf16[768,144]{1,0:T(8,128)(2,1)} %copy.68.field_ref, s32[1,8192]{1,0:T(1,128)} %reshape.143.idx_ref), custom_call_target="tpu_custom_call" | custom-call | tf_op jit(solution)/shard_map/pallas_call | solution.py:32
  51.3 6.0 %collective-permute-start.2 = (f32[768,16]{0,1:T(8,128)S(1)}, f32[768,16]{0,1:T(8,128)S(1)}, u32[]{:S(2)}, u32[]{:S(2)}) collective-permute-start(f32[768,16]{0,1:T(8,128)S(1)} %get-tuple-element.32), channel_id=1, source_target_pairs={{8,0},{16,8},{24,16},{32,24},{40,32},{48,40},{56,48},{64,56},{72,6... | collective-permute-start | bytes 147464 | tf_op jit(solution)/shard_map/ppermute | solution.py:109
  59.4 6.2 %collective-permute-done.3 = f32[768,16]{0,1:T(8,128)S(1)} collective-permute-done((f32[768,16]{0,1:T(8,128)S(1)}, f32[768,16]{0,1:T(8,128)S(1)}, u32[]{:S(2)}, u32[]{:S(2)}) %collective-permute-start.3) | collective-permute-done | bytes 49184 | tf_op jit(solution)/shard_map/ppermute | solution.py:109
  83.1 4.0 %collective-permute-start.9 = (f32[2]{0:T(128)S(1)}, f32[2]{0:T(128)S(1)}, u32[]{:S(2)}, u32[]{:S(2)}) collective-permute-start(f32[2]{0:T(128)S(1)} %fusion.57), channel_id=1, source_target_pairs={{0,16},{8,24},{16,0},{24,8},{1,17},{9,25},{17,1},{25,9},{2,18},{10... | collective-permute-start | bytes 32 | tf_op jit(solution)/shard_map/ppermute | solution.py:116
  106.3 6.6 %shard_map.96 = bf16[6,8192]{1,0:T(8,128)(2,1)} custom-call(bf16[768,144]{1,0:T(8,128)(2,1)} %copy.65.field_ref, s32[1,8192]{1,0:T(1,128)} %reshape.143.idx_ref), custom_call_target="tpu_custom_call" | custom-call | tf_op jit(solution)/shard_map/pallas_call | solution.py:32
  114.4 29.1 %fusion.5 = (f32[128,192]{1,0:T(8,128)S(1)}, f32[128,192]{1,0:T(8,128)S(1)}) fusion(f32[128,384]{1,0:T(8,128)S(1)} %copy.127, bf16[128,192,384]{2,1,0:T(8,128)(2,1)} %param.8, f32[128,384]{1,0:T(8,128)S(1)} %copy.126), kind=kLoop, calls=%fused_computation.13 | loop fusion | flops 47136768 | bytes 19464192
  144.6 9.1 %fusion.1 = f32[128,384]{1,0:T(8,128)S(1)} fusion(bf16[128,192,384]{2,1,0:T(8,128)(2,1)} %param.8, f32[128,192]{1,0:T(8,128)S(1)} %copy.128), kind=kLoop, calls=%fused_computation.9 | loop fusion | flops 28262400 | bytes 19169280
  154.9 9.8 %shard_map.98 = f32[768,144]{1,0:T(8,128)} custom-call(f32[6,8192]{1,0:T(8,128)} %reshape.158.push_ref, s32[1,8192]{1,0:T(1,128)} %reshape.143.idx_ref), custom_call_target="tpu_custom_call" | custom-call | tf_op jit(solution)/shard_map/pallas_call | solution.py:69
  174.6 4.5 %collective-permute-start.24 = (f32[768,16]{0,1:T(8,128)S(1)}, f32[768,16]{0,1:T(8,128)S(1)}, u32[]{:S(2)}, u32[]{:S(2)}) collective-permute-start(f32[768,16]{0,1:T(8,128)S(1)} %get-tuple-element.30), channel_id=1, source_target_pairs={{8,0},{16,8},{24,16},{32,24},{40,32},{48,40},{56,48},{64,56},{72,6... | collective-permute-start | bytes 147464 | tf_op jit(solution)/shard_map/ppermute | solution.py:109
  181.1 6.2 %collective-permute-done.25 = f32[768,16]{0,1:T(8,128)S(1)} collective-permute-done((f32[768,16]{0,1:T(8,128)S(1)}, f32[768,16]{0,1:T(8,128)S(1)}, u32[]{:S(2)}, u32[]{:S(2)}) %collective-permute-start.25) | collective-permute-done | bytes 49184 | tf_op jit(solution)/shard_map/ppermute | solution.py:109
  227.7 6.6 %shard_map.99 = bf16[6,8192]{1,0:T(8,128)(2,1)} custom-call(bf16[768,144]{1,0:T(8,128)(2,1)} %copy.74.field_ref, s32[1,8192]{1,0:T(1,128)} %reshape.143.idx_ref), custom_call_target="tpu_custom_call" | custom-call | tf_op jit(solution)/shard_map/pallas_call | solution.py:32
  235.7 15.7 %fusion.6 = f32[128,192]{1,0:T(8,128)S(1)} fusion(f32[128,384]{1,0:T(8,128)S(1)} %copy.129, bf16[128,192,384]{2,1,0:T(8,128)(2,1)} %param.8), kind=kLoop, calls=%fused_computation.14 | loop fusion | flops 28286976 | bytes 19169280
  252.3 9.1 %fusion.2 = f32[128,384]{1,0:T(8,128)S(1)} fusion(bf16[128,192,384]{2,1,0:T(8,128)(2,1)} %param.8, f32[128,192]{1,0:T(8,128)S(1)} %copy.130), kind=kLoop, calls=%fused_computation.10 | loop fusion | flops 28262400 | bytes 19169280
  262.6 9.8 %shard_map.100 = f32[768,144]{1,0:T(8,128)} custom-call(f32[6,8192]{1,0:T(8,128)} %reshape.168.push_ref, s32[1,8192]{1,0:T(1,128)} %reshape.143.idx_ref), custom_call_target="tpu_custom_call" | custom-call | tf_op jit(solution)/shard_map/pallas_call | solution.py:69
  288.4 5.5 %collective-permute-done.43 = f32[768,16]{0,1:T(8,128)S(1)} collective-permute-done((f32[768,16]{0,1:T(8,128)S(1)}, f32[768,16]{0,1:T(8,128)S(1)}, u32[]{:S(2)}, u32[]{:S(2)}) %collective-permute-start.43) | collective-permute-done | bytes 49184 | tf_op jit(solution)/shard_map/ppermute | solution.py:109
  332.8 6.6 %shard_map.101 = bf16[6,8192]{1,0:T(8,128)(2,1)} custom-call(bf16[768,144]{1,0:T(8,128)(2,1)} %copy.80.field_ref, s32[1,8192]{1,0:T(1,128)} %reshape.143.idx_ref), custom_call_target="tpu_custom_call" | custom-call | tf_op jit(solution)/shard_map/pallas_call | solution.py:32
  340.8 15.7 %fusion.7 = f32[128,192]{1,0:T(8,128)S(1)} fusion(f32[128,384]{1,0:T(8,128)S(1)} %copy.131, bf16[128,192,384]{2,1,0:T(8,128)(2,1)} %param.8), kind=kLoop, calls=%fused_computation.15 | loop fusion | flops 28286976 | bytes 19169280
  357.5 9.1 %fusion.3 = f32[128,384]{1,0:T(8,128)S(1)} fusion(bf16[128,192,384]{2,1,0:T(8,128)(2,1)} %param.8, f32[128,192]{1,0:T(8,128)S(1)} %copy.132), kind=kLoop, calls=%fused_computation.11 | loop fusion | flops 28262400 | bytes 19169280
  367.8 9.8 %shard_map.102 = f32[768,144]{1,0:T(8,128)} custom-call(f32[6,8192]{1,0:T(8,128)} %reshape.178.push_ref, s32[1,8192]{1,0:T(1,128)} %reshape.143.idx_ref), custom_call_target="tpu_custom_call" | custom-call | tf_op jit(solution)/shard_map/pallas_call | solution.py:69
  387.6 3.9 collective-permute-start.60
  393.5 6.0 %collective-permute-done.61 = f32[768,16]{0,1:T(8,128)S(1)} collective-permute-done((f32[768,16]{0,1:T(8,128)S(1)}, f32[768,16]{0,1:T(8,128)S(1)}, u32[]{:S(2)}, u32[]{:S(2)}) %collective-permute-start.61) | collective-permute-done | bytes 49184 | tf_op jit(solution)/shard_map/ppermute | solution.py:109
  (252 shorter events, 184.1 us)
Async XLA Ops:
  1.6 31.0 %collective-permute-start.19 = (bf16[768,1,1,16]{0,3,2,1:T(8,128)(2,1)S(1)}, bf16[768,1,1,16]{0,3,2,1:T(8,128)(2,1)S(1)}, u32[]{:S(2)}, u32[]{:S(2)}) collective-permute-start(bf16[768,1,1,16]{0,3,2,1:T(8,128)(2,1)S(1)} %reshape.153), channel_id=1, source_target_pairs={{8,0},{16,8},{24,16},{32,24},{40,32},{48,40},{56,48},{64,56},{72,6... | collective-permute-start | bytes 73736 | tf_op jit(solution)/shard_map/ppermute | solution.py:101
  6.1 26.5 %collective-permute-start.18 = (bf16[768,1,1,16]{0,3,2,1:T(8,128)(2,1)S(1)}, bf16[768,1,1,16]{0,3,2,1:T(8,128)(2,1)S(1)}, u32[]{:S(2)}, u32[]{:S(2)}) collective-permute-start(bf16[768,1,1,16]{0,3,2,1:T(8,128)(2,1)S(1)} %reshape.153), channel_id=1, source_target_pairs={{0,8},{8,16},{16,24},{24,32},{32,40},{40,48},{48,56},{56,64},{64,7... | collective-permute-start | bytes 73736 | tf_op jit(solution)/shard_map/ppermute | solution.py:100
  32.6 9.7 %collective-permute-start.21 = (bf16[768,3,1,16]{0,3,2,1:T(8,128)(2,1)S(1)}, bf16[768,3,1,16]{0,3,2,1:T(8,128)(2,1)S(1)}, u32[]{:S(2)}, u32[]{:S(2)}) collective-permute-start(bf16[768,3,1,16]{0,3,2,1:T(8,128)(2,1)S(1)} %constant_dynamic-update-slice_fusion.3), channel_id=1, source_target_pairs={{1,0},{2,1},{3,2},{4,3},{5,4},{6,5},{7,6},{9,8},{10,9},{11,10},{12... | collective-permute-start | bytes 221192 | tf_op jit(solution)/shard_map/ppermute | solution.py:101
  34.6 7.8 %collective-permute-start.20 = (bf16[768,3,1,16]{0,3,2,1:T(8,128)(2,1)S(1)}, bf16[768,3,1,16]{0,3,2,1:T(8,128)(2,1)S(1)}, u32[]{:S(2)}, u32[]{:S(2)}) collective-permute-start(bf16[768,3,1,16]{0,3,2,1:T(8,128)(2,1)S(1)} %constant_dynamic-update-slice_fusion.3), channel_id=1, source_target_pairs={{0,1},{1,2},{2,3},{3,4},{4,5},{5,6},{6,7},{8,9},{9,10},{10,11},{11... | collective-permute-start | bytes 221192 | tf_op jit(solution)/shard_map/ppermute | solution.py:100
  37.0 14.2 %collective-permute-start = (f32[768,3,16]{0,2,1:T(8,128)S(1)}, f32[768,3,16]{0,2,1:T(8,128)S(1)}, u32[]{:S(2)}, u32[]{:S(2)}) collective-permute-start(f32[768,3,16]{0,2,1:T(8,128)S(1)} %get-tuple-element.24), channel_id=1, source_target_pairs={{1,0},{2,1},{3,2},{4,3},{5,4},{6,5},{7,6},{9,8},{10,9},{11,10},{12... | collective-permute-start | bytes 442376 | tf_op jit(solution)/shard_map/ppermute | solution.py:109
  40.2 11.0 %collective-permute-start.1 = (f32[768,3,16]{0,2,1:T(8,128)S(1)}, f32[768,3,16]{0,2,1:T(8,128)S(1)}, u32[]{:S(2)}, u32[]{:S(2)}) collective-permute-start(f32[768,3,16]{0,2,1:T(8,128)S(1)} %get-tuple-element.25), channel_id=1, source_target_pairs={{0,1},{1,2},{2,3},{3,4},{4,5},{5,6},{6,7},{8,9},{9,10},{10,11},{11... | collective-permute-start | bytes 442376 | tf_op jit(solution)/shard_map/ppermute | solution.py:109
  51.3 8.1 %collective-permute-start.2 = (f32[768,16]{0,1:T(8,128)S(1)}, f32[768,16]{0,1:T(8,128)S(1)}, u32[]{:S(2)}, u32[]{:S(2)}) collective-permute-start(f32[768,16]{0,1:T(8,128)S(1)} %get-tuple-element.32), channel_id=1, source_target_pairs={{8,0},{16,8},{24,16},{32,24},{40,32},{48,40},{56,48},{64,56},{72,6... | collective-permute-start | bytes 147464 | tf_op jit(solution)/shard_map/ppermute | solution.py:109
  57.3 8.3 %collective-permute-start.3 = (f32[768,16]{0,1:T(8,128)S(1)}, f32[768,16]{0,1:T(8,128)S(1)}, u32[]{:S(2)}, u32[]{:S(2)}) collective-permute-start(f32[768,16]{0,1:T(8,128)S(1)} %get-tuple-element.33), channel_id=1, source_target_pairs={{0,8},{8,16},{16,24},{24,32},{32,40},{40,48},{48,56},{56,64},{64,7... | collective-permute-start | bytes 147464 | tf_op jit(solution)/shard_map/ppermute | solution.py:109
  66.3 31.5 %collective-permute-start.15 = (bf16[768,1,1,16]{0,3,2,1:T(8,128)(2,1)S(1)}, bf16[768,1,1,16]{0,3,2,1:T(8,128)(2,1)S(1)}, u32[]{:S(2)}, u32[]{:S(2)}) collective-permute-start(bf16[768,1,1,16]{0,3,2,1:T(8,128)(2,1)S(1)} %reshape.148), channel_id=1, source_target_pairs={{8,0},{16,8},{24,16},{32,24},{40,32},{48,40},{56,48},{64,56},{72,6... | collective-permute-start | bytes 73736 | tf_op jit(solution)/shard_map/ppermute | solution.py:101
  68.2 29.5 %collective-permute-start.14 = (bf16[768,1,1,16]{0,3,2,1:T(8,128)(2,1)S(1)}, bf16[768,1,1,16]{0,3,2,1:T(8,128)(2,1)S(1)}, u32[]{:S(2)}, u32[]{:S(2)}) collective-permute-start(bf16[768,1,1,16]{0,3,2,1:T(8,128)(2,1)S(1)} %reshape.148), channel_id=1, source_target_pairs={{0,8},{8,16},{16,24},{24,32},{32,40},{40,48},{48,56},{56,64},{64,7... | collective-permute-start | bytes 73736 | tf_op jit(solution)/shard_map/ppermute | solution.py:100
  97.8 6.4 %collective-permute-start.17 = (bf16[768,3,1,16]{0,3,2,1:T(8,128)(2,1)S(1)}, bf16[768,3,1,16]{0,3,2,1:T(8,128)(2,1)S(1)}, u32[]{:S(2)}, u32[]{:S(2)}) collective-permute-start(bf16[768,3,1,16]{0,3,2,1:T(8,128)(2,1)S(1)} %constant_dynamic-update-slice_fusion), channel_id=1, source_target_pairs={{1,0},{2,1},{3,2},{4,3},{5,4},{6,5},{7,6},{9,8},{10,9},{11,10},{12... | collective-permute-start | bytes 221192 | tf_op jit(solution)/shard_map/ppermute | solution.py:101
  168.1 6.5 %collective-permute-start.23 = (f32[768,3,16]{0,2,1:T(8,128)S(1)}, f32[768,3,16]{0,2,1:T(8,128)S(1)}, u32[]{:S(2)}, u32[]{:S(2)}) collective-permute-start(f32[768,3,16]{0,2,1:T(8,128)S(1)} %get-tuple-element.23), channel_id=1, source_target_pairs={{0,1},{1,2},{2,3},{3,4},{4,5},{5,6},{6,7},{8,9},{9,10},{10,11},{11... | collective-permute-start | bytes 442376 | tf_op jit(solution)/shard_map/ppermute | solution.py:109
  174.6 6.5 %collective-permute-start.24 = (f32[768,16]{0,1:T(8,128)S(1)}, f32[768,16]{0,1:T(8,128)S(1)}, u32[]{:S(2)}, u32[]{:S(2)}) collective-permute-start(f32[768,16]{0,1:T(8,128)S(1)} %get-tuple-element.30), channel_id=1, source_target_pairs={{8,0},{16,8},{24,16},{32,24},{40,32},{48,40},{56,48},{64,56},{72,6... | collective-permute-start | bytes 147464 | tf_op jit(solution)/shard_map/ppermute | solution.py:109
  179.1 8.1 %collective-permute-start.25 = (f32[768,16]{0,1:T(8,128)S(1)}, f32[768,16]{0,1:T(8,128)S(1)}, u32[]{:S(2)}, u32[]{:S(2)}) collective-permute-start(f32[768,16]{0,1:T(8,128)S(1)} %get-tuple-element.31), channel_id=1, source_target_pairs={{0,8},{8,16},{16,24},{24,32},{32,40},{40,48},{48,56},{56,64},{64,7... | collective-permute-start | bytes 147464 | tf_op jit(solution)/shard_map/ppermute | solution.py:109
  188.0 30.5 %collective-permute-start.37 = (bf16[768,1,1,16]{0,3,2,1:T(8,128)(2,1)S(1)}, bf16[768,1,1,16]{0,3,2,1:T(8,128)(2,1)S(1)}, u32[]{:S(2)}, u32[]{:S(2)}) collective-permute-start(bf16[768,1,1,16]{0,3,2,1:T(8,128)(2,1)S(1)} %reshape.163), channel_id=1, source_target_pairs={{8,0},{16,8},{24,16},{32,24},{40,32},{48,40},{56,48},{64,56},{72,6... | collective-permute-start | bytes 73736 | tf_op jit(solution)/shard_map/ppermute | solution.py:101
  189.9 28.5 %collective-permute-start.36 = (bf16[768,1,1,16]{0,3,2,1:T(8,128)(2,1)S(1)}, bf16[768,1,1,16]{0,3,2,1:T(8,128)(2,1)S(1)}, u32[]{:S(2)}, u32[]{:S(2)}) collective-permute-start(bf16[768,1,1,16]{0,3,2,1:T(8,128)(2,1)S(1)} %reshape.163), channel_id=1, source_target_pairs={{0,8},{8,16},{16,24},{24,32},{32,40},{40,48},{48,56},{56,64},{64,7... | collective-permute-start | bytes 73736 | tf_op jit(solution)/shard_map/ppermute | solution.py:100
  218.5 6.4 %collective-permute-start.39 = (bf16[768,3,1,16]{0,3,2,1:T(8,128)(2,1)S(1)}, bf16[768,3,1,16]{0,3,2,1:T(8,128)(2,1)S(1)}, u32[]{:S(2)}, u32[]{:S(2)}) collective-permute-start(bf16[768,3,1,16]{0,3,2,1:T(8,128)(2,1)S(1)} %constant_dynamic-update-slice_fusion.6), channel_id=1, source_target_pairs={{1,0},{2,1},{3,2},{4,3},{5,4},{6,5},{7,6},{9,8},{10,9},{11,10},{12... | collective-permute-start | bytes 221192 | tf_op jit(solution)/shard_map/ppermute | solution.py:101
  275.9 6.5 %collective-permute-start.41 = (f32[768,3,16]{0,2,1:T(8,128)S(1)}, f32[768,3,16]{0,2,1:T(8,128)S(1)}, u32[]{:S(2)}, u32[]{:S(2)}) collective-permute-start(f32[768,3,16]{0,2,1:T(8,128)S(1)} %get-tuple-element.21), channel_id=1, source_target_pairs={{0,1},{1,2},{2,3},{3,4},{4,5},{5,6},{6,7},{8,9},{9,10},{10,11},{11... | collective-permute-start | bytes 442376 | tf_op jit(solution)/shard_map/ppermute | solution.py:109
  285.8 8.1 %collective-permute-start.43 = (f32[768,16]{0,1:T(8,128)S(1)}, f32[768,16]{0,1:T(8,128)S(1)}, u32[]{:S(2)}, u32[]{:S(2)}) collective-permute-start(f32[768,16]{0,1:T(8,128)S(1)} %get-tuple-element.29), channel_id=1, source_target_pairs={{0,8},{8,16},{16,24},{24,32},{32,40},{40,48},{48,56},{56,64},{64,7... | collective-permute-start | bytes 147464 | tf_op jit(solution)/shard_map/ppermute | solution.py:109
  294.6 29.5 %collective-permute-start.55 = (bf16[768,1,1,16]{0,3,2,1:T(8,128)(2,1)S(1)}, bf16[768,1,1,16]{0,3,2,1:T(8,128)(2,1)S(1)}, u32[]{:S(2)}, u32[]{:S(2)}) collective-permute-start(bf16[768,1,1,16]{0,3,2,1:T(8,128)(2,1)S(1)} %reshape.173), channel_id=1, source_target_pairs={{8,0},{16,8},{24,16},{32,24},{40,32},{48,40},{56,48},{64,56},{72,6... | collective-permute-start | bytes 73736 | tf_op jit(solution)/shard_map/ppermute | solution.py:101
  296.5 27.5 %collective-permute-start.54 = (bf16[768,1,1,16]{0,3,2,1:T(8,128)(2,1)S(1)}, bf16[768,1,1,16]{0,3,2,1:T(8,128)(2,1)S(1)}, u32[]{:S(2)}, u32[]{:S(2)}) collective-permute-start(bf16[768,1,1,16]{0,3,2,1:T(8,128)(2,1)S(1)} %reshape.173), channel_id=1, source_target_pairs={{0,8},{8,16},{16,24},{24,32},{32,40},{40,48},{48,56},{56,64},{64,7... | collective-permute-start | bytes 73736 | tf_op jit(solution)/shard_map/ppermute | solution.py:100
  324.1 6.5 %collective-permute-start.57 = (bf16[768,3,1,16]{0,3,2,1:T(8,128)(2,1)S(1)}, bf16[768,3,1,16]{0,3,2,1:T(8,128)(2,1)S(1)}, u32[]{:S(2)}, u32[]{:S(2)}) collective-permute-start(bf16[768,3,1,16]{0,3,2,1:T(8,128)(2,1)S(1)} %constant_dynamic-update-slice_fusion.9), channel_id=1, source_target_pairs={{1,0},{2,1},{3,2},{4,3},{5,4},{6,5},{7,6},{9,8},{10,9},{11,10},{12... | collective-permute-start | bytes 221192 | tf_op jit(solution)/shard_map/ppermute | solution.py:101
  381.0 6.5 %collective-permute-start.59 = (f32[768,3,16]{0,2,1:T(8,128)S(1)}, f32[768,3,16]{0,2,1:T(8,128)S(1)}, u32[]{:S(2)}, u32[]{:S(2)}) collective-permute-start(f32[768,3,16]{0,2,1:T(8,128)S(1)} %get-tuple-element.19), channel_id=1, source_target_pairs={{0,1},{1,2},{2,3},{3,4},{4,5},{5,6},{6,7},{8,9},{9,10},{10,11},{11... | collective-permute-start | bytes 442376 | tf_op jit(solution)/shard_map/ppermute | solution.py:109
  391.5 8.1 %collective-permute-start.61 = (f32[768,16]{0,1:T(8,128)S(1)}, f32[768,16]{0,1:T(8,128)S(1)}, u32[]{:S(2)}, u32[]{:S(2)}) collective-permute-start(f32[768,16]{0,1:T(8,128)S(1)} %get-tuple-element.27), channel_id=1, source_target_pairs={{0,8},{8,16},{16,24},{24,32},{32,40},{40,48},{48,56},{56,64},{64,7... | collective-permute-start | bytes 147464 | tf_op jit(solution)/shard_map/ppermute | solution.py:109
  (44 other events, 685.9 us)

commit v9 on v8

--- a/solution.py
+++ b/solution.py
@@ -116,15 +116,10 @@
             lax.ppermute(array, axis, [(i, (i + k) % size) for i in range(size)])
             for k in range(1, size)
         ]
-        own = lax.axis_index(axis)
-        ordered = []
-        for position in range(size):
-            chosen = parts[0]
-            for k in range(1, size):
-                chosen = jnp.where((own - k) % size == position, parts[k], chosen)
-            ordered.append(chosen)
+        ordered = parts
         while len(ordered) > 1:
-            ordered = [ordered[i] + ordered[i + 1] for i in range(0, len(ordered), 2)]
+            half = len(ordered) // 2
+            ordered = [ordered[i] + ordered[i + half] for i in range(half)]
         array = ordered[0]
     return array
 
@@ -200,10 +195,10 @@
 
     constraint_bias = velocity_bias + forward(free_velocity.astype(jnp.bfloat16))
     extrapolated = impulse_start * live_mask
-    previous = extrapolated
-    current = extrapolated
-    weights = momentum_weights(ITERS)
-    for iteration in range(ITERS):
+    weights = jnp.asarray(momentum_weights(ITERS), jnp.float32)
+
+    def iteration_step(iteration, carried):
+        extrapolated, previous = carried
         pushed = backward(extrapolated.astype(jnp.bfloat16))
         moved = inverse_mass * pushed
         totals = exchange_sum(
@@ -214,8 +209,9 @@
         gradient = (forward(moved.astype(jnp.bfloat16)) + constraint_bias) * live_mask
         step_size = size_total / (energy_total + epsilon)
         current = project_cone(extrapolated - step_size * gradient, friction) * live_mask
-        extrapolated = current + weights[iteration] * (current - previous)
-        previous = current
+        return current + weights[iteration] * (current - previous), current
+
+    extrapolated, current = lax.fori_loop(0, ITERS, iteration_step, (extrapolated, extrapolated))
     final_push = backward(current.astype(jnp.bfloat16))
     return (current, free_velocity + inverse_mass * final_push)
 

time: 405 us -> 406 us (level)
  other arithmetic: 113 us -> 19.8 us
  matrix products: 0 us -> 85.8 us
  starting transfers between devices: 123 us -> 140 us
  waiting for transfers between devices: 69.3 us -> 58.6 us
  local copies, waits for them, and re-layouts: 22.9 us -> 28.5 us
  between operations: 6.53 us -> 1.55 us
  loops' own time: 0 us -> 4.66 us
    unnamed x14 -> x0, other arithmetic: 97.8 us -> none
    dot_general x0 -> x8, matrix products: none -> 85.8 us  [the longest x4 51.7 us: forward(): jnp.einsum('bij,bj->bi', jacobian, picked, preferred_element_type=jnp.flo...]
    ppermute x16, waiting for transfers between devices: 36.6 us -> 18.9 us  [from_behind(): return lax.ppermute(block, axis, route)]
    ppermute x8, starting transfers between devices: 17.9 us -> 33.1 us  [with_halo(): after = lax.ppermute(leading, axis, down)]
    ppermute x16, starting transfers between devices: 44.1 us -> 50.8 us  [from_behind(): return lax.ppermute(block, axis, route)]
    ppermute x8, starting transfers between devices: 24 us -> 18.4 us  [with_halo(): before = lax.ppermute(last, axis, up)]
    another operation x0 -> x1, loops' own time: none -> 4.66 us  [shards(): lax.fori_loop(0, ITERS, iteration_step, (extrapolated, extrapolated))]
  transfers between devices with their start and end apart: 62 -> 62, of which waited for: 36 -> 40; matrix products, arithmetic and copies ran while one was open for 7% -> 5% of each run, Pallas kernels for 4% -> 0%
where the time goes in v9:
time: 406 us; the launch traced here: 404 us
  starting transfers between devices  140 us (34%)
  matrix products  85.8 us (21%)
  Pallas kernels  64.7 us (16%)
  waiting for transfers between devices  58.6 us (14%)
  local copies, waits for them, and re-layouts  28.5 us (7%)
  other arithmetic  19.8 us (5%)
  loops' own time  4.66 us (1%)
    dot_general x4, matrix products, forward(): jnp.einsum('bij,bj->bi', jacobian, picked, preferred_element_type=jnp.flo...  51.7 us
    ppermute x16, starting transfers between devices, from_behind(): return lax.ppermute(block, axis, route)  50.8 us
    pallas_call x4, Pallas kernels, scatter_field(): pl.pallas_call(_scatter_kernel, grid=(slots // TILE,), in_specs=[pl.Block...  39.3 us
    ppermute x30, starting transfers between devices, exchange_sum(): lax.ppermute(array, axis, [(i, (i + k) % size) for i in range(size)])  37.9 us
    dot_general x4, matrix products, backward(): jnp.einsum('bij,bi->bj', jacobian, impulse_field, preferred_element_type=...  34.1 us
    ppermute x8, starting transfers between devices, with_halo(): after = lax.ppermute(leading, axis, down)  33.1 us
    ppermute x30, waiting for transfers between devices, exchange_sum(): lax.ppermute(array, axis, [(i, (i + k) % size) for i in range(size)])  30.1 us
    pallas_call x4, Pallas kernels, gather_field(): pl.pallas_call(_gather_kernel, grid=(slots // TILE,), in_specs=[pl.BlockS...  25.5 us
  transfers between devices with their start and end apart: 62, of which 40 were waited for; matrix products, arithmetic and copies ran while one was open for 5% of the time, Pallas kernels for 0%

profile of v9, /device:TPU:34, one launch (start us, length us, event | category | flops | bytes accessed | tf_op | source)
XLA Modules:
  0.0 403.9 jit_solution(16199422538569206168)
XLA Ops:
  22.6 6.4 %shard_map.104 = bf16[6,8192]{1,0:T(8,128)(2,1)} custom-call(bf16[768,144]{1,0:T(8,128)(2,1)} %copy.57.field_ref, s32[1,8192]{1,0:T(1,128)S(1)} %reshape.121.idx_ref), custom_call_target="tpu_custom_call" | custom-call | tf_op jit(solution)/shard_map/pallas_call | solution.py:32
  30.4 12.9 %fusion.28 = f32[128,1,192]{2,1,0:T(1,128)S(1)} fusion(bf16[128,384,1]{1,2,0:T(2,128)(2,1)S(1)} %copy.71, bf16[128,192,384]{2,1,0:T(8,128)(2,1)} %param.11), kind=kOutput, calls=%fused_computation.73 | convolution fusion | flops 18874368 | bytes 19070976 | tf_op jit(solution)/shard_map/bij,bj->bi/dot_general | solution.py:179
  44.1 316.4 %while.18 = (s32[]{:T(128)}, f32[128,192]{1,0:T(8,128)S(1)}, f32[128,192]{1,0:T(8,128)S(1)}, bf16[128,192,384]{2,1,0:T(8,128)(2,1)}, s32[1,8192]{1,0:T(1,128)S(1...) while((s32[]{:T(128)}, f32[128,192]{1,0:T(8,128)S(1)}, ...), condition=%wide.region_3.4_spmd.clone.clone, body=%wide.region_0.3_spmd.sunk.clone.clone.sunk | while | flops 38609176 | bytes 47377276 | solution.py:214
  44.3 8.1 %fusion.54 = f32[128,1,384]{2,1,0:T(1,128)S(1)} fusion(bf16[128,192,384]{2,1,0:T(8,128)(2,1)} %get-tuple-element.527, bf16[128,192,1]{1,0,2:T(8,128)(2,1)S(1)} %convert_bitcast_fusion.4), kind=kOutput, calls=%fused_computation.14.clone.1 | convolution fusion | flops 18874368 | bytes 19120128 | tf_op jit(solution)/shard_map/while/body/eval_jaxpr/bij,bi->bj/dot_general | solution.py:182
  53.6 9.8 %eval_jaxpr.12 = f32[768,144]{1,0:T(8,128)} custom-call(f32[6,8192]{1,0:T(8,128)} %reshape.171.push_ref, s32[1,8192]{1,0:T(1,128)S(1)} %get-tuple-element.528.idx_ref), custom_call_target="tpu_custom_call" | custom-call | tf_op jit(solution)/shard_map/while/body/eval_jaxpr/pallas_call | solution.py:69
  75.1 6.0 %collective-permute-start.3 = (f32[768,16]{0,1:T(8,128)S(1)}, f32[768,16]{0,1:T(8,128)S(1)}, u32[]{:S(2)}, u32[]{:S(2)}) collective-permute-start(f32[768,16]{0,1:T(8,128)S(1)} %get-tuple-element.485), channel_id=1, source_target_pairs={{8,0},{16,8},{24,16},{32,24},{40,32},{48,40},{56,48},{64,56},{72,6... | collective-permute-start | bytes 147464 | tf_op jit(solution)/shard_map/while/body/eval_jaxpr/ppermute | solution.py:109
  85.6 6.4 %collective-permute-start.5 = (bf16[768,1,1,16]{0,3,2,1:T(8,128)(2,1)S(1)}, bf16[768,1,1,16]{0,3,2,1:T(8,128)(2,1)S(1)}, u32[]{:S(2)}, u32[]{:S(2)}) collective-permute-start(bf16[768,1,1,16]{0,3,2,1:T(8,128)(2,1)S(1)} %reshape.173), channel_id=1, source_target_pairs={{8,0},{16,8},{24,16},{32,24},{40,32},{48,40},{56,48},{64,56},{72,6... | collective-permute-start | bytes 73736 | tf_op jit(solution)/shard_map/while/body/eval_jaxpr/ppermute | solution.py:101
  127.1 6.4 %eval_jaxpr.13 = bf16[6,8192]{1,0:T(8,128)(2,1)} custom-call(bf16[768,144]{1,0:T(8,128)(2,1)} %copy.96.field_ref, s32[1,8192]{1,0:T(1,128)S(1)} %get-tuple-element.528.idx_ref), custom_call_target="tpu_custom_call" | custom-call | tf_op jit(solution)/shard_map/while/body/eval_jaxpr/pallas_call | solution.py:32
  134.9 12.9 %fusion.58 = f32[128,1,192]{2,1,0:T(1,128)S(1)} fusion(bf16[128,384,1]{1,2,0:T(2,128)(2,1)S(1)} %copy.98, bf16[128,192,384]{2,1,0:T(8,128)(2,1)} %get-tuple-element.527), kind=kOutput, calls=%fused_computation.72.clone.1 | convolution fusion | flops 18874368 | bytes 19070976 | tf_op jit(solution)/shard_map/while/body/eval_jaxpr/bij,bj->bi/dot_general | solution.py:179
  149.6 8.1 %fusion.54 = f32[128,1,384]{2,1,0:T(1,128)S(1)} fusion(bf16[128,192,384]{2,1,0:T(8,128)(2,1)} %get-tuple-element.527, bf16[128,192,1]{1,0,2:T(8,128)(2,1)S(1)} %convert_bitcast_fusion.4), kind=kOutput, calls=%fused_computation.14.clone.1 | convolution fusion | flops 18874368 | bytes 19120128 | tf_op jit(solution)/shard_map/while/body/eval_jaxpr/bij,bi->bj/dot_general | solution.py:182
  159.0 9.8 %eval_jaxpr.12 = f32[768,144]{1,0:T(8,128)} custom-call(f32[6,8192]{1,0:T(8,128)} %reshape.171.push_ref, s32[1,8192]{1,0:T(1,128)S(1)} %get-tuple-element.528.idx_ref), custom_call_target="tpu_custom_call" | custom-call | tf_op jit(solution)/shard_map/while/body/eval_jaxpr/pallas_call | solution.py:69
  180.4 6.0 %collective-permute-start.3 = (f32[768,16]{0,1:T(8,128)S(1)}, f32[768,16]{0,1:T(8,128)S(1)}, u32[]{:S(2)}, u32[]{:S(2)}) collective-permute-start(f32[768,16]{0,1:T(8,128)S(1)} %get-tuple-element.485), channel_id=1, source_target_pairs={{8,0},{16,8},{24,16},{32,24},{40,32},{48,40},{56,48},{64,56},{72,6... | collective-permute-start | bytes 147464 | tf_op jit(solution)/shard_map/while/body/eval_jaxpr/ppermute | solution.py:109
  191.1 6.5 %collective-permute-start.5 = (bf16[768,1,1,16]{0,3,2,1:T(8,128)(2,1)S(1)}, bf16[768,1,1,16]{0,3,2,1:T(8,128)(2,1)S(1)}, u32[]{:S(2)}, u32[]{:S(2)}) collective-permute-start(bf16[768,1,1,16]{0,3,2,1:T(8,128)(2,1)S(1)} %reshape.173), channel_id=1, source_target_pairs={{8,0},{16,8},{24,16},{32,24},{40,32},{48,40},{56,48},{64,56},{72,6... | collective-permute-start | bytes 73736 | tf_op jit(solution)/shard_map/while/body/eval_jaxpr/ppermute | solution.py:101
  232.8 6.4 %eval_jaxpr.13 = bf16[6,8192]{1,0:T(8,128)(2,1)} custom-call(bf16[768,144]{1,0:T(8,128)(2,1)} %copy.96.field_ref, s32[1,8192]{1,0:T(1,128)S(1)} %get-tuple-element.528.idx_ref), custom_call_target="tpu_custom_call" | custom-call | tf_op jit(solution)/shard_map/while/body/eval_jaxpr/pallas_call | solution.py:32
  240.6 12.9 %fusion.58 = f32[128,1,192]{2,1,0:T(1,128)S(1)} fusion(bf16[128,384,1]{1,2,0:T(2,128)(2,1)S(1)} %copy.98, bf16[128,192,384]{2,1,0:T(8,128)(2,1)} %get-tuple-element.527), kind=kOutput, calls=%fused_computation.72.clone.1 | convolution fusion | flops 18874368 | bytes 19070976 | tf_op jit(solution)/shard_map/while/body/eval_jaxpr/bij,bj->bi/dot_general | solution.py:179
  255.3 8.1 %fusion.54 = f32[128,1,384]{2,1,0:T(1,128)S(1)} fusion(bf16[128,192,384]{2,1,0:T(8,128)(2,1)} %get-tuple-element.527, bf16[128,192,1]{1,0,2:T(8,128)(2,1)S(1)} %convert_bitcast_fusion.4), kind=kOutput, calls=%fused_computation.14.clone.1 | convolution fusion | flops 18874368 | bytes 19120128 | tf_op jit(solution)/shard_map/while/body/eval_jaxpr/bij,bi->bj/dot_general | solution.py:182
  264.6 9.8 %eval_jaxpr.12 = f32[768,144]{1,0:T(8,128)} custom-call(f32[6,8192]{1,0:T(8,128)} %reshape.171.push_ref, s32[1,8192]{1,0:T(1,128)S(1)} %get-tuple-element.528.idx_ref), custom_call_target="tpu_custom_call" | custom-call | tf_op jit(solution)/shard_map/while/body/eval_jaxpr/pallas_call | solution.py:69
  286.0 6.0 %collective-permute-start.3 = (f32[768,16]{0,1:T(8,128)S(1)}, f32[768,16]{0,1:T(8,128)S(1)}, u32[]{:S(2)}, u32[]{:S(2)}) collective-permute-start(f32[768,16]{0,1:T(8,128)S(1)} %get-tuple-element.485), channel_id=1, source_target_pairs={{8,0},{16,8},{24,16},{32,24},{40,32},{48,40},{56,48},{64,56},{72,6... | collective-permute-start | bytes 147464 | tf_op jit(solution)/shard_map/while/body/eval_jaxpr/ppermute | solution.py:109
  296.5 6.4 %collective-permute-start.5 = (bf16[768,1,1,16]{0,3,2,1:T(8,128)(2,1)S(1)}, bf16[768,1,1,16]{0,3,2,1:T(8,128)(2,1)S(1)}, u32[]{:S(2)}, u32[]{:S(2)}) collective-permute-start(bf16[768,1,1,16]{0,3,2,1:T(8,128)(2,1)S(1)} %reshape.173), channel_id=1, source_target_pairs={{8,0},{16,8},{24,16},{32,24},{40,32},{48,40},{56,48},{64,56},{72,6... | collective-permute-start | bytes 73736 | tf_op jit(solution)/shard_map/while/body/eval_jaxpr/ppermute | solution.py:101
  338.0 6.4 %eval_jaxpr.13 = bf16[6,8192]{1,0:T(8,128)(2,1)} custom-call(bf16[768,144]{1,0:T(8,128)(2,1)} %copy.96.field_ref, s32[1,8192]{1,0:T(1,128)S(1)} %get-tuple-element.528.idx_ref), custom_call_target="tpu_custom_call" | custom-call | tf_op jit(solution)/shard_map/while/body/eval_jaxpr/pallas_call | solution.py:32
  345.8 12.9 %fusion.58 = f32[128,1,192]{2,1,0:T(1,128)S(1)} fusion(bf16[128,384,1]{1,2,0:T(2,128)(2,1)S(1)} %copy.98, bf16[128,192,384]{2,1,0:T(8,128)(2,1)} %get-tuple-element.527), kind=kOutput, calls=%fused_computation.72.clone.1 | convolution fusion | flops 18874368 | bytes 19070976 | tf_op jit(solution)/shard_map/while/body/eval_jaxpr/bij,bj->bi/dot_general | solution.py:179
  360.5 9.7 %fusion.20 = f32[128,1,384]{2,1,0:T(1,128)S(1)} fusion(bf16[128,192,384]{2,1,0:T(8,128)(2,1)} %get-tuple-element.538, bf16[128,192,1]{1,0,2:T(8,128)(2,1)S(1)} %convert_bitcast_fusion.1), kind=kOutput, calls=%fused_computation.55 | convolution fusion | flops 18874368 | bytes 19120128 | tf_op jit(solution)/shard_map/bij,bi->bj/dot_general | solution.py:182
  371.5 9.8 %shard_map.105 = f32[768,144]{1,0:T(8,128)} custom-call(f32[6,8192]{1,0:T(8,128)} %reshape.128.push_ref, s32[1,8192]{1,0:T(1,128)S(1)} %get-tuple-element.539), custom_call_target="tpu_custom_call" | custom-call | tf_op jit(solution)/shard_map/pallas_call | solution.py:69
  397.8 5.4 %collective-permute-done.25 = f32[768,16]{0,1:T(8,128)S(1)} collective-permute-done((f32[768,16]{0,1:T(8,128)S(1)}, f32[768,16]{0,1:T(8,128)S(1)}, u32[]{:S(2)}, u32[]{:S(2)}) %collective-permute-start.25) | collective-permute-done | bytes 49184 | tf_op jit(solution)/shard_map/ppermute | solution.py:109
  (250 shorter events, 204.4 us)
Async XLA Ops:
  1.6 12.5 %collective-permute-start.18 = (bf16[768,1,1,16]{0,3,2,1:T(8,128)(2,1)S(1)}, bf16[768,1,1,16]{0,3,2,1:T(8,128)(2,1)S(1)}, u32[]{:S(2)}, u32[]{:S(2)}) collective-permute-start(bf16[768,1,1,16]{0,3,2,1:T(8,128)(2,1)S(1)} %reshape.123), channel_id=1, source_target_pairs={{0,8},{8,16},{16,24},{24,32},{32,40},{40,48},{48,56},{56,64},{64,7... | collective-permute-start | bytes 73736 | tf_op jit(solution)/shard_map/ppermute | solution.py:100
  5.1 9.0 %collective-permute-start.19 = (bf16[768,1,1,16]{0,3,2,1:T(8,128)(2,1)S(1)}, bf16[768,1,1,16]{0,3,2,1:T(8,128)(2,1)S(1)}, u32[]{:S(2)}, u32[]{:S(2)}) collective-permute-start(bf16[768,1,1,16]{0,3,2,1:T(8,128)(2,1)S(1)} %reshape.123), channel_id=1, source_target_pairs={{8,0},{16,8},{24,16},{32,24},{40,32},{48,40},{56,48},{64,56},{72,6... | collective-permute-start | bytes 73736 | tf_op jit(solution)/shard_map/ppermute | solution.py:101
  64.9 6.5 %collective-permute-start = (f32[768,3,16]{0,2,1:T(8,128)S(1)}, f32[768,3,16]{0,2,1:T(8,128)S(1)}, u32[]{:S(2)}, u32[]{:S(2)}) collective-permute-start(f32[768,3,16]{0,2,1:T(8,128)S(1)} %get-tuple-element.482), channel_id=1, source_target_pairs={{0,1},{1,2},{2,3},{3,4},{4,5},{5,6},{6,7},{8,9},{9,10},{10,11},{11... | collective-permute-start | bytes 442376 | tf_op jit(solution)/shard_map/while/body/eval_jaxpr/ppermute | solution.py:109
  73.2 9.3 %collective-permute-start.2 = (f32[768,16]{0,1:T(8,128)S(1)}, f32[768,16]{0,1:T(8,128)S(1)}, u32[]{:S(2)}, u32[]{:S(2)}) collective-permute-start(f32[768,16]{0,1:T(8,128)S(1)} %get-tuple-element.484), channel_id=1, source_target_pairs={{0,8},{8,16},{16,24},{24,32},{32,40},{40,48},{48,56},{56,64},{64,7... | collective-permute-start | bytes 147464 | tf_op jit(solution)/shard_map/while/body/eval_jaxpr/ppermute | solution.py:109
  75.1 7.8 %collective-permute-start.3 = (f32[768,16]{0,1:T(8,128)S(1)}, f32[768,16]{0,1:T(8,128)S(1)}, u32[]{:S(2)}, u32[]{:S(2)}) collective-permute-start(f32[768,16]{0,1:T(8,128)S(1)} %get-tuple-element.485), channel_id=1, source_target_pairs={{8,0},{16,8},{24,16},{32,24},{40,32},{48,40},{56,48},{64,56},{72,6... | collective-permute-start | bytes 147464 | tf_op jit(solution)/shard_map/while/body/eval_jaxpr/ppermute | solution.py:109
  83.6 34.4 %collective-permute-start.4 = (bf16[768,1,1,16]{0,3,2,1:T(8,128)(2,1)S(1)}, bf16[768,1,1,16]{0,3,2,1:T(8,128)(2,1)S(1)}, u32[]{:S(2)}, u32[]{:S(2)}) collective-permute-start(bf16[768,1,1,16]{0,3,2,1:T(8,128)(2,1)S(1)} %reshape.173), channel_id=1, source_target_pairs={{0,8},{8,16},{16,24},{24,32},{32,40},{40,48},{48,56},{56,64},{64,7... | collective-permute-start | bytes 73736 | tf_op jit(solution)/shard_map/while/body/eval_jaxpr/ppermute | solution.py:100
  85.6 32.5 %collective-permute-start.5 = (bf16[768,1,1,16]{0,3,2,1:T(8,128)(2,1)S(1)}, bf16[768,1,1,16]{0,3,2,1:T(8,128)(2,1)S(1)}, u32[]{:S(2)}, u32[]{:S(2)}) collective-permute-start(bf16[768,1,1,16]{0,3,2,1:T(8,128)(2,1)S(1)} %reshape.173), channel_id=1, source_target_pairs={{8,0},{16,8},{24,16},{32,24},{40,32},{48,40},{56,48},{64,56},{72,6... | collective-permute-start | bytes 73736 | tf_op jit(solution)/shard_map/while/body/eval_jaxpr/ppermute | solution.py:101
  170.2 6.5 %collective-permute-start = (f32[768,3,16]{0,2,1:T(8,128)S(1)}, f32[768,3,16]{0,2,1:T(8,128)S(1)}, u32[]{:S(2)}, u32[]{:S(2)}) collective-permute-start(f32[768,3,16]{0,2,1:T(8,128)S(1)} %get-tuple-element.482), channel_id=1, source_target_pairs={{0,1},{1,2},{2,3},{3,4},{4,5},{5,6},{6,7},{8,9},{9,10},{10,11},{11... | collective-permute-start | bytes 442376 | tf_op jit(solution)/shard_map/while/body/eval_jaxpr/ppermute | solution.py:109
  172.1 6.3 %collective-permute-start.1 = (f32[768,3,16]{0,2,1:T(8,128)S(1)}, f32[768,3,16]{0,2,1:T(8,128)S(1)}, u32[]{:S(2)}, u32[]{:S(2)}) collective-permute-start(f32[768,3,16]{0,2,1:T(8,128)S(1)} %get-tuple-element.483), channel_id=1, source_target_pairs={{1,0},{2,1},{3,2},{4,3},{5,4},{6,5},{7,6},{9,8},{10,9},{11,10},{12... | collective-permute-start | bytes 442376 | tf_op jit(solution)/shard_map/while/body/eval_jaxpr/ppermute | solution.py:109
  178.5 9.3 %collective-permute-start.2 = (f32[768,16]{0,1:T(8,128)S(1)}, f32[768,16]{0,1:T(8,128)S(1)}, u32[]{:S(2)}, u32[]{:S(2)}) collective-permute-start(f32[768,16]{0,1:T(8,128)S(1)} %get-tuple-element.484), channel_id=1, source_target_pairs={{0,8},{8,16},{16,24},{24,32},{32,40},{40,48},{48,56},{56,64},{64,7... | collective-permute-start | bytes 147464 | tf_op jit(solution)/shard_map/while/body/eval_jaxpr/ppermute | solution.py:109
  180.4 8.1 %collective-permute-start.3 = (f32[768,16]{0,1:T(8,128)S(1)}, f32[768,16]{0,1:T(8,128)S(1)}, u32[]{:S(2)}, u32[]{:S(2)}) collective-permute-start(f32[768,16]{0,1:T(8,128)S(1)} %get-tuple-element.485), channel_id=1, source_target_pairs={{8,0},{16,8},{24,16},{32,24},{40,32},{48,40},{56,48},{64,56},{72,6... | collective-permute-start | bytes 147464 | tf_op jit(solution)/shard_map/while/body/eval_jaxpr/ppermute | solution.py:109
  189.2 33.6 %collective-permute-start.4 = (bf16[768,1,1,16]{0,3,2,1:T(8,128)(2,1)S(1)}, bf16[768,1,1,16]{0,3,2,1:T(8,128)(2,1)S(1)}, u32[]{:S(2)}, u32[]{:S(2)}) collective-permute-start(bf16[768,1,1,16]{0,3,2,1:T(8,128)(2,1)S(1)} %reshape.173), channel_id=1, source_target_pairs={{0,8},{8,16},{16,24},{24,32},{32,40},{40,48},{48,56},{56,64},{64,7... | collective-permute-start | bytes 73736 | tf_op jit(solution)/shard_map/while/body/eval_jaxpr/ppermute | solution.py:100
  191.1 31.7 %collective-permute-start.5 = (bf16[768,1,1,16]{0,3,2,1:T(8,128)(2,1)S(1)}, bf16[768,1,1,16]{0,3,2,1:T(8,128)(2,1)S(1)}, u32[]{:S(2)}, u32[]{:S(2)}) collective-permute-start(bf16[768,1,1,16]{0,3,2,1:T(8,128)(2,1)S(1)} %reshape.173), channel_id=1, source_target_pairs={{8,0},{16,8},{24,16},{32,24},{40,32},{48,40},{56,48},{64,56},{72,6... | collective-permute-start | bytes 73736 | tf_op jit(solution)/shard_map/while/body/eval_jaxpr/ppermute | solution.py:101
  224.7 7.1 %collective-permute-start.7 = (bf16[768,3,1,16]{0,3,2,1:T(8,128)(2,1)S(1)}, bf16[768,3,1,16]{0,3,2,1:T(8,128)(2,1)S(1)}, u32[]{:S(2)}, u32[]{:S(2)}) collective-permute-start(bf16[768,3,1,16]{0,3,2,1:T(8,128)(2,1)S(1)} %constant_dynamic-update-slice_fusion.11), channel_id=1, source_target_pairs={{0,1},{1,2},{2,3},{3,4},{4,5},{5,6},{6,7},{8,9},{9,10},{10,11},{11... | collective-permute-start | bytes 221192 | tf_op jit(solution)/shard_map/while/body/eval_jaxpr/ppermute | solution.py:100
  275.8 6.5 %collective-permute-start = (f32[768,3,16]{0,2,1:T(8,128)S(1)}, f32[768,3,16]{0,2,1:T(8,128)S(1)}, u32[]{:S(2)}, u32[]{:S(2)}) collective-permute-start(f32[768,3,16]{0,2,1:T(8,128)S(1)} %get-tuple-element.482), channel_id=1, source_target_pairs={{0,1},{1,2},{2,3},{3,4},{4,5},{5,6},{6,7},{8,9},{9,10},{10,11},{11... | collective-permute-start | bytes 442376 | tf_op jit(solution)/shard_map/while/body/eval_jaxpr/ppermute | solution.py:109
  277.8 6.3 %collective-permute-start.1 = (f32[768,3,16]{0,2,1:T(8,128)S(1)}, f32[768,3,16]{0,2,1:T(8,128)S(1)}, u32[]{:S(2)}, u32[]{:S(2)}) collective-permute-start(f32[768,3,16]{0,2,1:T(8,128)S(1)} %get-tuple-element.483), channel_id=1, source_target_pairs={{1,0},{2,1},{3,2},{4,3},{5,4},{6,5},{7,6},{9,8},{10,9},{11,10},{12... | collective-permute-start | bytes 442376 | tf_op jit(solution)/shard_map/while/body/eval_jaxpr/ppermute | solution.py:109
  284.1 9.3 %collective-permute-start.2 = (f32[768,16]{0,1:T(8,128)S(1)}, f32[768,16]{0,1:T(8,128)S(1)}, u32[]{:S(2)}, u32[]{:S(2)}) collective-permute-start(f32[768,16]{0,1:T(8,128)S(1)} %get-tuple-element.484), channel_id=1, source_target_pairs={{0,8},{8,16},{16,24},{24,32},{32,40},{40,48},{48,56},{56,64},{64,7... | collective-permute-start | bytes 147464 | tf_op jit(solution)/shard_map/while/body/eval_jaxpr/ppermute | solution.py:109
  286.0 7.8 %collective-permute-start.3 = (f32[768,16]{0,1:T(8,128)S(1)}, f32[768,16]{0,1:T(8,128)S(1)}, u32[]{:S(2)}, u32[]{:S(2)}) collective-permute-start(f32[768,16]{0,1:T(8,128)S(1)} %get-tuple-element.485), channel_id=1, source_target_pairs={{8,0},{16,8},{24,16},{32,24},{40,32},{48,40},{56,48},{64,56},{72,6... | collective-permute-start | bytes 147464 | tf_op jit(solution)/shard_map/while/body/eval_jaxpr/ppermute | solution.py:109
  294.6 33.2 %collective-permute-start.4 = (bf16[768,1,1,16]{0,3,2,1:T(8,128)(2,1)S(1)}, bf16[768,1,1,16]{0,3,2,1:T(8,128)(2,1)S(1)}, u32[]{:S(2)}, u32[]{:S(2)}) collective-permute-start(bf16[768,1,1,16]{0,3,2,1:T(8,128)(2,1)S(1)} %reshape.173), channel_id=1, source_target_pairs={{0,8},{8,16},{16,24},{24,32},{32,40},{40,48},{48,56},{56,64},{64,7... | collective-permute-start | bytes 73736 | tf_op jit(solution)/shard_map/while/body/eval_jaxpr/ppermute | solution.py:100
  296.5 31.3 %collective-permute-start.5 = (bf16[768,1,1,16]{0,3,2,1:T(8,128)(2,1)S(1)}, bf16[768,1,1,16]{0,3,2,1:T(8,128)(2,1)S(1)}, u32[]{:S(2)}, u32[]{:S(2)}) collective-permute-start(bf16[768,1,1,16]{0,3,2,1:T(8,128)(2,1)S(1)} %reshape.173), channel_id=1, source_target_pairs={{8,0},{16,8},{24,16},{32,24},{40,32},{48,40},{56,48},{64,56},{72,6... | collective-permute-start | bytes 73736 | tf_op jit(solution)/shard_map/while/body/eval_jaxpr/ppermute | solution.py:101
  329.7 7.3 %collective-permute-start.7 = (bf16[768,3,1,16]{0,3,2,1:T(8,128)(2,1)S(1)}, bf16[768,3,1,16]{0,3,2,1:T(8,128)(2,1)S(1)}, u32[]{:S(2)}, u32[]{:S(2)}) collective-permute-start(bf16[768,3,1,16]{0,3,2,1:T(8,128)(2,1)S(1)} %constant_dynamic-update-slice_fusion.11), channel_id=1, source_target_pairs={{0,1},{1,2},{2,3},{3,4},{4,5},{5,6},{6,7},{8,9},{9,10},{10,11},{11... | collective-permute-start | bytes 221192 | tf_op jit(solution)/shard_map/while/body/eval_jaxpr/ppermute | solution.py:100
  384.6 6.5 %collective-permute-start.23 = (f32[768,3,16]{0,2,1:T(8,128)S(1)}, f32[768,3,16]{0,2,1:T(8,128)S(1)}, u32[]{:S(2)}, u32[]{:S(2)}) collective-permute-start(f32[768,3,16]{0,2,1:T(8,128)S(1)} %get-tuple-element.397), channel_id=1, source_target_pairs={{0,1},{1,2},{2,3},{3,4},{4,5},{5,6},{6,7},{8,9},{9,10},{10,11},{11... | collective-permute-start | bytes 442376 | tf_op jit(solution)/shard_map/ppermute | solution.py:109
  391.2 6.6 %collective-permute-start.24 = (f32[768,16]{0,1:T(8,128)S(1)}, f32[768,16]{0,1:T(8,128)S(1)}, u32[]{:S(2)}, u32[]{:S(2)}) collective-permute-start(f32[768,16]{0,1:T(8,128)S(1)} %get-tuple-element.398), channel_id=1, source_target_pairs={{8,0},{16,8},{24,16},{32,24},{40,32},{48,40},{56,48},{64,56},{72,6... | collective-permute-start | bytes 147464 | tf_op jit(solution)/shard_map/ppermute | solution.py:109
  395.1 8.1 %collective-permute-start.25 = (f32[768,16]{0,1:T(8,128)S(1)}, f32[768,16]{0,1:T(8,128)S(1)}, u32[]{:S(2)}, u32[]{:S(2)}) collective-permute-start(f32[768,16]{0,1:T(8,128)S(1)} %get-tuple-element.399), channel_id=1, source_target_pairs={{0,8},{8,16},{16,24},{24,32},{32,40},{40,48},{48,56},{56,64},{64,7... | collective-permute-start | bytes 147464 | tf_op jit(solution)/shard_map/ppermute | solution.py:109
  (41 other events, 301.5 us)

commit v10 on v8

--- a/solution.py
+++ b/solution.py
@@ -180,8 +180,12 @@
         nearby = with_halo(own, ((GX, 1), (GY, 2)), 1)
         nearby = nearby.reshape(6 * 128, 9 * grains // 128)
         picked = gather_field(nearby, slot_index)
-        picked = jnp.transpose(picked.reshape(6, blocks, GB), (1, 0, 2)).reshape(blocks, 6 * GB)
-        return jnp.einsum("bij,bj->bi", jacobian, picked, preferred_element_type=jnp.float32)
+        return jnp.einsum(
+            "bidj,dbj->bi",
+            jacobian.reshape(blocks, 3 * CB, 6, GB),
+            picked.reshape(6, blocks, GB),
+            preferred_element_type=jnp.float32,
+        )
 
     def backward(impulse_field):
         pushes = jnp.einsum(

time: 405 us -> 398 us (0.983)
  other arithmetic: 113 us -> 82.2 us
  local copies, waits for them, and re-layouts: 22.9 us -> 47.1 us
    unnamed x14 -> x11, other arithmetic: 97.8 us -> 37.3 us
    dot_general x0 -> x3, other arithmetic: none -> 30 us  [forward(): jnp.einsum('bidj,dbj->bi', jacobian.reshape(blocks, 3 * CB, 6, GB), picke...]
    unnamed x29 -> x30, local copies, waits for them, and re-layouts: 1.05 us -> 26 us
  transfers between devices with their start and end apart: 62 -> 62, of which waited for: 36 -> 36; matrix products, arithmetic and copies ran while one was open for 7% -> 13% of each run, Pallas kernels for 4% -> 4%
where the time goes in v10:
time: 398 us; the launch traced here: 394 us
  starting transfers between devices  123 us (31%)
  other arithmetic  82.2 us (21%)
  waiting for transfers between devices  69.3 us (17%)
  Pallas kernels  65.7 us (17%)
  local copies, waits for them, and re-layouts  47.1 us (12%)
  between operations  6.47 us (2%)
    ppermute x16, starting transfers between devices, from_behind(): return lax.ppermute(block, axis, route)  44.1 us
    pallas_call x4, Pallas kernels, scatter_field(): pl.pallas_call(_scatter_kernel, grid=(slots // TILE,), in_specs=[pl.Block...  39.2 us
    unnamed x11, other arithmetic  37.3 us
    ppermute x30, starting transfers between devices, exchange_sum(): lax.ppermute(array, axis, [(i, (i + k) % size) for i in range(size)])  36.9 us
    ppermute x16, waiting for transfers between devices, from_behind(): return lax.ppermute(block, axis, route)  36.6 us
    dot_general x3, other arithmetic, forward(): jnp.einsum('bidj,dbj->bi', jacobian.reshape(blocks, 3 * CB, 6, GB), picke...  30 us
    ppermute x30, waiting for transfers between devices, exchange_sum(): lax.ppermute(array, axis, [(i, (i + k) % size) for i in range(size)])  28.5 us
    pallas_call x4, Pallas kernels, gather_field(): pl.pallas_call(_gather_kernel, grid=(slots // TILE,), in_specs=[pl.BlockS...  26.5 us
  transfers between devices with their start and end apart: 62, of which 36 were waited for; matrix products, arithmetic and copies ran while one was open for 13% of the time, Pallas kernels for 4%

profile of v10, /device:TPU:34, one launch (start us, length us, event | category | flops | bytes accessed | tf_op | source)
XLA Modules:
  0.0 393.7 jit_solution(16182604476371624201)
XLA Ops:
  1.5 4.5 %collective-permute-start.19 = (bf16[768,1,1,16]{0,3,2,1:T(8,128)(2,1)S(1)}, bf16[768,1,1,16]{0,3,2,1:T(8,128)(2,1)S(1)}, u32[]{:S(2)}, u32[]{:S(2)}) collective-permute-start(bf16[768,1,1,16]{0,3,2,1:T(8,128)(2,1)S(1)} %reshape.147), channel_id=1, source_target_pairs={{8,0},{16,8},{24,16},{32,24},{40,32},{48,40},{56,48},{64,56},{72,6... | collective-permute-start | bytes 73736 | tf_op jit(solution)/shard_map/ppermute | solution.py:101
  10.2 9.1 %fusion = f32[128,384]{1,0:T(8,128)S(1)} fusion(bf16[128,192,384]{2,1,0:T(8,128)(2,1)} %param.8, f32[128,192]{1,0:T(8,128)S(1)} %copy.131), kind=kLoop, calls=%fused_computation.8 | loop fusion | flops 28262400 | bytes 19169280
  21.3 9.8 %shard_map.95 = f32[768,144]{1,0:T(8,128)} custom-call(f32[6,8192]{1,0:T(8,128)} %reshape.136.push_ref, s32[1,8192]{1,0:T(1,128)} %reshape.137.idx_ref), custom_call_target="tpu_custom_call" | custom-call | tf_op jit(solution)/shard_map/pallas_call | solution.py:69
  42.3 24.9 %copy.123 = bf16[128,192,384]{0,2,1:T(8,128)(2,1)} copy(bf16[128,192,384]{2,1,0:T(8,128)(2,1)} %param.8) | data formatting | bytes 37748736
  68.2 6.6 %shard_map.97 = bf16[6,8192]{1,0:T(8,128)(2,1)} custom-call(bf16[768,144]{1,0:T(8,128)(2,1)} %copy.65.field_ref, s32[1,8192]{1,0:T(1,128)} %reshape.137.idx_ref), custom_call_target="tpu_custom_call" | custom-call | tf_op jit(solution)/shard_map/pallas_call | solution.py:32
  76.0 6.0 %collective-permute-start.2 = (f32[768,16]{0,1:T(8,128)S(1)}, f32[768,16]{0,1:T(8,128)S(1)}, u32[]{:S(2)}, u32[]{:S(2)}) collective-permute-start(f32[768,16]{0,1:T(8,128)S(1)} %get-tuple-element.32), channel_id=1, source_target_pairs={{8,0},{16,8},{24,16},{32,24},{40,32},{48,40},{56,48},{64,56},{72,6... | collective-permute-start | bytes 147464 | tf_op jit(solution)/shard_map/ppermute | solution.py:109
  84.2 6.1 %collective-permute-done.3 = f32[768,16]{0,1:T(8,128)S(1)} collective-permute-done((f32[768,16]{0,1:T(8,128)S(1)}, f32[768,16]{0,1:T(8,128)S(1)}, u32[]{:S(2)}, u32[]{:S(2)}) %collective-permute-start.3) | collective-permute-done | bytes 49184 | tf_op jit(solution)/shard_map/ppermute | solution.py:109
  107.8 4.0 %collective-permute-start.9 = (f32[2]{0:T(128)S(1)}, f32[2]{0:T(128)S(1)}, u32[]{:S(2)}, u32[]{:S(2)}) collective-permute-start(f32[2]{0:T(128)S(1)} %fusion.57), channel_id=1, source_target_pairs={{0,16},{8,24},{16,0},{24,8},{1,17},{9,25},{17,1},{25,9},{2,18},{10... | collective-permute-start | bytes 32 | tf_op jit(solution)/shard_map/ppermute | solution.py:116
  131.1 6.6 %shard_map.96 = bf16[6,8192]{1,0:T(8,128)(2,1)} custom-call(bf16[768,144]{1,0:T(8,128)(2,1)} %copy.62.field_ref, s32[1,8192]{1,0:T(1,128)} %reshape.137.idx_ref), custom_call_target="tpu_custom_call" | custom-call | tf_op jit(solution)/shard_map/pallas_call | solution.py:32
  139.0 11.1 %fusion.5 = (f32[128,192]{0,1:T(8,128)S(1)}, f32[128,192]{0,1:T(8,128)S(1)}) fusion(bf16[128,6,64,192]{0,2,1,3:T(8,128)(2,1)} %bitcast.217, f32[128,6,64]{0,2,1:T(8,128)S(1)} %copy.133, f32[128,6,64]{0,2,1:T(8,128)S(1)} %copy.132), kind=kLoop, calls=%fused_computation.13 | loop fusion | flops 47136768 | bytes 19464192 | tf_op jit(solution)/shard_map/bidj,dbj->bi/dot_general | solution.py:183
  151.0 9.1 %fusion.1 = f32[128,384]{1,0:T(8,128)S(1)} fusion(bf16[128,192,384]{2,1,0:T(8,128)(2,1)} %param.8, f32[128,192]{1,0:T(8,128)S(1)} %copy.134), kind=kLoop, calls=%fused_computation.9 | loop fusion | flops 28262400 | bytes 19169280
  161.3 9.8 %shard_map.98 = f32[768,144]{1,0:T(8,128)} custom-call(f32[6,8192]{1,0:T(8,128)} %reshape.151.push_ref, s32[1,8192]{1,0:T(1,128)} %reshape.137.idx_ref), custom_call_target="tpu_custom_call" | custom-call | tf_op jit(solution)/shard_map/pallas_call | solution.py:69
  181.0 4.5 %collective-permute-start.24 = (f32[768,16]{0,1:T(8,128)S(1)}, f32[768,16]{0,1:T(8,128)S(1)}, u32[]{:S(2)}, u32[]{:S(2)}) collective-permute-start(f32[768,16]{0,1:T(8,128)S(1)} %get-tuple-element.30), channel_id=1, source_target_pairs={{8,0},{16,8},{24,16},{32,24},{40,32},{48,40},{56,48},{64,56},{72,6... | collective-permute-start | bytes 147464 | tf_op jit(solution)/shard_map/ppermute | solution.py:109
  187.5 6.2 %collective-permute-done.25 = f32[768,16]{0,1:T(8,128)S(1)} collective-permute-done((f32[768,16]{0,1:T(8,128)S(1)}, f32[768,16]{0,1:T(8,128)S(1)}, u32[]{:S(2)}, u32[]{:S(2)}) %collective-permute-start.25) | collective-permute-done | bytes 49184 | tf_op jit(solution)/shard_map/ppermute | solution.py:109
  234.1 6.6 %shard_map.99 = bf16[6,8192]{1,0:T(8,128)(2,1)} custom-call(bf16[768,144]{1,0:T(8,128)(2,1)} %copy.70.field_ref, s32[1,8192]{1,0:T(1,128)} %reshape.137.idx_ref), custom_call_target="tpu_custom_call" | custom-call | tf_op jit(solution)/shard_map/pallas_call | solution.py:32
  242.0 9.4 %fusion.6 = f32[128,192]{0,1:T(8,128)S(1)} fusion(bf16[128,6,64,192]{0,2,1,3:T(8,128)(2,1)} %bitcast.218, f32[128,6,64]{0,2,1:T(8,128)S(1)} %copy.135), kind=kLoop, calls=%fused_computation.14 | loop fusion | flops 28286976 | bytes 19169280 | tf_op jit(solution)/shard_map/bidj,dbj->bi/dot_general | solution.py:183
  252.3 9.1 %fusion.2 = f32[128,384]{1,0:T(8,128)S(1)} fusion(bf16[128,192,384]{2,1,0:T(8,128)(2,1)} %param.8, f32[128,192]{1,0:T(8,128)S(1)} %copy.136), kind=kLoop, calls=%fused_computation.10 | loop fusion | flops 28262400 | bytes 19169280
  262.6 9.8 %shard_map.100 = f32[768,144]{1,0:T(8,128)} custom-call(f32[6,8192]{1,0:T(8,128)} %reshape.160.push_ref, s32[1,8192]{1,0:T(1,128)} %reshape.137.idx_ref), custom_call_target="tpu_custom_call" | custom-call | tf_op jit(solution)/shard_map/pallas_call | solution.py:69
  288.3 5.5 %collective-permute-done.43 = f32[768,16]{0,1:T(8,128)S(1)} collective-permute-done((f32[768,16]{0,1:T(8,128)S(1)}, f32[768,16]{0,1:T(8,128)S(1)}, u32[]{:S(2)}, u32[]{:S(2)}) %collective-permute-start.43) | collective-permute-done | bytes 49184 | tf_op jit(solution)/shard_map/ppermute | solution.py:109
  332.7 6.6 %shard_map.101 = bf16[6,8192]{1,0:T(8,128)(2,1)} custom-call(bf16[768,144]{1,0:T(8,128)(2,1)} %copy.75.field_ref, s32[1,8192]{1,0:T(1,128)} %reshape.137.idx_ref), custom_call_target="tpu_custom_call" | custom-call | tf_op jit(solution)/shard_map/pallas_call | solution.py:32
  340.6 9.4 %fusion.7 = f32[128,192]{0,1:T(8,128)S(1)} fusion(bf16[128,6,64,192]{0,2,1,3:T(8,128)(2,1)} %bitcast.219, f32[128,6,64]{0,2,1:T(8,128)S(1)} %copy.137), kind=kLoop, calls=%fused_computation.15 | loop fusion | flops 28286976 | bytes 19169280 | tf_op jit(solution)/shard_map/bidj,dbj->bi/dot_general | solution.py:183
  350.9 9.1 %fusion.3 = f32[128,384]{1,0:T(8,128)S(1)} fusion(bf16[128,192,384]{2,1,0:T(8,128)(2,1)} %param.8, f32[128,192]{1,0:T(8,128)S(1)} %copy.138), kind=kLoop, calls=%fused_computation.11 | loop fusion | flops 28262400 | bytes 19169280
  361.2 9.8 %shard_map.102 = f32[768,144]{1,0:T(8,128)} custom-call(f32[6,8192]{1,0:T(8,128)} %reshape.169.push_ref, s32[1,8192]{1,0:T(1,128)} %reshape.137.idx_ref), custom_call_target="tpu_custom_call" | custom-call | tf_op jit(solution)/shard_map/pallas_call | solution.py:69
  387.0 6.0 %collective-permute-done.61 = f32[768,16]{0,1:T(8,128)S(1)} collective-permute-done((f32[768,16]{0,1:T(8,128)S(1)}, f32[768,16]{0,1:T(8,128)S(1)}, u32[]{:S(2)}, u32[]{:S(2)}) %collective-permute-start.61) | collective-permute-done | bytes 49184 | tf_op jit(solution)/shard_map/ppermute | solution.py:109
  (245 shorter events, 187.3 us)
Async XLA Ops:
  1.5 31.0 %collective-permute-start.19 = (bf16[768,1,1,16]{0,3,2,1:T(8,128)(2,1)S(1)}, bf16[768,1,1,16]{0,3,2,1:T(8,128)(2,1)S(1)}, u32[]{:S(2)}, u32[]{:S(2)}) collective-permute-start(bf16[768,1,1,16]{0,3,2,1:T(8,128)(2,1)S(1)} %reshape.147), channel_id=1, source_target_pairs={{8,0},{16,8},{24,16},{32,24},{40,32},{48,40},{56,48},{64,56},{72,6... | collective-permute-start | bytes 73736 | tf_op jit(solution)/shard_map/ppermute | solution.py:101
  6.0 26.5 %collective-permute-start.18 = (bf16[768,1,1,16]{0,3,2,1:T(8,128)(2,1)S(1)}, bf16[768,1,1,16]{0,3,2,1:T(8,128)(2,1)S(1)}, u32[]{:S(2)}, u32[]{:S(2)}) collective-permute-start(bf16[768,1,1,16]{0,3,2,1:T(8,128)(2,1)S(1)} %reshape.147), channel_id=1, source_target_pairs={{0,8},{8,16},{16,24},{24,32},{32,40},{40,48},{48,56},{56,64},{64,7... | collective-permute-start | bytes 73736 | tf_op jit(solution)/shard_map/ppermute | solution.py:100
  32.6 34.6 %collective-permute-start.21 = (bf16[768,3,1,16]{0,3,2,1:T(8,128)(2,1)S(1)}, bf16[768,3,1,16]{0,3,2,1:T(8,128)(2,1)S(1)}, u32[]{:S(2)}, u32[]{:S(2)}) collective-permute-start(bf16[768,3,1,16]{0,3,2,1:T(8,128)(2,1)S(1)} %constant_dynamic-update-slice_fusion.3), channel_id=1, source_target_pairs={{1,0},{2,1},{3,2},{4,3},{5,4},{6,5},{7,6},{9,8},{10,9},{11,10},{12... | collective-permute-start | bytes 221192 | tf_op jit(solution)/shard_map/ppermute | solution.py:101
  34.5 32.7 %collective-permute-start.20 = (bf16[768,3,1,16]{0,3,2,1:T(8,128)(2,1)S(1)}, bf16[768,3,1,16]{0,3,2,1:T(8,128)(2,1)S(1)}, u32[]{:S(2)}, u32[]{:S(2)}) collective-permute-start(bf16[768,3,1,16]{0,3,2,1:T(8,128)(2,1)S(1)} %constant_dynamic-update-slice_fusion.3), channel_id=1, source_target_pairs={{0,1},{1,2},{2,3},{3,4},{4,5},{5,6},{6,7},{8,9},{9,10},{10,11},{11... | collective-permute-start | bytes 221192 | tf_op jit(solution)/shard_map/ppermute | solution.py:100
  36.9 39.0 %collective-permute-start = (f32[768,3,16]{0,2,1:T(8,128)S(1)}, f32[768,3,16]{0,2,1:T(8,128)S(1)}, u32[]{:S(2)}, u32[]{:S(2)}) collective-permute-start(f32[768,3,16]{0,2,1:T(8,128)S(1)} %get-tuple-element.24), channel_id=1, source_target_pairs={{1,0},{2,1},{3,2},{4,3},{5,4},{6,5},{7,6},{9,8},{10,9},{11,10},{12... | collective-permute-start | bytes 442376 | tf_op jit(solution)/shard_map/ppermute | solution.py:109
  40.1 35.8 %collective-permute-start.1 = (f32[768,3,16]{0,2,1:T(8,128)S(1)}, f32[768,3,16]{0,2,1:T(8,128)S(1)}, u32[]{:S(2)}, u32[]{:S(2)}) collective-permute-start(f32[768,3,16]{0,2,1:T(8,128)S(1)} %get-tuple-element.25), channel_id=1, source_target_pairs={{0,1},{1,2},{2,3},{3,4},{4,5},{5,6},{6,7},{8,9},{9,10},{10,11},{11... | collective-permute-start | bytes 442376 | tf_op jit(solution)/shard_map/ppermute | solution.py:109
  76.0 8.2 %collective-permute-start.2 = (f32[768,16]{0,1:T(8,128)S(1)}, f32[768,16]{0,1:T(8,128)S(1)}, u32[]{:S(2)}, u32[]{:S(2)}) collective-permute-start(f32[768,16]{0,1:T(8,128)S(1)} %get-tuple-element.32), channel_id=1, source_target_pairs={{8,0},{16,8},{24,16},{32,24},{40,32},{48,40},{56,48},{64,56},{72,6... | collective-permute-start | bytes 147464 | tf_op jit(solution)/shard_map/ppermute | solution.py:109
  82.0 8.3 %collective-permute-start.3 = (f32[768,16]{0,1:T(8,128)S(1)}, f32[768,16]{0,1:T(8,128)S(1)}, u32[]{:S(2)}, u32[]{:S(2)}) collective-permute-start(f32[768,16]{0,1:T(8,128)S(1)} %get-tuple-element.33), channel_id=1, source_target_pairs={{0,8},{8,16},{16,24},{24,32},{32,40},{40,48},{48,56},{56,64},{64,7... | collective-permute-start | bytes 147464 | tf_op jit(solution)/shard_map/ppermute | solution.py:109
  91.1 31.4 %collective-permute-start.15 = (bf16[768,1,1,16]{0,3,2,1:T(8,128)(2,1)S(1)}, bf16[768,1,1,16]{0,3,2,1:T(8,128)(2,1)S(1)}, u32[]{:S(2)}, u32[]{:S(2)}) collective-permute-start(bf16[768,1,1,16]{0,3,2,1:T(8,128)(2,1)S(1)} %reshape.142), channel_id=1, source_target_pairs={{8,0},{16,8},{24,16},{32,24},{40,32},{48,40},{56,48},{64,56},{72,6... | collective-permute-start | bytes 73736 | tf_op jit(solution)/shard_map/ppermute | solution.py:101
  93.0 29.5 %collective-permute-start.14 = (bf16[768,1,1,16]{0,3,2,1:T(8,128)(2,1)S(1)}, bf16[768,1,1,16]{0,3,2,1:T(8,128)(2,1)S(1)}, u32[]{:S(2)}, u32[]{:S(2)}) collective-permute-start(bf16[768,1,1,16]{0,3,2,1:T(8,128)(2,1)S(1)} %reshape.142), channel_id=1, source_target_pairs={{0,8},{8,16},{16,24},{24,32},{32,40},{40,48},{48,56},{56,64},{64,7... | collective-permute-start | bytes 73736 | tf_op jit(solution)/shard_map/ppermute | solution.py:100
  122.5 6.4 %collective-permute-start.17 = (bf16[768,3,1,16]{0,3,2,1:T(8,128)(2,1)S(1)}, bf16[768,3,1,16]{0,3,2,1:T(8,128)(2,1)S(1)}, u32[]{:S(2)}, u32[]{:S(2)}) collective-permute-start(bf16[768,3,1,16]{0,3,2,1:T(8,128)(2,1)S(1)} %constant_dynamic-update-slice_fusion), channel_id=1, source_target_pairs={{1,0},{2,1},{3,2},{4,3},{5,4},{6,5},{7,6},{9,8},{10,9},{11,10},{12... | collective-permute-start | bytes 221192 | tf_op jit(solution)/shard_map/ppermute | solution.py:101
  174.5 6.5 %collective-permute-start.23 = (f32[768,3,16]{0,2,1:T(8,128)S(1)}, f32[768,3,16]{0,2,1:T(8,128)S(1)}, u32[]{:S(2)}, u32[]{:S(2)}) collective-permute-start(f32[768,3,16]{0,2,1:T(8,128)S(1)} %get-tuple-element.23), channel_id=1, source_target_pairs={{0,1},{1,2},{2,3},{3,4},{4,5},{5,6},{6,7},{8,9},{9,10},{10,11},{11... | collective-permute-start | bytes 442376 | tf_op jit(solution)/shard_map/ppermute | solution.py:109
  181.0 6.5 %collective-permute-start.24 = (f32[768,16]{0,1:T(8,128)S(1)}, f32[768,16]{0,1:T(8,128)S(1)}, u32[]{:S(2)}, u32[]{:S(2)}) collective-permute-start(f32[768,16]{0,1:T(8,128)S(1)} %get-tuple-element.30), channel_id=1, source_target_pairs={{8,0},{16,8},{24,16},{32,24},{40,32},{48,40},{56,48},{64,56},{72,6... | collective-permute-start | bytes 147464 | tf_op jit(solution)/shard_map/ppermute | solution.py:109
  185.5 8.1 %collective-permute-start.25 = (f32[768,16]{0,1:T(8,128)S(1)}, f32[768,16]{0,1:T(8,128)S(1)}, u32[]{:S(2)}, u32[]{:S(2)}) collective-permute-start(f32[768,16]{0,1:T(8,128)S(1)} %get-tuple-element.31), channel_id=1, source_target_pairs={{0,8},{8,16},{16,24},{24,32},{32,40},{40,48},{48,56},{56,64},{64,7... | collective-permute-start | bytes 147464 | tf_op jit(solution)/shard_map/ppermute | solution.py:109
  194.4 30.5 %collective-permute-start.37 = (bf16[768,1,1,16]{0,3,2,1:T(8,128)(2,1)S(1)}, bf16[768,1,1,16]{0,3,2,1:T(8,128)(2,1)S(1)}, u32[]{:S(2)}, u32[]{:S(2)}) collective-permute-start(bf16[768,1,1,16]{0,3,2,1:T(8,128)(2,1)S(1)} %reshape.156), channel_id=1, source_target_pairs={{8,0},{16,8},{24,16},{32,24},{40,32},{48,40},{56,48},{64,56},{72,6... | collective-permute-start | bytes 73736 | tf_op jit(solution)/shard_map/ppermute | solution.py:101
  196.3 28.5 %collective-permute-start.36 = (bf16[768,1,1,16]{0,3,2,1:T(8,128)(2,1)S(1)}, bf16[768,1,1,16]{0,3,2,1:T(8,128)(2,1)S(1)}, u32[]{:S(2)}, u32[]{:S(2)}) collective-permute-start(bf16[768,1,1,16]{0,3,2,1:T(8,128)(2,1)S(1)} %reshape.156), channel_id=1, source_target_pairs={{0,8},{8,16},{16,24},{24,32},{32,40},{40,48},{48,56},{56,64},{64,7... | collective-permute-start | bytes 73736 | tf_op jit(solution)/shard_map/ppermute | solution.py:100
  224.9 6.4 %collective-permute-start.39 = (bf16[768,3,1,16]{0,3,2,1:T(8,128)(2,1)S(1)}, bf16[768,3,1,16]{0,3,2,1:T(8,128)(2,1)S(1)}, u32[]{:S(2)}, u32[]{:S(2)}) collective-permute-start(bf16[768,3,1,16]{0,3,2,1:T(8,128)(2,1)S(1)} %constant_dynamic-update-slice_fusion.6), channel_id=1, source_target_pairs={{1,0},{2,1},{3,2},{4,3},{5,4},{6,5},{7,6},{9,8},{10,9},{11,10},{12... | collective-permute-start | bytes 221192 | tf_op jit(solution)/shard_map/ppermute | solution.py:101
  275.8 6.5 %collective-permute-start.41 = (f32[768,3,16]{0,2,1:T(8,128)S(1)}, f32[768,3,16]{0,2,1:T(8,128)S(1)}, u32[]{:S(2)}, u32[]{:S(2)}) collective-permute-start(f32[768,3,16]{0,2,1:T(8,128)S(1)} %get-tuple-element.21), channel_id=1, source_target_pairs={{0,1},{1,2},{2,3},{3,4},{4,5},{5,6},{6,7},{8,9},{9,10},{10,11},{11... | collective-permute-start | bytes 442376 | tf_op jit(solution)/shard_map/ppermute | solution.py:109
  285.7 8.1 %collective-permute-start.43 = (f32[768,16]{0,1:T(8,128)S(1)}, f32[768,16]{0,1:T(8,128)S(1)}, u32[]{:S(2)}, u32[]{:S(2)}) collective-permute-start(f32[768,16]{0,1:T(8,128)S(1)} %get-tuple-element.29), channel_id=1, source_target_pairs={{0,8},{8,16},{16,24},{24,32},{32,40},{40,48},{48,56},{56,64},{64,7... | collective-permute-start | bytes 147464 | tf_op jit(solution)/shard_map/ppermute | solution.py:109
  294.5 29.5 %collective-permute-start.55 = (bf16[768,1,1,16]{0,3,2,1:T(8,128)(2,1)S(1)}, bf16[768,1,1,16]{0,3,2,1:T(8,128)(2,1)S(1)}, u32[]{:S(2)}, u32[]{:S(2)}) collective-permute-start(bf16[768,1,1,16]{0,3,2,1:T(8,128)(2,1)S(1)} %reshape.165), channel_id=1, source_target_pairs={{8,0},{16,8},{24,16},{32,24},{40,32},{48,40},{56,48},{64,56},{72,6... | collective-permute-start | bytes 73736 | tf_op jit(solution)/shard_map/ppermute | solution.py:101
  296.5 27.5 %collective-permute-start.54 = (bf16[768,1,1,16]{0,3,2,1:T(8,128)(2,1)S(1)}, bf16[768,1,1,16]{0,3,2,1:T(8,128)(2,1)S(1)}, u32[]{:S(2)}, u32[]{:S(2)}) collective-permute-start(bf16[768,1,1,16]{0,3,2,1:T(8,128)(2,1)S(1)} %reshape.165), channel_id=1, source_target_pairs={{0,8},{8,16},{16,24},{24,32},{32,40},{40,48},{48,56},{56,64},{64,7... | collective-permute-start | bytes 73736 | tf_op jit(solution)/shard_map/ppermute | solution.py:100
  324.0 6.5 %collective-permute-start.57 = (bf16[768,3,1,16]{0,3,2,1:T(8,128)(2,1)S(1)}, bf16[768,3,1,16]{0,3,2,1:T(8,128)(2,1)S(1)}, u32[]{:S(2)}, u32[]{:S(2)}) collective-permute-start(bf16[768,3,1,16]{0,3,2,1:T(8,128)(2,1)S(1)} %constant_dynamic-update-slice_fusion.9), channel_id=1, source_target_pairs={{1,0},{2,1},{3,2},{4,3},{5,4},{6,5},{7,6},{9,8},{10,9},{11,10},{12... | collective-permute-start | bytes 221192 | tf_op jit(solution)/shard_map/ppermute | solution.py:101
  374.5 6.5 %collective-permute-start.59 = (f32[768,3,16]{0,2,1:T(8,128)S(1)}, f32[768,3,16]{0,2,1:T(8,128)S(1)}, u32[]{:S(2)}, u32[]{:S(2)}) collective-permute-start(f32[768,3,16]{0,2,1:T(8,128)S(1)} %get-tuple-element.19), channel_id=1, source_target_pairs={{0,1},{1,2},{2,3},{3,4},{4,5},{5,6},{6,7},{8,9},{9,10},{10,11},{11... | collective-permute-start | bytes 442376 | tf_op jit(solution)/shard_map/ppermute | solution.py:109
  384.9 8.1 %collective-permute-start.61 = (f32[768,16]{0,1:T(8,128)S(1)}, f32[768,16]{0,1:T(8,128)S(1)}, u32[]{:S(2)}, u32[]{:S(2)}) collective-permute-start(f32[768,16]{0,1:T(8,128)S(1)} %get-tuple-element.27), channel_id=1, source_target_pairs={{0,8},{8,16},{16,24},{24,32},{32,40},{40,48},{48,56},{56,64},{64,7... | collective-permute-start | bytes 147464 | tf_op jit(solution)/shard_map/ppermute | solution.py:109
  (44 other events, 538.5 us)

commit v11 on v10

--- a/solution.py
+++ b/solution.py
@@ -116,15 +116,10 @@
             lax.ppermute(array, axis, [(i, (i + k) % size) for i in range(size)])
             for k in range(1, size)
         ]
-        own = lax.axis_index(axis)
-        ordered = []
-        for position in range(size):
-            chosen = parts[0]
-            for k in range(1, size):
-                chosen = jnp.where((own - k) % size == position, parts[k], chosen)
-            ordered.append(chosen)
+        ordered = parts
         while len(ordered) > 1:
-            ordered = [ordered[i] + ordered[i + 1] for i in range(0, len(ordered), 2)]
+            half = len(ordered) // 2
+            ordered = [ordered[i] + ordered[i + half] for i in range(half)]
         array = ordered[0]
     return array
 

time: 398 us -> 406 us (1.020)
  starting transfers between devices: 123 us -> 136 us
  waiting for transfers between devices: 69.3 us -> 64.2 us
    ppermute x30, starting transfers between devices: 36.9 us -> 47.9 us  [exchange_sum(): lax.ppermute(array, axis, [(i, (i + k) % size) for i in range(size)])]
    ppermute x30, waiting for transfers between devices: 28.5 us -> 23.7 us  [exchange_sum(): lax.ppermute(array, axis, [(i, (i + k) % size) for i in range(size)])]
  transfers between devices with their start and end apart: 62 -> 62, of which waited for: 36 -> 28; matrix products, arithmetic and copies ran while one was open for 13% -> 13% of each run, Pallas kernels for 4% -> 4%
where the time goes in v11:
time: 406 us; the launch traced here: 401 us
  starting transfers between devices  136 us (33%)
  other arithmetic  82.2 us (20%)
  Pallas kernels  65.7 us (16%)
  waiting for transfers between devices  64.2 us (16%)
  local copies, waits for them, and re-layouts  47.1 us (12%)
  between operations  6.21 us (2%)
    ppermute x30, starting transfers between devices, exchange_sum(): lax.ppermute(array, axis, [(i, (i + k) % size) for i in range(size)])  47.9 us
    ppermute x16, starting transfers between devices, from_behind(): return lax.ppermute(block, axis, route)  45.8 us
    pallas_call x4, Pallas kernels, scatter_field(): pl.pallas_call(_scatter_kernel, grid=(slots // TILE,), in_specs=[pl.Block...  39.2 us
    unnamed x11, other arithmetic  37.3 us
    ppermute x16, waiting for transfers between devices, from_behind(): return lax.ppermute(block, axis, route)  37.1 us
    dot_general x3, other arithmetic, forward(): jnp.einsum('bidj,dbj->bi', jacobian.reshape(blocks, 3 * CB, 6, GB), picke...  30 us
    pallas_call x4, Pallas kernels, gather_field(): pl.pallas_call(_gather_kernel, grid=(slots // TILE,), in_specs=[pl.BlockS...  26.5 us
    unnamed x30, local copies, waits for them, and re-layouts  26 us
  transfers between devices with their start and end apart: 62, of which 28 were waited for; matrix products, arithmetic and copies ran while one was open for 13% of the time, Pallas kernels for 4%

profile of v11, /device:TPU:34, one launch (start us, length us, event | category | flops | bytes accessed | tf_op | source)
XLA Modules:
  0.0 401.0 jit_solution(3863052478503887354)
XLA Ops:
  10.2 9.1 %fusion = f32[128,384]{1,0:T(8,128)S(1)} fusion(bf16[128,192,384]{2,1,0:T(8,128)(2,1)} %param.8, f32[128,192]{1,0:T(8,128)S(1)} %copy.131), kind=kLoop, calls=%fused_computation.8 | loop fusion | flops 28262400 | bytes 19169280
  21.3 9.8 %shard_map.95 = f32[768,144]{1,0:T(8,128)} custom-call(f32[6,8192]{1,0:T(8,128)} %reshape.136.push_ref, s32[1,8192]{1,0:T(1,128)} %reshape.137.idx_ref), custom_call_target="tpu_custom_call" | custom-call | tf_op jit(solution)/shard_map/pallas_call | solution.py:69
  42.2 24.9 %copy.123 = bf16[128,192,384]{0,2,1:T(8,128)(2,1)} copy(bf16[128,192,384]{2,1,0:T(8,128)(2,1)} %param.8) | data formatting | bytes 37748736
  68.0 6.6 %shard_map.97 = bf16[6,8192]{1,0:T(8,128)(2,1)} custom-call(bf16[768,144]{1,0:T(8,128)(2,1)} %copy.65.field_ref, s32[1,8192]{1,0:T(1,128)} %reshape.137.idx_ref), custom_call_target="tpu_custom_call" | custom-call | tf_op jit(solution)/shard_map/pallas_call | solution.py:32
  75.9 6.0 %collective-permute-start.2 = (f32[768,16]{0,1:T(8,128)S(1)}, f32[768,16]{0,1:T(8,128)S(1)}, u32[]{:S(2)}, u32[]{:S(2)}) collective-permute-start(f32[768,16]{0,1:T(8,128)S(1)} %get-tuple-element.32), channel_id=1, source_target_pairs={{8,0},{16,8},{24,16},{32,24},{40,32},{48,40},{56,48},{64,56},{72,6... | collective-permute-start | bytes 147464 | tf_op jit(solution)/shard_map/ppermute | solution.py:109
  84.0 6.1 %collective-permute-done.3 = f32[768,16]{0,1:T(8,128)S(1)} collective-permute-done((f32[768,16]{0,1:T(8,128)S(1)}, f32[768,16]{0,1:T(8,128)S(1)}, u32[]{:S(2)}, u32[]{:S(2)}) %collective-permute-start.3) | collective-permute-done | bytes 49184 | tf_op jit(solution)/shard_map/ppermute | solution.py:109
  131.6 6.6 %shard_map.96 = bf16[6,8192]{1,0:T(8,128)(2,1)} custom-call(bf16[768,144]{1,0:T(8,128)(2,1)} %copy.62.field_ref, s32[1,8192]{1,0:T(1,128)} %reshape.137.idx_ref), custom_call_target="tpu_custom_call" | custom-call | tf_op jit(solution)/shard_map/pallas_call | solution.py:32
  139.6 11.1 %fusion.5 = (f32[128,192]{0,1:T(8,128)S(1)}, f32[128,192]{0,1:T(8,128)S(1)}) fusion(bf16[128,6,64,192]{0,2,1,3:T(8,128)(2,1)} %bitcast.217, f32[128,6,64]{0,2,1:T(8,128)S(1)} %copy.133, f32[128,6,64]{0,2,1:T(8,128)S(1)} %copy.132), kind=kLoop, calls=%fused_computation.13 | loop fusion | flops 47136768 | bytes 19464192 | tf_op jit(solution)/shard_map/bidj,dbj->bi/dot_general | solution.py:178
  151.6 9.1 %fusion.1 = f32[128,384]{1,0:T(8,128)S(1)} fusion(bf16[128,192,384]{2,1,0:T(8,128)(2,1)} %param.8, f32[128,192]{1,0:T(8,128)S(1)} %copy.134), kind=kLoop, calls=%fused_computation.9 | loop fusion | flops 28262400 | bytes 19169280
  161.9 9.8 %shard_map.98 = f32[768,144]{1,0:T(8,128)} custom-call(f32[6,8192]{1,0:T(8,128)} %reshape.151.push_ref, s32[1,8192]{1,0:T(1,128)} %reshape.137.idx_ref), custom_call_target="tpu_custom_call" | custom-call | tf_op jit(solution)/shard_map/pallas_call | solution.py:69
  181.6 4.6 %collective-permute-start.24 = (f32[768,16]{0,1:T(8,128)S(1)}, f32[768,16]{0,1:T(8,128)S(1)}, u32[]{:S(2)}, u32[]{:S(2)}) collective-permute-start(f32[768,16]{0,1:T(8,128)S(1)} %get-tuple-element.30), channel_id=1, source_target_pairs={{8,0},{16,8},{24,16},{32,24},{40,32},{48,40},{56,48},{64,56},{72,6... | collective-permute-start | bytes 147464 | tf_op jit(solution)/shard_map/ppermute | solution.py:109
  188.1 6.2 %collective-permute-done.25 = f32[768,16]{0,1:T(8,128)S(1)} collective-permute-done((f32[768,16]{0,1:T(8,128)S(1)}, f32[768,16]{0,1:T(8,128)S(1)}, u32[]{:S(2)}, u32[]{:S(2)}) %collective-permute-start.25) | collective-permute-done | bytes 49184 | tf_op jit(solution)/shard_map/ppermute | solution.py:109
  236.1 6.6 %shard_map.99 = bf16[6,8192]{1,0:T(8,128)(2,1)} custom-call(bf16[768,144]{1,0:T(8,128)(2,1)} %copy.70.field_ref, s32[1,8192]{1,0:T(1,128)} %reshape.137.idx_ref), custom_call_target="tpu_custom_call" | custom-call | tf_op jit(solution)/shard_map/pallas_call | solution.py:32
  244.0 9.4 %fusion.6 = f32[128,192]{0,1:T(8,128)S(1)} fusion(bf16[128,6,64,192]{0,2,1,3:T(8,128)(2,1)} %bitcast.218, f32[128,6,64]{0,2,1:T(8,128)S(1)} %copy.135), kind=kLoop, calls=%fused_computation.14 | loop fusion | flops 28286976 | bytes 19169280 | tf_op jit(solution)/shard_map/bidj,dbj->bi/dot_general | solution.py:178
  254.3 9.1 %fusion.2 = f32[128,384]{1,0:T(8,128)S(1)} fusion(bf16[128,192,384]{2,1,0:T(8,128)(2,1)} %param.8, f32[128,192]{1,0:T(8,128)S(1)} %copy.136), kind=kLoop, calls=%fused_computation.10 | loop fusion | flops 28262400 | bytes 19169280
  264.6 9.8 %shard_map.100 = f32[768,144]{1,0:T(8,128)} custom-call(f32[6,8192]{1,0:T(8,128)} %reshape.160.push_ref, s32[1,8192]{1,0:T(1,128)} %reshape.137.idx_ref), custom_call_target="tpu_custom_call" | custom-call | tf_op jit(solution)/shard_map/pallas_call | solution.py:69
  284.3 4.6 %collective-permute-start.42 = (f32[768,16]{0,1:T(8,128)S(1)}, f32[768,16]{0,1:T(8,128)S(1)}, u32[]{:S(2)}, u32[]{:S(2)}) collective-permute-start(f32[768,16]{0,1:T(8,128)S(1)} %get-tuple-element.28), channel_id=1, source_target_pairs={{8,0},{16,8},{24,16},{32,24},{40,32},{48,40},{56,48},{64,56},{72,6... | collective-permute-start | bytes 147464 | tf_op jit(solution)/shard_map/ppermute | solution.py:109
  290.9 6.2 %collective-permute-done.43 = f32[768,16]{0,1:T(8,128)S(1)} collective-permute-done((f32[768,16]{0,1:T(8,128)S(1)}, f32[768,16]{0,1:T(8,128)S(1)}, u32[]{:S(2)}, u32[]{:S(2)}) %collective-permute-start.43) | collective-permute-done | bytes 49184 | tf_op jit(solution)/shard_map/ppermute | solution.py:109
  309.6 4.7 %collective-permute-start.45 = (f32[2]{0:T(128)S(1)}, f32[2]{0:T(128)S(1)}, u32[]{:S(2)}, u32[]{:S(2)}) collective-permute-start(f32[2]{0:T(128)S(1)} %fusion.50), channel_id=1, source_target_pairs={{0,4},{2,6},{4,0},{6,2},{1,5},{3,7},{5,1},{7,3},{8,12},{10,14},{12... | collective-permute-start | bytes 32 | tf_op jit(solution)/shard_map/ppermute | solution.py:116
  339.3 6.6 %shard_map.101 = bf16[6,8192]{1,0:T(8,128)(2,1)} custom-call(bf16[768,144]{1,0:T(8,128)(2,1)} %copy.75.field_ref, s32[1,8192]{1,0:T(1,128)} %reshape.137.idx_ref), custom_call_target="tpu_custom_call" | custom-call | tf_op jit(solution)/shard_map/pallas_call | solution.py:32
  347.2 9.4 %fusion.7 = f32[128,192]{0,1:T(8,128)S(1)} fusion(bf16[128,6,64,192]{0,2,1,3:T(8,128)(2,1)} %bitcast.219, f32[128,6,64]{0,2,1:T(8,128)S(1)} %copy.137), kind=kLoop, calls=%fused_computation.15 | loop fusion | flops 28286976 | bytes 19169280 | tf_op jit(solution)/shard_map/bidj,dbj->bi/dot_general | solution.py:178
  357.5 9.1 %fusion.3 = f32[128,384]{1,0:T(8,128)S(1)} fusion(bf16[128,192,384]{2,1,0:T(8,128)(2,1)} %param.8, f32[128,192]{1,0:T(8,128)S(1)} %copy.138), kind=kLoop, calls=%fused_computation.11 | loop fusion | flops 28262400 | bytes 19169280
  367.8 9.8 %shard_map.102 = f32[768,144]{1,0:T(8,128)} custom-call(f32[6,8192]{1,0:T(8,128)} %reshape.169.push_ref, s32[1,8192]{1,0:T(1,128)} %reshape.137.idx_ref), custom_call_target="tpu_custom_call" | custom-call | tf_op jit(solution)/shard_map/pallas_call | solution.py:69
  394.2 6.2 %collective-permute-done.61 = f32[768,16]{0,1:T(8,128)S(1)} collective-permute-done((f32[768,16]{0,1:T(8,128)S(1)}, f32[768,16]{0,1:T(8,128)S(1)}, u32[]{:S(2)}, u32[]{:S(2)}) %collective-permute-start.61) | collective-permute-done | bytes 49184 | tf_op jit(solution)/shard_map/ppermute | solution.py:109
  (245 shorter events, 193.1 us)
Async XLA Ops:
  1.5 31.0 %collective-permute-start.19 = (bf16[768,1,1,16]{0,3,2,1:T(8,128)(2,1)S(1)}, bf16[768,1,1,16]{0,3,2,1:T(8,128)(2,1)S(1)}, u32[]{:S(2)}, u32[]{:S(2)}) collective-permute-start(bf16[768,1,1,16]{0,3,2,1:T(8,128)(2,1)S(1)} %reshape.147), channel_id=1, source_target_pairs={{8,0},{16,8},{24,16},{32,24},{40,32},{48,40},{56,48},{64,56},{72,6... | collective-permute-start | bytes 73736 | tf_op jit(solution)/shard_map/ppermute | solution.py:101
  6.0 26.5 %collective-permute-start.18 = (bf16[768,1,1,16]{0,3,2,1:T(8,128)(2,1)S(1)}, bf16[768,1,1,16]{0,3,2,1:T(8,128)(2,1)S(1)}, u32[]{:S(2)}, u32[]{:S(2)}) collective-permute-start(bf16[768,1,1,16]{0,3,2,1:T(8,128)(2,1)S(1)} %reshape.147), channel_id=1, source_target_pairs={{0,8},{8,16},{16,24},{24,32},{32,40},{40,48},{48,56},{56,64},{64,7... | collective-permute-start | bytes 73736 | tf_op jit(solution)/shard_map/ppermute | solution.py:100
  32.6 34.5 %collective-permute-start.21 = (bf16[768,3,1,16]{0,3,2,1:T(8,128)(2,1)S(1)}, bf16[768,3,1,16]{0,3,2,1:T(8,128)(2,1)S(1)}, u32[]{:S(2)}, u32[]{:S(2)}) collective-permute-start(bf16[768,3,1,16]{0,3,2,1:T(8,128)(2,1)S(1)} %constant_dynamic-update-slice_fusion.3), channel_id=1, source_target_pairs={{1,0},{2,1},{3,2},{4,3},{5,4},{6,5},{7,6},{9,8},{10,9},{11,10},{12... | collective-permute-start | bytes 221192 | tf_op jit(solution)/shard_map/ppermute | solution.py:101
  34.5 32.6 %collective-permute-start.20 = (bf16[768,3,1,16]{0,3,2,1:T(8,128)(2,1)S(1)}, bf16[768,3,1,16]{0,3,2,1:T(8,128)(2,1)S(1)}, u32[]{:S(2)}, u32[]{:S(2)}) collective-permute-start(bf16[768,3,1,16]{0,3,2,1:T(8,128)(2,1)S(1)} %constant_dynamic-update-slice_fusion.3), channel_id=1, source_target_pairs={{0,1},{1,2},{2,3},{3,4},{4,5},{5,6},{6,7},{8,9},{9,10},{10,11},{11... | collective-permute-start | bytes 221192 | tf_op jit(solution)/shard_map/ppermute | solution.py:100
  36.9 38.9 %collective-permute-start = (f32[768,3,16]{0,2,1:T(8,128)S(1)}, f32[768,3,16]{0,2,1:T(8,128)S(1)}, u32[]{:S(2)}, u32[]{:S(2)}) collective-permute-start(f32[768,3,16]{0,2,1:T(8,128)S(1)} %get-tuple-element.24), channel_id=1, source_target_pairs={{1,0},{2,1},{3,2},{4,3},{5,4},{6,5},{7,6},{9,8},{10,9},{11,10},{12... | collective-permute-start | bytes 442376 | tf_op jit(solution)/shard_map/ppermute | solution.py:109
  40.1 35.7 %collective-permute-start.1 = (f32[768,3,16]{0,2,1:T(8,128)S(1)}, f32[768,3,16]{0,2,1:T(8,128)S(1)}, u32[]{:S(2)}, u32[]{:S(2)}) collective-permute-start(f32[768,3,16]{0,2,1:T(8,128)S(1)} %get-tuple-element.25), channel_id=1, source_target_pairs={{0,1},{1,2},{2,3},{3,4},{4,5},{5,6},{6,7},{8,9},{9,10},{10,11},{11... | collective-permute-start | bytes 442376 | tf_op jit(solution)/shard_map/ppermute | solution.py:109
  75.9 8.2 %collective-permute-start.2 = (f32[768,16]{0,1:T(8,128)S(1)}, f32[768,16]{0,1:T(8,128)S(1)}, u32[]{:S(2)}, u32[]{:S(2)}) collective-permute-start(f32[768,16]{0,1:T(8,128)S(1)} %get-tuple-element.32), channel_id=1, source_target_pairs={{8,0},{16,8},{24,16},{32,24},{40,32},{48,40},{56,48},{64,56},{72,6... | collective-permute-start | bytes 147464 | tf_op jit(solution)/shard_map/ppermute | solution.py:109
  81.9 8.3 %collective-permute-start.3 = (f32[768,16]{0,1:T(8,128)S(1)}, f32[768,16]{0,1:T(8,128)S(1)}, u32[]{:S(2)}, u32[]{:S(2)}) collective-permute-start(f32[768,16]{0,1:T(8,128)S(1)} %get-tuple-element.33), channel_id=1, source_target_pairs={{0,8},{8,16},{16,24},{24,32},{32,40},{40,48},{48,56},{56,64},{64,7... | collective-permute-start | bytes 147464 | tf_op jit(solution)/shard_map/ppermute | solution.py:109
  90.9 32.1 %collective-permute-start.15 = (bf16[768,1,1,16]{0,3,2,1:T(8,128)(2,1)S(1)}, bf16[768,1,1,16]{0,3,2,1:T(8,128)(2,1)S(1)}, u32[]{:S(2)}, u32[]{:S(2)}) collective-permute-start(bf16[768,1,1,16]{0,3,2,1:T(8,128)(2,1)S(1)} %reshape.142), channel_id=1, source_target_pairs={{8,0},{16,8},{24,16},{32,24},{40,32},{48,40},{56,48},{64,56},{72,6... | collective-permute-start | bytes 73736 | tf_op jit(solution)/shard_map/ppermute | solution.py:101
  92.8 30.2 %collective-permute-start.14 = (bf16[768,1,1,16]{0,3,2,1:T(8,128)(2,1)S(1)}, bf16[768,1,1,16]{0,3,2,1:T(8,128)(2,1)S(1)}, u32[]{:S(2)}, u32[]{:S(2)}) collective-permute-start(bf16[768,1,1,16]{0,3,2,1:T(8,128)(2,1)S(1)} %reshape.142), channel_id=1, source_target_pairs={{0,8},{8,16},{16,24},{24,32},{32,40},{40,48},{48,56},{56,64},{64,7... | collective-permute-start | bytes 73736 | tf_op jit(solution)/shard_map/ppermute | solution.py:100
  181.6 6.6 %collective-permute-start.24 = (f32[768,16]{0,1:T(8,128)S(1)}, f32[768,16]{0,1:T(8,128)S(1)}, u32[]{:S(2)}, u32[]{:S(2)}) collective-permute-start(f32[768,16]{0,1:T(8,128)S(1)} %get-tuple-element.30), channel_id=1, source_target_pairs={{8,0},{16,8},{24,16},{32,24},{40,32},{48,40},{56,48},{64,56},{72,6... | collective-permute-start | bytes 147464 | tf_op jit(solution)/shard_map/ppermute | solution.py:109
  186.2 8.1 %collective-permute-start.25 = (f32[768,16]{0,1:T(8,128)S(1)}, f32[768,16]{0,1:T(8,128)S(1)}, u32[]{:S(2)}, u32[]{:S(2)}) collective-permute-start(f32[768,16]{0,1:T(8,128)S(1)} %get-tuple-element.31), channel_id=1, source_target_pairs={{0,8},{8,16},{16,24},{24,32},{32,40},{40,48},{48,56},{56,64},{64,7... | collective-permute-start | bytes 147464 | tf_op jit(solution)/shard_map/ppermute | solution.py:109
  195.0 32.5 %collective-permute-start.37 = (bf16[768,1,1,16]{0,3,2,1:T(8,128)(2,1)S(1)}, bf16[768,1,1,16]{0,3,2,1:T(8,128)(2,1)S(1)}, u32[]{:S(2)}, u32[]{:S(2)}) collective-permute-start(bf16[768,1,1,16]{0,3,2,1:T(8,128)(2,1)S(1)} %reshape.156), channel_id=1, source_target_pairs={{8,0},{16,8},{24,16},{32,24},{40,32},{48,40},{56,48},{64,56},{72,6... | collective-permute-start | bytes 73736 | tf_op jit(solution)/shard_map/ppermute | solution.py:101
  197.0 30.5 %collective-permute-start.36 = (bf16[768,1,1,16]{0,3,2,1:T(8,128)(2,1)S(1)}, bf16[768,1,1,16]{0,3,2,1:T(8,128)(2,1)S(1)}, u32[]{:S(2)}, u32[]{:S(2)}) collective-permute-start(bf16[768,1,1,16]{0,3,2,1:T(8,128)(2,1)S(1)} %reshape.156), channel_id=1, source_target_pairs={{0,8},{8,16},{16,24},{24,32},{32,40},{40,48},{48,56},{56,64},{64,7... | collective-permute-start | bytes 73736 | tf_op jit(solution)/shard_map/ppermute | solution.py:100
  277.8 6.5 %collective-permute-start.41 = (f32[768,3,16]{0,2,1:T(8,128)S(1)}, f32[768,3,16]{0,2,1:T(8,128)S(1)}, u32[]{:S(2)}, u32[]{:S(2)}) collective-permute-start(f32[768,3,16]{0,2,1:T(8,128)S(1)} %get-tuple-element.21), channel_id=1, source_target_pairs={{0,1},{1,2},{2,3},{3,4},{4,5},{5,6},{6,7},{8,9},{9,10},{10,11},{11... | collective-permute-start | bytes 442376 | tf_op jit(solution)/shard_map/ppermute | solution.py:109
  284.3 6.6 %collective-permute-start.42 = (f32[768,16]{0,1:T(8,128)S(1)}, f32[768,16]{0,1:T(8,128)S(1)}, u32[]{:S(2)}, u32[]{:S(2)}) collective-permute-start(f32[768,16]{0,1:T(8,128)S(1)} %get-tuple-element.28), channel_id=1, source_target_pairs={{8,0},{16,8},{24,16},{32,24},{40,32},{48,40},{56,48},{64,56},{72,6... | collective-permute-start | bytes 147464 | tf_op jit(solution)/shard_map/ppermute | solution.py:109
  289.0 8.1 %collective-permute-start.43 = (f32[768,16]{0,1:T(8,128)S(1)}, f32[768,16]{0,1:T(8,128)S(1)}, u32[]{:S(2)}, u32[]{:S(2)}) collective-permute-start(f32[768,16]{0,1:T(8,128)S(1)} %get-tuple-element.29), channel_id=1, source_target_pairs={{0,8},{8,16},{16,24},{24,32},{32,40},{40,48},{48,56},{56,64},{64,7... | collective-permute-start | bytes 147464 | tf_op jit(solution)/shard_map/ppermute | solution.py:109
  297.8 32.9 %collective-permute-start.55 = (bf16[768,1,1,16]{0,3,2,1:T(8,128)(2,1)S(1)}, bf16[768,1,1,16]{0,3,2,1:T(8,128)(2,1)S(1)}, u32[]{:S(2)}, u32[]{:S(2)}) collective-permute-start(bf16[768,1,1,16]{0,3,2,1:T(8,128)(2,1)S(1)} %reshape.165), channel_id=1, source_target_pairs={{8,0},{16,8},{24,16},{32,24},{40,32},{48,40},{56,48},{64,56},{72,6... | collective-permute-start | bytes 73736 | tf_op jit(solution)/shard_map/ppermute | solution.py:101
  299.7 31.0 %collective-permute-start.54 = (bf16[768,1,1,16]{0,3,2,1:T(8,128)(2,1)S(1)}, bf16[768,1,1,16]{0,3,2,1:T(8,128)(2,1)S(1)}, u32[]{:S(2)}, u32[]{:S(2)}) collective-permute-start(bf16[768,1,1,16]{0,3,2,1:T(8,128)(2,1)S(1)} %reshape.165), channel_id=1, source_target_pairs={{0,8},{8,16},{16,24},{24,32},{32,40},{40,48},{48,56},{56,64},{64,7... | collective-permute-start | bytes 73736 | tf_op jit(solution)/shard_map/ppermute | solution.py:100
  307.5 6.8 %collective-permute-start.47 = (f32[2]{0:T(128)S(1)}, f32[2]{0:T(128)S(1)}, u32[]{:S(2)}, u32[]{:S(2)}) collective-permute-start(f32[2]{0:T(128)S(1)} %fusion.50), channel_id=1, source_target_pairs={{0,6},{2,0},{4,2},{6,4},{1,7},{3,1},{5,3},{7,5},{8,14},{10,8},{12,... | collective-permute-start | bytes 32 | tf_op jit(solution)/shard_map/ppermute | solution.py:116
  307.6 6.8 %collective-permute-start.46 = (f32[2]{0:T(128)S(1)}, f32[2]{0:T(128)S(1)}, u32[]{:S(2)}, u32[]{:S(2)}) collective-permute-start(f32[2]{0:T(128)S(1)} %fusion.50), channel_id=1, source_target_pairs={{0,2},{2,4},{4,6},{6,0},{1,3},{3,5},{5,7},{7,1},{8,10},{10,12},{12... | collective-permute-start | bytes 32 | tf_op jit(solution)/shard_map/ppermute | solution.py:116
  330.7 6.5 %collective-permute-start.57 = (bf16[768,3,1,16]{0,3,2,1:T(8,128)(2,1)S(1)}, bf16[768,3,1,16]{0,3,2,1:T(8,128)(2,1)S(1)}, u32[]{:S(2)}, u32[]{:S(2)}) collective-permute-start(bf16[768,3,1,16]{0,3,2,1:T(8,128)(2,1)S(1)} %constant_dynamic-update-slice_fusion.9), channel_id=1, source_target_pairs={{1,0},{2,1},{3,2},{4,3},{5,4},{6,5},{7,6},{9,8},{10,9},{11,10},{12... | collective-permute-start | bytes 221192 | tf_op jit(solution)/shard_map/ppermute | solution.py:101
  387.6 6.6 %collective-permute-start.60 = (f32[768,16]{0,1:T(8,128)S(1)}, f32[768,16]{0,1:T(8,128)S(1)}, u32[]{:S(2)}, u32[]{:S(2)}) collective-permute-start(f32[768,16]{0,1:T(8,128)S(1)} %get-tuple-element.26), channel_id=1, source_target_pairs={{8,0},{16,8},{24,16},{32,24},{40,32},{48,40},{56,48},{64,56},{72,6... | collective-permute-start | bytes 147464 | tf_op jit(solution)/shard_map/ppermute | solution.py:109
  392.2 8.1 %collective-permute-start.61 = (f32[768,16]{0,1:T(8,128)S(1)}, f32[768,16]{0,1:T(8,128)S(1)}, u32[]{:S(2)}, u32[]{:S(2)}) collective-permute-start(f32[768,16]{0,1:T(8,128)S(1)} %get-tuple-element.27), channel_id=1, source_target_pairs={{0,8},{8,16},{16,24},{24,32},{32,40},{40,48},{48,56},{56,64},{64,7... | collective-permute-start | bytes 147464 | tf_op jit(solution)/shard_map/ppermute | solution.py:109
  (44 other events, 565.9 us)

commit v12 on v10

--- a/solution.py
+++ b/solution.py
@@ -189,9 +189,11 @@
 
     def backward(impulse_field):
         pushes = jnp.einsum(
-            "bij,bi->bj", jacobian, impulse_field, preferred_element_type=jnp.float32
-        )
-        pushes = jnp.transpose(pushes.reshape(blocks, 6, GB), (1, 0, 2)).reshape(6, blocks * GB)
+            "bidj,bi->dbj",
+            jacobian.reshape(blocks, 3 * CB, 6, GB),
+            impulse_field,
+            preferred_element_type=jnp.float32,
+        ).reshape(6, blocks * GB)
         nearby = scatter_field(pushes, slot_index, 9 * grains // 128)
         nearby = nearby.reshape(6 * 128, 3, 3, grains // 128)
         row_sums = nearby[:, :, 1]

time: 398 us -> 393 us (0.987)
  other arithmetic: 82.2 us -> 77.8 us
    unnamed x30 -> x26, local copies, waits for them, and re-layouts: 26 us -> 25.7 us
where the time goes in v12:
time: 393 us; the launch traced here: 388 us
  starting transfers between devices  123 us (31%)
  other arithmetic  77.8 us (20%)
  waiting for transfers between devices  69.3 us (18%)
  Pallas kernels  65.7 us (17%)
  local copies, waits for them, and re-layouts  46.2 us (12%)
  between operations  6.39 us (2%)
    ppermute x16, starting transfers between devices, from_behind(): return lax.ppermute(block, axis, route)  44.1 us
    pallas_call x4, Pallas kernels, scatter_field(): pl.pallas_call(_scatter_kernel, grid=(slots // TILE,), in_specs=[pl.Block...  39.2 us
    ppermute x30, starting transfers between devices, exchange_sum(): lax.ppermute(array, axis, [(i, (i + k) % size) for i in range(size)])  36.9 us
    ppermute x16, waiting for transfers between devices, from_behind(): return lax.ppermute(block, axis, route)  36.5 us
    unnamed x11, other arithmetic  33.7 us
    dot_general x3, other arithmetic, forward(): jnp.einsum('bidj,dbj->bi', jacobian.reshape(blocks, 3 * CB, 6, GB), picke...  30 us
    ppermute x30, waiting for transfers between devices, exchange_sum(): lax.ppermute(array, axis, [(i, (i + k) % size) for i in range(size)])  28.5 us
    pallas_call x4, Pallas kernels, gather_field(): pl.pallas_call(_gather_kernel, grid=(slots // TILE,), in_specs=[pl.BlockS...  26.5 us
  transfers between devices with their start and end apart: 62, of which 36 were waited for; matrix products, arithmetic and copies ran while one was open for 13% of the time, Pallas kernels for 4%

profile of v12, /device:TPU:34, one launch (start us, length us, event | category | flops | bytes accessed | tf_op | source)
XLA Modules:
  0.0 388.3 jit_solution(3883816443998707738)
XLA Ops:
  1.5 4.5 %collective-permute-start.19 = (bf16[768,1,1,16]{0,3,2,1:T(8,128)(2,1)S(1)}, bf16[768,1,1,16]{0,3,2,1:T(8,128)(2,1)S(1)}, u32[]{:S(2)}, u32[]{:S(2)}) collective-permute-start(bf16[768,1,1,16]{0,3,2,1:T(8,128)(2,1)S(1)} %reshape.138), channel_id=1, source_target_pairs={{8,0},{16,8},{24,16},{32,24},{40,32},{48,40},{56,48},{64,56},{72,6... | collective-permute-start | bytes 73736 | tf_op jit(solution)/shard_map/ppermute | solution.py:101
  8.6 24.9 %copy.53 = bf16[128,192,384]{0,2,1:T(8,128)(2,1)} copy(bf16[128,192,384]{2,1,0:T(8,128)(2,1)} %param.8) | data formatting | bytes 37748736 | tf_op args[0]
  34.2 8.2 %fusion = f32[128,6,64]{0,2,1:T(8,128)S(1)} fusion(bf16[128,192,6,64]{0,3,2,1:T(8,128)(2,1)} %bitcast.209, f32[128,192]{0,1:T(8,128)S(1)} %get-tuple-element.44), kind=kLoop, calls=%fused_computation.8 | loop fusion | flops 28262400 | bytes 19169280
  44.3 9.8 %shard_map.95 = f32[768,144]{1,0:T(8,128)} custom-call(f32[6,8192]{1,0:T(8,128)} %reshape.128.push_ref, s32[1,8192]{1,0:T(1,128)} %reshape.129.idx_ref), custom_call_target="tpu_custom_call" | custom-call | tf_op jit(solution)/shard_map/pallas_call | solution.py:69
  66.2 6.6 %shard_map.97 = bf16[6,8192]{1,0:T(8,128)(2,1)} custom-call(bf16[768,144]{1,0:T(8,128)(2,1)} %copy.60.field_ref, s32[1,8192]{1,0:T(1,128)} %reshape.129.idx_ref), custom_call_target="tpu_custom_call" | custom-call | tf_op jit(solution)/shard_map/pallas_call | solution.py:32
  74.0 6.0 %collective-permute-start.2 = (f32[768,16]{0,1:T(8,128)S(1)}, f32[768,16]{0,1:T(8,128)S(1)}, u32[]{:S(2)}, u32[]{:S(2)}) collective-permute-start(f32[768,16]{0,1:T(8,128)S(1)} %get-tuple-element.32), channel_id=1, source_target_pairs={{8,0},{16,8},{24,16},{32,24},{40,32},{48,40},{56,48},{64,56},{72,6... | collective-permute-start | bytes 147464 | tf_op jit(solution)/shard_map/ppermute | solution.py:109
  82.1 6.1 %collective-permute-done.3 = f32[768,16]{0,1:T(8,128)S(1)} collective-permute-done((f32[768,16]{0,1:T(8,128)S(1)}, f32[768,16]{0,1:T(8,128)S(1)}, u32[]{:S(2)}, u32[]{:S(2)}) %collective-permute-start.3) | collective-permute-done | bytes 49184 | tf_op jit(solution)/shard_map/ppermute | solution.py:109
  105.8 4.0 %collective-permute-start.9 = (f32[2]{0:T(128)S(1)}, f32[2]{0:T(128)S(1)}, u32[]{:S(2)}, u32[]{:S(2)}) collective-permute-start(f32[2]{0:T(128)S(1)} %fusion.57), channel_id=1, source_target_pairs={{0,16},{8,24},{16,0},{24,8},{1,17},{9,25},{17,1},{25,9},{2,18},{10... | collective-permute-start | bytes 32 | tf_op jit(solution)/shard_map/ppermute | solution.py:116
  129.1 6.6 %shard_map.96 = bf16[6,8192]{1,0:T(8,128)(2,1)} custom-call(bf16[768,144]{1,0:T(8,128)(2,1)} %copy.58.field_ref, s32[1,8192]{1,0:T(1,128)} %reshape.129.idx_ref), custom_call_target="tpu_custom_call" | custom-call | tf_op jit(solution)/shard_map/pallas_call | solution.py:32
  137.0 11.1 %fusion.5 = (f32[128,192]{0,1:T(8,128)S(1)}, f32[128,192]{0,1:T(8,128)S(1)}) fusion(bf16[128,6,64,192]{0,2,1,3:T(8,128)(2,1)} %bitcast.210, f32[128,6,64]{0,2,1:T(8,128)S(1)} %copy.129, f32[128,6,64]{0,2,1:T(8,128)S(1)} %copy.128), kind=kLoop, calls=%fused_computation.13 | loop fusion | flops 47136768 | bytes 19464192 | tf_op jit(solution)/shard_map/bidj,dbj->bi/dot_general | solution.py:183
  148.9 8.2 %fusion.1 = f32[128,6,64]{0,2,1:T(8,128)S(1)} fusion(bf16[128,192,6,64]{0,3,2,1:T(8,128)(2,1)} %bitcast.211, f32[128,192]{0,1:T(8,128)S(1)} %convert_convert_fusion.2), kind=kLoop, calls=%fused_computation.9 | loop fusion | flops 28262400 | bytes 19169280
  158.2 9.8 %shard_map.98 = f32[768,144]{1,0:T(8,128)} custom-call(f32[6,8192]{1,0:T(8,128)} %reshape.141.push_ref, s32[1,8192]{1,0:T(1,128)} %reshape.129.idx_ref), custom_call_target="tpu_custom_call" | custom-call | tf_op jit(solution)/shard_map/pallas_call | solution.py:69
  177.9 4.5 %collective-permute-start.24 = (f32[768,16]{0,1:T(8,128)S(1)}, f32[768,16]{0,1:T(8,128)S(1)}, u32[]{:S(2)}, u32[]{:S(2)}) collective-permute-start(f32[768,16]{0,1:T(8,128)S(1)} %get-tuple-element.30), channel_id=1, source_target_pairs={{8,0},{16,8},{24,16},{32,24},{40,32},{48,40},{56,48},{64,56},{72,6... | collective-permute-start | bytes 147464 | tf_op jit(solution)/shard_map/ppermute | solution.py:109
  184.3 6.2 %collective-permute-done.25 = f32[768,16]{0,1:T(8,128)S(1)} collective-permute-done((f32[768,16]{0,1:T(8,128)S(1)}, f32[768,16]{0,1:T(8,128)S(1)}, u32[]{:S(2)}, u32[]{:S(2)}) %collective-permute-start.25) | collective-permute-done | bytes 49184 | tf_op jit(solution)/shard_map/ppermute | solution.py:109
  230.9 6.6 %shard_map.99 = bf16[6,8192]{1,0:T(8,128)(2,1)} custom-call(bf16[768,144]{1,0:T(8,128)(2,1)} %copy.64.field_ref, s32[1,8192]{1,0:T(1,128)} %reshape.129.idx_ref), custom_call_target="tpu_custom_call" | custom-call | tf_op jit(solution)/shard_map/pallas_call | solution.py:32
  238.9 9.4 %fusion.6 = f32[128,192]{0,1:T(8,128)S(1)} fusion(bf16[128,6,64,192]{0,2,1,3:T(8,128)(2,1)} %bitcast.212, f32[128,6,64]{0,2,1:T(8,128)S(1)} %copy.131), kind=kLoop, calls=%fused_computation.14 | loop fusion | flops 28286976 | bytes 19169280 | tf_op jit(solution)/shard_map/bidj,dbj->bi/dot_general | solution.py:183
  249.0 8.2 %fusion.2 = f32[128,6,64]{0,2,1:T(8,128)S(1)} fusion(bf16[128,192,6,64]{0,3,2,1:T(8,128)(2,1)} %bitcast.213, f32[128,192]{0,1:T(8,128)S(1)} %convert_convert_fusion.1), kind=kLoop, calls=%fused_computation.10 | loop fusion | flops 28262400 | bytes 19169280
  258.3 9.8 %shard_map.100 = f32[768,144]{1,0:T(8,128)} custom-call(f32[6,8192]{1,0:T(8,128)} %reshape.149.push_ref, s32[1,8192]{1,0:T(1,128)} %reshape.129.idx_ref), custom_call_target="tpu_custom_call" | custom-call | tf_op jit(solution)/shard_map/pallas_call | solution.py:69
  284.0 5.5 %collective-permute-done.43 = f32[768,16]{0,1:T(8,128)S(1)} collective-permute-done((f32[768,16]{0,1:T(8,128)S(1)}, f32[768,16]{0,1:T(8,128)S(1)}, u32[]{:S(2)}, u32[]{:S(2)}) %collective-permute-start.43) | collective-permute-done | bytes 49184 | tf_op jit(solution)/shard_map/ppermute | solution.py:109
  328.4 6.6 %shard_map.101 = bf16[6,8192]{1,0:T(8,128)(2,1)} custom-call(bf16[768,144]{1,0:T(8,128)(2,1)} %copy.68.field_ref, s32[1,8192]{1,0:T(1,128)} %reshape.129.idx_ref), custom_call_target="tpu_custom_call" | custom-call | tf_op jit(solution)/shard_map/pallas_call | solution.py:32
  336.4 9.4 %fusion.7 = f32[128,192]{0,1:T(8,128)S(1)} fusion(bf16[128,6,64,192]{0,2,1,3:T(8,128)(2,1)} %bitcast.214, f32[128,6,64]{0,2,1:T(8,128)S(1)} %copy.133), kind=kLoop, calls=%fused_computation.15 | loop fusion | flops 28286976 | bytes 19169280 | tf_op jit(solution)/shard_map/bidj,dbj->bi/dot_general | solution.py:183
  346.5 8.2 %fusion.3 = f32[128,6,64]{0,2,1:T(8,128)S(1)} fusion(bf16[128,192,6,64]{0,3,2,1:T(8,128)(2,1)} %bitcast.215, f32[128,192]{0,1:T(8,128)S(1)} %get-tuple-element.4), kind=kLoop, calls=%fused_computation.11 | loop fusion | flops 28262400 | bytes 19169280
  355.8 9.8 %shard_map.102 = f32[768,144]{1,0:T(8,128)} custom-call(f32[6,8192]{1,0:T(8,128)} %reshape.157.push_ref, s32[1,8192]{1,0:T(1,128)} %reshape.129.idx_ref), custom_call_target="tpu_custom_call" | custom-call | tf_op jit(solution)/shard_map/pallas_call | solution.py:69
  381.6 6.0 %collective-permute-done.61 = f32[768,16]{0,1:T(8,128)S(1)} collective-permute-done((f32[768,16]{0,1:T(8,128)S(1)}, f32[768,16]{0,1:T(8,128)S(1)}, u32[]{:S(2)}, u32[]{:S(2)}) %collective-permute-start.61) | collective-permute-done | bytes 49184 | tf_op jit(solution)/shard_map/ppermute | solution.py:109
  (237 shorter events, 185.5 us)
Async XLA Ops:
  1.5 53.9 %collective-permute-start.19 = (bf16[768,1,1,16]{0,3,2,1:T(8,128)(2,1)S(1)}, bf16[768,1,1,16]{0,3,2,1:T(8,128)(2,1)S(1)}, u32[]{:S(2)}, u32[]{:S(2)}) collective-permute-start(bf16[768,1,1,16]{0,3,2,1:T(8,128)(2,1)S(1)} %reshape.138), channel_id=1, source_target_pairs={{8,0},{16,8},{24,16},{32,24},{40,32},{48,40},{56,48},{64,56},{72,6... | collective-permute-start | bytes 73736 | tf_op jit(solution)/shard_map/ppermute | solution.py:101
  6.0 49.4 %collective-permute-start.18 = (bf16[768,1,1,16]{0,3,2,1:T(8,128)(2,1)S(1)}, bf16[768,1,1,16]{0,3,2,1:T(8,128)(2,1)S(1)}, u32[]{:S(2)}, u32[]{:S(2)}) collective-permute-start(bf16[768,1,1,16]{0,3,2,1:T(8,128)(2,1)S(1)} %reshape.138), channel_id=1, source_target_pairs={{0,8},{8,16},{16,24},{24,32},{32,40},{40,48},{48,56},{56,64},{64,7... | collective-permute-start | bytes 73736 | tf_op jit(solution)/shard_map/ppermute | solution.py:100
  55.5 9.7 %collective-permute-start.21 = (bf16[768,3,1,16]{0,3,2,1:T(8,128)(2,1)S(1)}, bf16[768,3,1,16]{0,3,2,1:T(8,128)(2,1)S(1)}, u32[]{:S(2)}, u32[]{:S(2)}) collective-permute-start(bf16[768,3,1,16]{0,3,2,1:T(8,128)(2,1)S(1)} %constant_dynamic-update-slice_fusion.3), channel_id=1, source_target_pairs={{1,0},{2,1},{3,2},{4,3},{5,4},{6,5},{7,6},{9,8},{10,9},{11,10},{12... | collective-permute-start | bytes 221192 | tf_op jit(solution)/shard_map/ppermute | solution.py:101
  57.4 7.8 %collective-permute-start.20 = (bf16[768,3,1,16]{0,3,2,1:T(8,128)(2,1)S(1)}, bf16[768,3,1,16]{0,3,2,1:T(8,128)(2,1)S(1)}, u32[]{:S(2)}, u32[]{:S(2)}) collective-permute-start(bf16[768,3,1,16]{0,3,2,1:T(8,128)(2,1)S(1)} %constant_dynamic-update-slice_fusion.3), channel_id=1, source_target_pairs={{0,1},{1,2},{2,3},{3,4},{4,5},{5,6},{6,7},{8,9},{9,10},{10,11},{11... | collective-permute-start | bytes 221192 | tf_op jit(solution)/shard_map/ppermute | solution.py:100
  59.8 14.1 %collective-permute-start = (f32[768,3,16]{0,2,1:T(8,128)S(1)}, f32[768,3,16]{0,2,1:T(8,128)S(1)}, u32[]{:S(2)}, u32[]{:S(2)}) collective-permute-start(f32[768,3,16]{0,2,1:T(8,128)S(1)} %get-tuple-element.24), channel_id=1, source_target_pairs={{1,0},{2,1},{3,2},{4,3},{5,4},{6,5},{7,6},{9,8},{10,9},{11,10},{12... | collective-permute-start | bytes 442376 | tf_op jit(solution)/shard_map/ppermute | solution.py:109
  63.0 10.9 %collective-permute-start.1 = (f32[768,3,16]{0,2,1:T(8,128)S(1)}, f32[768,3,16]{0,2,1:T(8,128)S(1)}, u32[]{:S(2)}, u32[]{:S(2)}) collective-permute-start(f32[768,3,16]{0,2,1:T(8,128)S(1)} %get-tuple-element.25), channel_id=1, source_target_pairs={{0,1},{1,2},{2,3},{3,4},{4,5},{5,6},{6,7},{8,9},{9,10},{10,11},{11... | collective-permute-start | bytes 442376 | tf_op jit(solution)/shard_map/ppermute | solution.py:109
  74.0 8.2 %collective-permute-start.2 = (f32[768,16]{0,1:T(8,128)S(1)}, f32[768,16]{0,1:T(8,128)S(1)}, u32[]{:S(2)}, u32[]{:S(2)}) collective-permute-start(f32[768,16]{0,1:T(8,128)S(1)} %get-tuple-element.32), channel_id=1, source_target_pairs={{8,0},{16,8},{24,16},{32,24},{40,32},{48,40},{56,48},{64,56},{72,6... | collective-permute-start | bytes 147464 | tf_op jit(solution)/shard_map/ppermute | solution.py:109
  80.0 8.3 %collective-permute-start.3 = (f32[768,16]{0,1:T(8,128)S(1)}, f32[768,16]{0,1:T(8,128)S(1)}, u32[]{:S(2)}, u32[]{:S(2)}) collective-permute-start(f32[768,16]{0,1:T(8,128)S(1)} %get-tuple-element.33), channel_id=1, source_target_pairs={{0,8},{8,16},{16,24},{24,32},{32,40},{40,48},{48,56},{56,64},{64,7... | collective-permute-start | bytes 147464 | tf_op jit(solution)/shard_map/ppermute | solution.py:109
  89.0 31.5 %collective-permute-start.15 = (bf16[768,1,1,16]{0,3,2,1:T(8,128)(2,1)S(1)}, bf16[768,1,1,16]{0,3,2,1:T(8,128)(2,1)S(1)}, u32[]{:S(2)}, u32[]{:S(2)}) collective-permute-start(bf16[768,1,1,16]{0,3,2,1:T(8,128)(2,1)S(1)} %reshape.134), channel_id=1, source_target_pairs={{8,0},{16,8},{24,16},{32,24},{40,32},{48,40},{56,48},{64,56},{72,6... | collective-permute-start | bytes 73736 | tf_op jit(solution)/shard_map/ppermute | solution.py:101
  90.9 29.5 %collective-permute-start.14 = (bf16[768,1,1,16]{0,3,2,1:T(8,128)(2,1)S(1)}, bf16[768,1,1,16]{0,3,2,1:T(8,128)(2,1)S(1)}, u32[]{:S(2)}, u32[]{:S(2)}) collective-permute-start(bf16[768,1,1,16]{0,3,2,1:T(8,128)(2,1)S(1)} %reshape.134), channel_id=1, source_target_pairs={{0,8},{8,16},{16,24},{24,32},{32,40},{40,48},{48,56},{56,64},{64,7... | collective-permute-start | bytes 73736 | tf_op jit(solution)/shard_map/ppermute | solution.py:100
  120.5 6.4 %collective-permute-start.17 = (bf16[768,3,1,16]{0,3,2,1:T(8,128)(2,1)S(1)}, bf16[768,3,1,16]{0,3,2,1:T(8,128)(2,1)S(1)}, u32[]{:S(2)}, u32[]{:S(2)}) collective-permute-start(bf16[768,3,1,16]{0,3,2,1:T(8,128)(2,1)S(1)} %constant_dynamic-update-slice_fusion), channel_id=1, source_target_pairs={{1,0},{2,1},{3,2},{4,3},{5,4},{6,5},{7,6},{9,8},{10,9},{11,10},{12... | collective-permute-start | bytes 221192 | tf_op jit(solution)/shard_map/ppermute | solution.py:101
  171.3 6.5 %collective-permute-start.23 = (f32[768,3,16]{0,2,1:T(8,128)S(1)}, f32[768,3,16]{0,2,1:T(8,128)S(1)}, u32[]{:S(2)}, u32[]{:S(2)}) collective-permute-start(f32[768,3,16]{0,2,1:T(8,128)S(1)} %get-tuple-element.23), channel_id=1, source_target_pairs={{0,1},{1,2},{2,3},{3,4},{4,5},{5,6},{6,7},{8,9},{9,10},{10,11},{11... | collective-permute-start | bytes 442376 | tf_op jit(solution)/shard_map/ppermute | solution.py:109
  177.9 6.5 %collective-permute-start.24 = (f32[768,16]{0,1:T(8,128)S(1)}, f32[768,16]{0,1:T(8,128)S(1)}, u32[]{:S(2)}, u32[]{:S(2)}) collective-permute-start(f32[768,16]{0,1:T(8,128)S(1)} %get-tuple-element.30), channel_id=1, source_target_pairs={{8,0},{16,8},{24,16},{32,24},{40,32},{48,40},{56,48},{64,56},{72,6... | collective-permute-start | bytes 147464 | tf_op jit(solution)/shard_map/ppermute | solution.py:109
  182.4 8.1 %collective-permute-start.25 = (f32[768,16]{0,1:T(8,128)S(1)}, f32[768,16]{0,1:T(8,128)S(1)}, u32[]{:S(2)}, u32[]{:S(2)}) collective-permute-start(f32[768,16]{0,1:T(8,128)S(1)} %get-tuple-element.31), channel_id=1, source_target_pairs={{0,8},{8,16},{16,24},{24,32},{32,40},{40,48},{48,56},{56,64},{64,7... | collective-permute-start | bytes 147464 | tf_op jit(solution)/shard_map/ppermute | solution.py:109
  191.2 30.5 %collective-permute-start.37 = (bf16[768,1,1,16]{0,3,2,1:T(8,128)(2,1)S(1)}, bf16[768,1,1,16]{0,3,2,1:T(8,128)(2,1)S(1)}, u32[]{:S(2)}, u32[]{:S(2)}) collective-permute-start(bf16[768,1,1,16]{0,3,2,1:T(8,128)(2,1)S(1)} %reshape.146), channel_id=1, source_target_pairs={{8,0},{16,8},{24,16},{32,24},{40,32},{48,40},{56,48},{64,56},{72,6... | collective-permute-start | bytes 73736 | tf_op jit(solution)/shard_map/ppermute | solution.py:101
  193.1 28.5 %collective-permute-start.36 = (bf16[768,1,1,16]{0,3,2,1:T(8,128)(2,1)S(1)}, bf16[768,1,1,16]{0,3,2,1:T(8,128)(2,1)S(1)}, u32[]{:S(2)}, u32[]{:S(2)}) collective-permute-start(bf16[768,1,1,16]{0,3,2,1:T(8,128)(2,1)S(1)} %reshape.146), channel_id=1, source_target_pairs={{0,8},{8,16},{16,24},{24,32},{32,40},{40,48},{48,56},{56,64},{64,7... | collective-permute-start | bytes 73736 | tf_op jit(solution)/shard_map/ppermute | solution.py:100
  221.7 6.4 %collective-permute-start.39 = (bf16[768,3,1,16]{0,3,2,1:T(8,128)(2,1)S(1)}, bf16[768,3,1,16]{0,3,2,1:T(8,128)(2,1)S(1)}, u32[]{:S(2)}, u32[]{:S(2)}) collective-permute-start(bf16[768,3,1,16]{0,3,2,1:T(8,128)(2,1)S(1)} %constant_dynamic-update-slice_fusion.6), channel_id=1, source_target_pairs={{1,0},{2,1},{3,2},{4,3},{5,4},{6,5},{7,6},{9,8},{10,9},{11,10},{12... | collective-permute-start | bytes 221192 | tf_op jit(solution)/shard_map/ppermute | solution.py:101
  271.5 6.5 %collective-permute-start.41 = (f32[768,3,16]{0,2,1:T(8,128)S(1)}, f32[768,3,16]{0,2,1:T(8,128)S(1)}, u32[]{:S(2)}, u32[]{:S(2)}) collective-permute-start(f32[768,3,16]{0,2,1:T(8,128)S(1)} %get-tuple-element.21), channel_id=1, source_target_pairs={{0,1},{1,2},{2,3},{3,4},{4,5},{5,6},{6,7},{8,9},{9,10},{10,11},{11... | collective-permute-start | bytes 442376 | tf_op jit(solution)/shard_map/ppermute | solution.py:109
  281.4 8.1 %collective-permute-start.43 = (f32[768,16]{0,1:T(8,128)S(1)}, f32[768,16]{0,1:T(8,128)S(1)}, u32[]{:S(2)}, u32[]{:S(2)}) collective-permute-start(f32[768,16]{0,1:T(8,128)S(1)} %get-tuple-element.29), channel_id=1, source_target_pairs={{0,8},{8,16},{16,24},{24,32},{32,40},{40,48},{48,56},{56,64},{64,7... | collective-permute-start | bytes 147464 | tf_op jit(solution)/shard_map/ppermute | solution.py:109
  290.2 29.5 %collective-permute-start.55 = (bf16[768,1,1,16]{0,3,2,1:T(8,128)(2,1)S(1)}, bf16[768,1,1,16]{0,3,2,1:T(8,128)(2,1)S(1)}, u32[]{:S(2)}, u32[]{:S(2)}) collective-permute-start(bf16[768,1,1,16]{0,3,2,1:T(8,128)(2,1)S(1)} %reshape.154), channel_id=1, source_target_pairs={{8,0},{16,8},{24,16},{32,24},{40,32},{48,40},{56,48},{64,56},{72,6... | collective-permute-start | bytes 73736 | tf_op jit(solution)/shard_map/ppermute | solution.py:101
  292.2 27.5 %collective-permute-start.54 = (bf16[768,1,1,16]{0,3,2,1:T(8,128)(2,1)S(1)}, bf16[768,1,1,16]{0,3,2,1:T(8,128)(2,1)S(1)}, u32[]{:S(2)}, u32[]{:S(2)}) collective-permute-start(bf16[768,1,1,16]{0,3,2,1:T(8,128)(2,1)S(1)} %reshape.154), channel_id=1, source_target_pairs={{0,8},{8,16},{16,24},{24,32},{32,40},{40,48},{48,56},{56,64},{64,7... | collective-permute-start | bytes 73736 | tf_op jit(solution)/shard_map/ppermute | solution.py:100
  319.8 6.5 %collective-permute-start.57 = (bf16[768,3,1,16]{0,3,2,1:T(8,128)(2,1)S(1)}, bf16[768,3,1,16]{0,3,2,1:T(8,128)(2,1)S(1)}, u32[]{:S(2)}, u32[]{:S(2)}) collective-permute-start(bf16[768,3,1,16]{0,3,2,1:T(8,128)(2,1)S(1)} %constant_dynamic-update-slice_fusion.9), channel_id=1, source_target_pairs={{1,0},{2,1},{3,2},{4,3},{5,4},{6,5},{7,6},{9,8},{10,9},{11,10},{12... | collective-permute-start | bytes 221192 | tf_op jit(solution)/shard_map/ppermute | solution.py:101
  369.1 6.5 %collective-permute-start.59 = (f32[768,3,16]{0,2,1:T(8,128)S(1)}, f32[768,3,16]{0,2,1:T(8,128)S(1)}, u32[]{:S(2)}, u32[]{:S(2)}) collective-permute-start(f32[768,3,16]{0,2,1:T(8,128)S(1)} %get-tuple-element.19), channel_id=1, source_target_pairs={{0,1},{1,2},{2,3},{3,4},{4,5},{5,6},{6,7},{8,9},{9,10},{10,11},{11... | collective-permute-start | bytes 442376 | tf_op jit(solution)/shard_map/ppermute | solution.py:109
  379.5 8.1 %collective-permute-start.61 = (f32[768,16]{0,1:T(8,128)S(1)}, f32[768,16]{0,1:T(8,128)S(1)}, u32[]{:S(2)}, u32[]{:S(2)}) collective-permute-start(f32[768,16]{0,1:T(8,128)S(1)} %get-tuple-element.27), channel_id=1, source_target_pairs={{0,8},{8,16},{16,24},{24,32},{32,40},{40,48},{48,56},{56,64},{64,7... | collective-permute-start | bytes 147464 | tf_op jit(solution)/shard_map/ppermute | solution.py:109
  (44 other events, 521.7 us)
